TPU v7x, 32 devices: a whole 2x2x4 slice. The times are simulated.
32 devices in a mesh: rep: 8 (over z, core), shard: 4 (over y, x).
Axes of the slice: x: 2, y: 2, z: 4, core: 2. Of those that a mesh axis runs over, the one named last changes fastest.
Arguments:
- tokens: bfloat16 [32, 1024, 1024], P(('rep', 'shard')), may hold values from -6 to 6
- segments: int32 [32, 1024], P(('rep', 'shard')), may hold values from 0 to 7, never falling along the last dimension, each value on 1 to 512 neighbouring positions
- cotangent: bfloat16 [32, 1024, 1024], P(('rep', 'shard')), may hold values from -6 to 6
- norm_mix: bfloat16 [1024], P('shard'), may hold values from 0.5 to 1.5
- w_query: bfloat16 [1024, 512], P('shard'), may hold values from -0.1875 to 0.1875
- w_key: bfloat16 [1024, 512], P('shard'), may hold values from -0.1875 to 0.1875
- w_value: bfloat16 [1024, 1024], P('shard'), may hold values from -0.1875 to 0.1875
- w_outgate: bfloat16 [1024, 1024], P('shard'), may hold values from -0.1875 to 0.1875
- w_low: bfloat16 [1024, 16], P('shard'), may hold values from -0.1875 to 0.1875
- w_high: bfloat16 [16, 512], P(None, 'shard'), may hold values from -1.5 to 1.5
- decay_bias: bfloat16 [512], P('shard'), may hold values from 0.5 to 4.5
- head_gain: bfloat16 [256], P('shard'), may hold values from 0.5 to 1.5
- w_out: bfloat16 [1024, 1024], P('shard'), may hold values from -0.1875 to 0.1875
- norm_mlp: bfloat16 [1024], P('shard'), may hold values from 0.5 to 1.5
- w_gate: bfloat16 [1024, 2816], P('shard'), may hold values from -0.1875 to 0.1875
- w_up: bfloat16 [1024, 2816], P('shard'), may hold values from -0.1875 to 0.1875
- w_down: bfloat16 [2816, 1024], P('shard'), may hold values from -0.109375 to 0.109375
Outputs:
- block_out: bfloat16 [32, 1024, 1024], P(('rep', 'shard'))
- grad_tokens: float32 [32, 1024, 1024], P(('rep', 'shard'))
- grad_norm_mix: float32 [1024], P('shard')
- grad_w_query: float32 [1024, 512], P('shard')
- grad_w_key: float32 [1024, 512], P('shard')
- grad_w_value: float32 [1024, 1024], P('shard')
- grad_w_outgate: float32 [1024, 1024], P('shard')
- grad_w_low: float32 [1024, 16], P('shard')
- grad_w_high: float32 [16, 512], P(None, 'shard')
- grad_decay_bias: float32 [512], P('shard')
- grad_head_gain: float32 [256], P('shard')
- grad_w_out: float32 [1024, 1024], P('shard')
- grad_norm_mlp: float32 [1024], P('shard')
- grad_w_gate: float32 [1024, 2816], P('shard')
- grad_w_up: float32 [1024, 2816], P('shard')
- grad_w_down: float32 [2816, 1024], P('shard')
Inputs may be any that keep to these rules, and one draw needn't show every extreme that they name: `segments`: segment numbers never fall along a sequence; a document has 1 to 512 tokens and some document has exactly 512.
All inputs are finite; a program needn't handle non-finite values.
Results may differ from a plain program's by a relative error of at most 0.018.
Values may be sent and summed in bfloat16 or wider, within the bound.
A program may use at most 256 MiB of HBM per device.

v0:
```python
from functools import partial

import jax
import jax.numpy as jnp
from jax import lax
from jax.sharding import PartitionSpec as P

HEADS = 4
KH = 128
VH = 256
BLOCK = 64
VD = 1024


HEAD_EPS = 1.0


def matmul(left, right):
    return jnp.dot(left, right, preferred_element_type=jnp.float32)


def left_trans(left, right):
    return lax.dot_general(
        left, right, (((0,), (0,)), ((), ())), preferred_element_type=jnp.float32
    )


def right_trans(left, right):
    return lax.dot_general(
        left, right, (((1,), (1,)), ((), ())), preferred_element_type=jnp.float32
    )


def rms_scale(values, gain, epsilon=1e-05):
    inverse = lax.rsqrt(jnp.mean(values * values, axis=-1, keepdims=True) + epsilon)
    return values * inverse * gain


def block_pass(query, keys, values, decay, segment):
    length, heads, key_size = query.shape
    value_size = values.shape[-1]
    blocks = length // BLOCK
    query = query * key_size ** (-0.5)
    lower = lax.broadcasted_iota(jnp.int32, (BLOCK, BLOCK), 0) >= lax.broadcasted_iota(
        jnp.int32, (BLOCK, BLOCK), 1
    )

    def advance(carry, item):
        state, last_seg = carry
        qblk, kblk, vblk, dblk, sblk = item
        cumul = jnp.cumsum(dblk, axis=0)
        q_scaled = qblk * jnp.exp(cumul)
        k_scaled = kblk * jnp.exp(-cumul)
        same = ((sblk[:, None] == sblk[None, :]) & lower).astype(jnp.float32)
        scores = (
            jnp.einsum("thd,shd->hts", q_scaled, k_scaled, precision=lax.Precision.HIGHEST)
            * same[None]
        )
        inner = jnp.einsum("hts,she->the", scores, vblk, precision=lax.Precision.HIGHEST)
        keep = (sblk == last_seg).astype(jnp.float32)
        carried = (
            jnp.einsum("thd,hde->the", q_scaled, state, precision=lax.Precision.HIGHEST)
            * keep[:, None, None]
        )
        final = cumul[-1]
        tail = (sblk == sblk[-1]).astype(jnp.float32)
        scaled = k_scaled * jnp.exp(final)[None] * tail[:, None, None]
        fresh = jnp.einsum("shd,she->hde", scaled, vblk, precision=lax.Precision.HIGHEST)
        stay = (sblk[-1] == last_seg).astype(jnp.float32)
        state = jnp.exp(final)[:, :, None] * state * stay + fresh
        return ((state, sblk[-1]), inner + carried)

    def shaped(array):
        return array.reshape((blocks, BLOCK) + array.shape[1:])

    start = (jnp.zeros((heads, key_size, value_size), jnp.float32), jnp.int32(-1))
    _, outputs = lax.scan(
        jax.checkpoint(advance),
        start,
        (shaped(query), shaped(keys), shaped(values), shaped(decay), shaped(segment)),
    )
    return outputs.reshape(length, heads, value_size)


def mixer_core(query, keys, values, outgate, lowpre, decay_bias, head_gain, segment):
    total = query.shape[0]
    seqs = segment.shape[0]
    length = segment.shape[1]
    decay = jax.nn.log_sigmoid(lowpre + decay_bias) / 16.0

    def split(array, width):
        return array.reshape(seqs, length, HEADS, width)

    mixed = jax.vmap(block_pass)(
        split(query, KH), split(keys, KH), split(values, VH), split(decay, KH), segment
    )
    normed = rms_scale(mixed, head_gain, HEAD_EPS)
    return normed.reshape(total, VD) * jax.nn.silu(outgate)


def local(
    tokens,
    segments,
    cotangent,
    norm_mix,
    w_query,
    w_key,
    w_value,
    w_outgate,
    w_low,
    w_high,
    decay_bias,
    head_gain,
    w_out,
    norm_mlp,
    w_gate,
    w_up,
    w_down,
):
    mixer_full = (
        lax.all_gather(norm_mix, "shard", axis=0, tiled=True),
        lax.all_gather(w_query, "shard", axis=0, tiled=True),
        lax.all_gather(w_key, "shard", axis=0, tiled=True),
        lax.all_gather(w_value, "shard", axis=0, tiled=True),
        lax.all_gather(w_outgate, "shard", axis=0, tiled=True),
        lax.all_gather(w_low, "shard", axis=0, tiled=True),
        lax.all_gather(w_high, "shard", axis=1, tiled=True),
        lax.all_gather(decay_bias, "shard", axis=0, tiled=True),
        lax.all_gather(head_gain, "shard", axis=0, tiled=True),
        lax.all_gather(w_out, "shard", axis=0, tiled=True),
    )
    feed_full = (
        lax.all_gather(norm_mlp, "shard", axis=0, tiled=True),
        lax.all_gather(w_gate, "shard", axis=0, tiled=True),
        lax.all_gather(w_up, "shard", axis=0, tiled=True),
        lax.all_gather(w_down, "shard", axis=0, tiled=True),
    )
    gain_mix, query_w, key_w, value_w, outgate_w, low_w, high_w, bias_w, headgain_w, out_w = (
        mixer_full
    )
    gain_feed, gate_w, up_w, down_w = feed_full
    total = tokens.shape[0] * tokens.shape[1]
    width = tokens.shape[2]
    inputs = tokens.reshape(total, width).astype(jnp.float32)
    normed_mix, mix_pull = jax.vjp(rms_scale, inputs, gain_mix.astype(jnp.float32))
    first = normed_mix.astype(jnp.bfloat16)
    query = matmul(first, query_w)
    keys = matmul(first, key_w)
    values = matmul(first, value_w)
    outgate = matmul(first, outgate_w)
    lowrank = matmul(first, low_w).astype(jnp.bfloat16)
    lowpre = matmul(lowrank, high_w)
    core_local = partial(mixer_core, segment=segments)
    mixed, core_pull = jax.vjp(
        core_local,
        query,
        keys,
        values,
        outgate,
        lowpre,
        bias_w.astype(jnp.float32),
        headgain_w.astype(jnp.float32),
    )
    mixed_low = mixed.astype(jnp.bfloat16)
    resid = inputs + matmul(mixed_low, out_w)
    normed_feed, feed_pull = jax.vjp(rms_scale, resid, gain_feed.astype(jnp.float32))
    second = normed_feed.astype(jnp.bfloat16)
    gate = matmul(second, gate_w)
    upward = matmul(second, up_w)
    sigma = jax.nn.sigmoid(gate)
    swish = gate * sigma
    hidden = (swish * upward).astype(jnp.bfloat16)
    result = (resid + matmul(hidden, down_w)).astype(jnp.bfloat16)
    feed_back = (
        lax.all_gather(norm_mlp, "shard", axis=0, tiled=True),
        lax.all_gather(w_gate, "shard", axis=0, tiled=True),
        lax.all_gather(w_up, "shard", axis=0, tiled=True),
        lax.all_gather(w_down, "shard", axis=0, tiled=True),
    )
    unused_gain, back_gate, back_up, back_down = feed_back
    grad_out = cotangent.reshape(total, width)
    part_down = left_trans(hidden, grad_out)
    grad_hidden = right_trans(grad_out, back_down)
    slope = sigma * (1.0 + gate * (1.0 - sigma))
    grad_gate = (grad_hidden * upward * slope).astype(jnp.bfloat16)
    grad_up = (grad_hidden * swish).astype(jnp.bfloat16)
    part_gate = left_trans(second, grad_gate)
    part_up = left_trans(second, grad_up)
    grad_second = right_trans(grad_gate, back_gate) + right_trans(grad_up, back_up)
    grad_resid_norm, part_norm_mlp = feed_pull(grad_second)
    grad_resid = grad_out.astype(jnp.float32) + grad_resid_norm
    grad_branch = grad_resid.astype(jnp.bfloat16)
    mixer_back = (
        lax.all_gather(norm_mix, "shard", axis=0, tiled=True),
        lax.all_gather(w_query, "shard", axis=0, tiled=True),
        lax.all_gather(w_key, "shard", axis=0, tiled=True),
        lax.all_gather(w_value, "shard", axis=0, tiled=True),
        lax.all_gather(w_outgate, "shard", axis=0, tiled=True),
        lax.all_gather(w_low, "shard", axis=0, tiled=True),
        lax.all_gather(w_high, "shard", axis=1, tiled=True),
        lax.all_gather(decay_bias, "shard", axis=0, tiled=True),
        lax.all_gather(head_gain, "shard", axis=0, tiled=True),
        lax.all_gather(w_out, "shard", axis=0, tiled=True),
    )
    (
        unused_mix,
        back_query,
        back_key,
        back_value,
        back_outgate,
        back_low,
        back_high,
        unused_bias,
        unused_headgain,
        back_out,
    ) = mixer_back
    part_out = left_trans(mixed_low, grad_branch)
    grad_mixed = right_trans(grad_branch, back_out)
    grad_query, grad_keys, grad_values, grad_outgate, grad_lowpre, part_bias, part_headgain = (
        core_pull(grad_mixed)
    )
    grad_query = grad_query.astype(jnp.bfloat16)
    grad_keys = grad_keys.astype(jnp.bfloat16)
    grad_values = grad_values.astype(jnp.bfloat16)
    grad_outgate = grad_outgate.astype(jnp.bfloat16)
    grad_lowpre = grad_lowpre.astype(jnp.bfloat16)
    part_high = left_trans(lowrank, grad_lowpre)
    grad_lowrank = right_trans(grad_lowpre, back_high).astype(jnp.bfloat16)
    part_low = left_trans(first, grad_lowrank)
    part_query = left_trans(first, grad_query)
    part_key = left_trans(first, grad_keys)
    part_value = left_trans(first, grad_values)
    part_outgate = left_trans(first, grad_outgate)
    grad_first = (
        right_trans(grad_query, back_query)
        + right_trans(grad_keys, back_key)
        + right_trans(grad_values, back_value)
    )
    grad_first = (
        grad_first + right_trans(grad_outgate, back_outgate) + right_trans(grad_lowrank, back_low)
    )
    grad_inputs_norm, part_norm_mix = mix_pull(grad_first)
    grad_inputs = (grad_resid + grad_inputs_norm).reshape(tokens.shape)
    feed_rows = (
        lax.psum_scatter(
            part_norm_mlp.astype(jnp.bfloat16), "shard", scatter_dimension=0, tiled=True
        ).astype(jnp.float32),
        lax.psum_scatter(
            part_gate.astype(jnp.bfloat16), "shard", scatter_dimension=0, tiled=True
        ).astype(jnp.float32),
        lax.psum_scatter(
            part_up.astype(jnp.bfloat16), "shard", scatter_dimension=0, tiled=True
        ).astype(jnp.float32),
        lax.psum_scatter(
            part_down.astype(jnp.bfloat16), "shard", scatter_dimension=0, tiled=True
        ).astype(jnp.float32),
    )
    feed_sums = (
        lax.psum(feed_rows[0].astype(jnp.bfloat16), "rep").astype(jnp.float32),
        lax.psum(feed_rows[1].astype(jnp.bfloat16), "rep").astype(jnp.float32),
        lax.psum(feed_rows[2].astype(jnp.bfloat16), "rep").astype(jnp.float32),
        lax.psum(feed_rows[3].astype(jnp.bfloat16), "rep").astype(jnp.float32),
    )
    mixer_rows = (
        lax.psum_scatter(
            part_norm_mix.astype(jnp.bfloat16), "shard", scatter_dimension=0, tiled=True
        ).astype(jnp.float32),
        lax.psum_scatter(
            part_query.astype(jnp.bfloat16), "shard", scatter_dimension=0, tiled=True
        ).astype(jnp.float32),
        lax.psum_scatter(
            part_key.astype(jnp.bfloat16), "shard", scatter_dimension=0, tiled=True
        ).astype(jnp.float32),
        lax.psum_scatter(
            part_value.astype(jnp.bfloat16), "shard", scatter_dimension=0, tiled=True
        ).astype(jnp.float32),
        lax.psum_scatter(
            part_outgate.astype(jnp.bfloat16), "shard", scatter_dimension=0, tiled=True
        ).astype(jnp.float32),
        lax.psum_scatter(
            part_low.astype(jnp.bfloat16), "shard", scatter_dimension=0, tiled=True
        ).astype(jnp.float32),
        lax.psum_scatter(
            part_high.astype(jnp.bfloat16), "shard", scatter_dimension=1, tiled=True
        ).astype(jnp.float32),
        lax.psum_scatter(
            part_bias.astype(jnp.bfloat16), "shard", scatter_dimension=0, tiled=True
        ).astype(jnp.float32),
        lax.psum_scatter(
            part_headgain.astype(jnp.bfloat16), "shard", scatter_dimension=0, tiled=True
        ).astype(jnp.float32),
        lax.psum_scatter(
            part_out.astype(jnp.bfloat16), "shard", scatter_dimension=0, tiled=True
        ).astype(jnp.float32),
    )
    mixer_sums = (
        lax.psum(mixer_rows[0].astype(jnp.bfloat16), "rep").astype(jnp.float32),
        lax.psum(mixer_rows[1].astype(jnp.bfloat16), "rep").astype(jnp.float32),
        lax.psum(mixer_rows[2].astype(jnp.bfloat16), "rep").astype(jnp.float32),
        lax.psum(mixer_rows[3].astype(jnp.bfloat16), "rep").astype(jnp.float32),
        lax.psum(mixer_rows[4].astype(jnp.bfloat16), "rep").astype(jnp.float32),
        lax.psum(mixer_rows[5].astype(jnp.bfloat16), "rep").astype(jnp.float32),
        lax.psum(mixer_rows[6].astype(jnp.bfloat16), "rep").astype(jnp.float32),
        lax.psum(mixer_rows[7].astype(jnp.bfloat16), "rep").astype(jnp.float32),
        lax.psum(mixer_rows[8].astype(jnp.bfloat16), "rep").astype(jnp.float32),
        lax.psum(mixer_rows[9].astype(jnp.bfloat16), "rep").astype(jnp.float32),
    )
    return (
        result.reshape(tokens.shape),
        grad_inputs,
        mixer_sums[0],
        mixer_sums[1],
        mixer_sums[2],
        mixer_sums[3],
        mixer_sums[4],
        mixer_sums[5],
        mixer_sums[6],
        mixer_sums[7],
        mixer_sums[8],
        mixer_sums[9],
        feed_sums[0],
        feed_sums[1],
        feed_sums[2],
        feed_sums[3],
    )


def solution(mesh):
    in_specs = (
        P(("rep", "shard"), None, None),
        P(("rep", "shard"), None),
        P(("rep", "shard"), None, None),
        P("shard"),
        P("shard", None),
        P("shard", None),
        P("shard", None),
        P("shard", None),
        P("shard", None),
        P(None, "shard"),
        P("shard"),
        P("shard"),
        P("shard", None),
        P("shard"),
        P("shard", None),
        P("shard", None),
        P("shard", None),
    )
    out_specs = (
        P(("rep", "shard"), None, None),
        P(("rep", "shard"), None, None),
        P("shard"),
        P("shard", None),
        P("shard", None),
        P("shard", None),
        P("shard", None),
        P("shard", None),
        P(None, "shard"),
        P("shard"),
        P("shard"),
        P("shard", None),
        P("shard"),
        P("shard", None),
        P("shard", None),
        P("shard", None),
    )
    return jax.shard_map(local, mesh=mesh, in_specs=in_specs, out_specs=out_specs, check_vma=False)
```

profile of v0, /device:TPU:1, one launch (start us, length us, event | category | flops | bytes accessed | tf_op | source)
XLA Modules:
  0.0 1310.9 jit_solution(10404058792352158195)
XLA Ops:
  15.6 2.9 copy.180
  19.0 7.2 all-gather
  28.0 4.0 copy.181
  32.0 6.8 all_gather.53
  39.5 5.6 all_gather.54
  45.1 5.3 all-gather.1
  50.5 3.4 negate_multiply_fusion
  53.9 2.9 reshape.789
  59.5 7.5 all-reduce.1
  67.6 5.8 all-gather.2
  73.3 4.1 copy.194
  77.5 2.3 copy.182
  79.8 2.3 copy.184
  82.0 4.6 fusion.120
  86.7 2.6 fusion.158
  89.3 15.3 %all-gather.14.cloned.1.call-done = bf16[1024,1024]{1,0:T(8,128)(2,1)} async-done(((bf16[256,1024]{1,0:T(8,128)(2,1)}), bf16[1024,1024]{1,0:T(8,128)(2,1)}) %all-gather.14.cloned.1.call-update) | async-done | bytes 2097168 | tf_op jit(solution)/shard_map/all_gather | solution.py:124
  104.6 4.0 copy.183
  108.6 6.5 convolution_bitcast_fusion.6
  115.1 177.8 %while.44 = (s32[]{:T(128)}, f32[1,4,128,256]{3,2,1,0:T(8,128)S(1)}, s32[1]{0:T(128)}, f32[16,1,64,4,256]{4,2,3,1,0:T(8,128)}, f32[16,1,4,128,256]{4,3,2,1,0:T(8...) while((s32[]{:T(128)}, ...), condition=%wide.region_3.4_spmd.clone.clone, body=%wide.region_1.3_spmd.clone.sunk.clone | while | flops 280002816 | bytes 6207163 | solution.py:77
  293.0 7.1 copy.190
  302.5 3.0 copy.250
  305.5 3.0 copy.249
  308.5 8.6 multiply_convert_fusion.4
  317.1 4.8 multiply_reduce_fusion.6
  325.8 11.8 fusion.159
  337.6 12.9 fusion.160
  350.5 31.1 %all-gather.26.cloned.1.call-done = bf16[2816,1024]{1,0:T(8,128)(2,1)} async-done(((bf16[704,1024]{1,0:T(8,128)(2,1)}), bf16[2816,1024]{1,0:T(8,128)(2,1)}) %all-gather.26.cloned.1.call-update) | async-done | bytes 5767184 | tf_op jit(solution)/shard_map/all_gather | solution.py:136
  381.6 21.6 %multiply_convert_fusion = (bf16[1024,2816]{1,0:T(8,128)(2,1)}, bf16[1024,2816]{1,0:T(8,128)(2,1)}, bf16[1024,2816]{1,0:T(8,128)(2,1)}) fusion(f32[1024,2816]{1,0:T(8,128)} %fusion.159, f32[1024,2816]{1,0:T(8,128)} %fusion.160, bf16[2816,1024]{1,0:T(8,128)(2,1)} %all-gather.26.cloned.1.call-done, bf16[1,1024,1024]{2,1,0:T(8,128)(2,1)S(1)} %copy-done.19), kind=kOutput, calls=%fused_computation.120 | convolution fusion | flops 5948833792 | bytes 48234496 | tf_op jit(solution)/shard_map/dot_general | solution.py:29
  403.2 10.2 fusion.161
  413.4 6.5 multiply_reduce_fusion.2
  421.6 2.7 copy-done.60
  425.5 6.0 multiply_reduce_fusion.3
  431.6 5.7 reshape.794
  437.2 4.4 multiply_reduce_fusion.4
  443.2 2.6 add_add_fusion.1
  449.2 259.2 %while.45 = (s32[]{:T(128)}, f32[1,4,128,256]{2,3,1,0:T(8,128)S(1)}, f32[16,1,64,4,128]{4,2,3,1,0:T(8,128)}, bf16[16,1,64,4,128]{4,2,3,1,0:T(8,128)(2,1)}, bf16[...) while((s32[]{:T(128)}, ...), condition=%wide.region_13.14_spmd.clone.clone, body=%wide.region_8.13_spmd.clone.sunk.clone | while | flops 585089280 | bytes 16077553 | solution.py:77
  711.4 2.2 fusion.123
  719.1 6.8 convolution_convert_fusion.3
  730.1 3.7 fusion.117
  733.9 5.3 convolution_convert_fusion.4
  739.3 10.9 convolution_convert_fusion.2
  750.3 11.1 convolution_convert_fusion.1
  761.6 11.1 convolution_convert_fusion
  774.7 2.3 multiply_negate_fusion
  785.0 6.7 fusion.162
  791.7 3.3 fusion.133
  795.0 4.4 fusion.163
  799.4 3.3 fusion.130
  802.7 8.4 reduce-scatter.23.cloned.1.call-done
  811.1 38.9 %reduce-scatter.17.cloned.1.call-done = bf16[256,1024]{1,0:T(8,128)(2,1)} async-done(((bf16[1024,1024]{1,0:T(8,128)(2,1)}), bf16[256,1024]{1,0:T(8,128)(2,1)}) %reduce-scatter.17.cloned.1.call-update) | async-done | bytes 524304 | tf_op jit(solution)/shard_map/reduce_scatter | solution.py:274
  850.0 38.2 %reduce-scatter.19.cloned.1.call-done = bf16[256,1024]{1,0:T(8,128)(2,1)} async-done(((bf16[1024,1024]{1,0:T(8,128)(2,1)}), bf16[256,1024]{1,0:T(8,128)(2,1)}) %reduce-scatter.19.cloned.1.call-update) | async-done | bytes 524304 | tf_op jit(solution)/shard_map/reduce_scatter | solution.py:277
  888.2 69.0 %reduce-scatter.25.cloned.1.call-done = bf16[256,2816]{1,0:T(8,128)(2,1)} async-done(((bf16[1024,2816]{1,0:T(8,128)(2,1)}), bf16[256,2816]{1,0:T(8,128)(2,1)}) %reduce-scatter.25.cloned.1.call-update) | async-done | bytes 1441808 | tf_op jit(solution)/shard_map/reduce_scatter | solution.py:248
  957.1 68.9 %reduce-scatter.27.cloned.1.call-done = bf16[256,2816]{1,0:T(8,128)(2,1)} async-done(((bf16[1024,2816]{1,0:T(8,128)(2,1)}), bf16[256,2816]{1,0:T(8,128)(2,1)}) %reduce-scatter.27.cloned.1.call-update) | async-done | bytes 1441808 | tf_op jit(solution)/shard_map/reduce_scatter | solution.py:251
  1026.1 68.9 %reduce-scatter.29.cloned.1.call-done = bf16[704,1024]{1,0:T(8,128)(2,1)} async-done(((bf16[2816,1024]{1,0:T(8,128)(2,1)}), bf16[704,1024]{1,0:T(8,128)(2,1)}) %reduce-scatter.29.cloned.1.call-update) | async-done | bytes 1441808 | tf_op jit(solution)/shard_map/reduce_scatter | solution.py:254
  1095.1 8.9 fusion.90
  1104.0 7.3 all-reduce.8
  1111.5 6.4 fusion.100
  1117.9 5.4 copy.213
  1123.3 10.6 fusion.102
  1133.9 2.6 copy.212
  1137.4 10.0 reduce-scatter.21.cloned.1.call-done
  1147.4 25.7 %all-reduce.6 = (bf16[256]{0:T(256)(128)(2,1)S(1)}, bf16[256,16]{0,1:T(8,128)(2,1)S(1)}, bf16[16,128]{1,0:T(8,128)(2,1)S(1)}, bf16[128]{0:T(256)(128)(2,1)S(1)},...) all-reduce(bf16[256]{0:T(256)(128)(2,1)S(1)} %dynamic-slice.2, ...), channel_id=1, replica_groups=mesh['rep'=8,'shard'=4] {'rep'}, use_global_device_ids=true, to_apply=%region_17.18 | all-reduce | flops 6848 | bytes 27392 | tf_op jit(solution)/shard_map/psum | solution.py:297
  1176.5 115.6 %all-reduce.11.cloned.1.call-done = (bf16[256,512]{1,0:T(8,128)(2,1)}, bf16[256,512]{1,0:T(8,128)(2,1)}, bf16[256,1024]{1,0:T(8,128)(2,1)}, bf16[256,1024]{1,0:T...) async-done(((bf16[256,512]{1,0:T(8,128)(2,1)}, bf16[256,512]{1,0:T(8,128)(2,1)}, ...) | async-done | bytes 6422544 | tf_op jit(solution)/shard_map/psum | solution.py:298
  1292.1 3.3 convert_element_type.335
  (961 shorter events, 454.7 us)
Async XLA Ops:
  7.2 70.3 %all-gather.12.cloned.1.call-start = ((), (), s32[]{:S(2)}) async-start(), calls=%async_computation.10 | async-start | bytes 1310720 | tf_op jit(solution)/shard_map/all_gather | solution.py:123
  7.9 71.9 %all-gather.16.cloned.1.call-start = ((), (), s32[]{:S(2)}) async-start(), calls=%async_computation.12 | async-start | bytes 1310720 | tf_op jit(solution)/shard_map/all_gather | solution.py:122
  8.7 96.0 %all-gather.14.cloned.1.call-start = ((), (), s32[]{:S(2)}) async-start(), calls=%async_computation.11 | async-start | bytes 2621440 | tf_op jit(solution)/shard_map/all_gather | solution.py:124
  9.4 299.1 %all-gather.18.cloned.1.call-start = ((), (), s32[]{:S(2)}) async-start(), calls=%async_computation.13 | async-start | bytes 2621440 | tf_op jit(solution)/shard_map/all_gather | solution.py:125
  10.0 307.1 %all-gather.20.cloned.1.call-start = ((), (), s32[]{:S(2)}) async-start(), calls=%async_computation.14 | async-start | bytes 2621440 | tf_op jit(solution)/shard_map/all_gather | solution.py:130
  10.6 313.9 %all-gather.22.cloned.1.call-start = ((), (), s32[]{:S(2)}) async-start(), calls=%async_computation.15 | async-start | bytes 7208960 | tf_op jit(solution)/shard_map/all_gather | solution.py:134
  11.1 326.5 %all-gather.24.cloned.1.call-start = ((), (), s32[]{:S(2)}) async-start(), calls=%async_computation.16 | async-start | bytes 7208960 | tf_op jit(solution)/shard_map/all_gather | solution.py:135
  11.9 369.7 %all-gather.26.cloned.1.call-start = ((), (), s32[]{:S(2)}) async-start(), calls=%async_computation.17 | async-start | bytes 7208960 | tf_op jit(solution)/shard_map/all_gather | solution.py:136
  12.6 790.1 %reduce-scatter.13.cloned.1.call-start = ((), (), s32[]{:S(2)}) async-start(), calls=%async_computation.18 | async-start | bytes 1310720 | tf_op jit(solution)/shard_map/reduce_scatter | solution.py:268
  14.4 4.6 copy-start.56
  18.4 298.7 %copy-start.2 = (bf16[1,1024,1024]{1,2,0:T(8,128)(2,1)}, bf16[1,1024,1024]{1,2,0:T(8,128)(2,1)S(1)}, u32[]{:S(2)}) copy-start(bf16[1,1024,1024]{1,2,0:T(8,128)(2,1)S(1)} %copy.180) | copy-start | bytes 6291460
  18.9 13.1 copy-start.40
  19.0 289.5 %copy-start.36 = (f32[1024]{0:T(1024)}, f32[1024]{0:T(1024)S(1)}, u32[]{:S(2)}) copy-start(f32[1024]{0:T(1024)S(1)} %fusion.144) | copy-start | bytes 12292
  26.2 282.3 %copy-start.38 = (f32[4,1,256]{2,1,0:T(1,128)}, f32[4,1,256]{2,1,0:T(1,128)S(1)}, u32[]{:S(2)}) copy-start(f32[4,1,256]{2,1,0:T(1,128)S(1)} %convert_element_type.341) | copy-start | bytes 12292
  26.2 5.8 copy-start.48
  28.0 11.4 copy-start.49
  28.0 17.1 %copy-start.52 = (bf16[128]{0:T(256)(128)(2,1)S(1)}, bf16[128]{0:T(256)(128)(2,1)}, u32[]{:S(2)}) copy-start(bf16[128]{0:T(256)(128)(2,1)} %param.31) | copy-start | bytes 772
  38.8 15.0 %copy-start.32 = (bf16[1024,16]{0,1:T(8,128)(2,1)}, bf16[1024,16]{0,1:T(8,128)(2,1)S(1)}, u32[]{:S(2)}) copy-start(bf16[1024,16]{0,1:T(8,128)(2,1)S(1)} %all_gather.53) | copy-start | bytes 98308
  39.5 47.2 %copy-start.42 = (bf16[1024,16]{0,1:T(8,128)(2,1)}, bf16[1024,16]{0,1:T(8,128)(2,1)S(1)}, u32[]{:S(2)}) copy-start(bf16[1024,16]{0,1:T(8,128)(2,1)S(1)} %convolution_convert_fusion.5) | copy-start | bytes 98308
  45.1 5.3 copy-start.34
  50.4 6.4 copy-start.46
  50.4 6.9 copy-start.50
  50.4 7.6 copy-start.51
  50.5 8.8 copy-start.57
  50.5 17.1 %copy-start.58 = (bf16[256]{0:T(256)(128)(2,1)S(1)}, bf16[256]{0:T(256)(128)(2,1)}, u32[]{:S(2)}) copy-start(bf16[256]{0:T(256)(128)(2,1)} %param.34) | copy-start | bytes 1540
  82.0 4.6 copy-start.22
  82.0 4.6 copy-start.26
  292.9 7.1 copy-start
  337.6 44.0 %copy-start.19 = (bf16[1,1024,1024]{2,1,0:T(8,128)(2,1)S(1)}, bf16[1,1024,1024]{2,1,0:T(8,128)(2,1)}, u32[]{:S(2)}) copy-start(bf16[1,1024,1024]{2,1,0:T(8,128)(2,1)} %param.23) | copy-start | bytes 6291460
  403.2 10.2 copy-start.8
  403.2 10.2 copy-start.53
  403.2 10.2 copy-start.62
  413.4 6.5 copy-start.14
  420.0 4.3 copy-start.60
  420.0 5.5 copy-start.61
  421.0 10.5 copy-start.9
  431.6 5.7 copy-start.45
  437.2 4.6 copy-start.1
  437.2 5.9 copy-start.4
  713.7 89.0 %reduce-scatter.15.cloned.1.call-start = ((), (), s32[]{:S(2)}) async-start(), calls=%async_computation.19 | async-start | bytes 1310720 | tf_op jit(solution)/shard_map/reduce_scatter | solution.py:271
  719.1 7.4 copy-start.13
  719.1 92.0 %reduce-scatter.23.cloned.1.call-start = ((), (), s32[]{:S(2)}) async-start(), calls=%async_computation.23 | async-start | bytes 2621440 | tf_op jit(solution)/shard_map/reduce_scatter | solution.py:292
  726.0 124.0 %reduce-scatter.17.cloned.1.call-start = ((), (), s32[]{:S(2)}) async-start(), calls=%async_computation.20 | async-start | bytes 2621440 | tf_op jit(solution)/shard_map/reduce_scatter | solution.py:274
  730.1 3.8 copy-start.37
  730.1 3.8 copy-start.39
  733.8 154.4 %reduce-scatter.19.cloned.1.call-start = ((), (), s32[]{:S(2)}) async-start(), calls=%async_computation.21 | async-start | bytes 2621440 | tf_op jit(solution)/shard_map/reduce_scatter | solution.py:277
  739.2 217.9 %reduce-scatter.25.cloned.1.call-start = ((), (), s32[]{:S(2)}) async-start(), calls=%async_computation.24 | async-start | bytes 7208960 | tf_op jit(solution)/shard_map/reduce_scatter | solution.py:248
  750.2 275.8 %reduce-scatter.27.cloned.1.call-start = ((), (), s32[]{:S(2)}) async-start(), calls=%async_computation.25 | async-start | bytes 7208960 | tf_op jit(solution)/shard_map/reduce_scatter | solution.py:251
  761.4 333.6 %reduce-scatter.29.cloned.1.call-start = ((), (), s32[]{:S(2)}) async-start(), calls=%async_computation.26 | async-start | bytes 7208960 | tf_op jit(solution)/shard_map/reduce_scatter | solution.py:254
  772.7 4.3 copy-start.47
  772.7 363.8 %reduce-scatter.31.cloned.1.call-start = ((), (), s32[]{:S(2)}) async-start(), calls=%async_computation.27 | async-start | bytes 163840
  777.1 4.2 copy-start.35
  783.3 364.1 %reduce-scatter.21.cloned.1.call-start = ((), (), s32[]{:S(2)}) async-start(), calls=%async_computation.22 | async-start | bytes 40960 | tf_op jit(solution)/shard_map/reduce_scatter | solution.py:280
  784.7 507.4 %all-reduce.11.cloned.1.call-start = ((), (), s32[]{:S(2)}) async-start(), calls=%async_computation.28 | async-start | bytes 12845056 | tf_op jit(solution)/shard_map/psum | solution.py:298
  785.0 6.7 copy-start.18
  795.0 4.4 copy-start.16
  795.0 4.4 copy-start.17
  802.7 292.3 %copy-start.33 = (bf16[1024,16]{0,1:T(8,128)(2,1)S(1)}, bf16[1024,16]{0,1:T(8,128)(2,1)}, u32[]{:S(2)}) copy-start(bf16[1024,16]{0,1:T(8,128)(2,1)} %copy-done.32) | copy-start | bytes 98308
  1095.0 16.4 %copy-start.41 = (f32[1024]{0:T(1024)S(1)}, f32[1024]{0:T(1024)}, u32[]{:S(2)}) copy-start(f32[1024]{0:T(1024)} %copy-done.40) | copy-start | bytes 12292
  1292.1 5.1 copy-start.24
  1295.4 4.8 copy-start.28
  1297.1 4.1 copy-start.27
  1297.1 5.2 copy-start.31
  1297.2 6.1 copy-start.30
  (18 other events, 45.1 us)
Sparse Core Ops, SparseCore 0:
  9.9 28.7 all-gather.11
  40.5 26.8 all-gather.15
  69.2 35.3 all-gather.13
  106.3 35.2 all-gather.17
  143.3 35.2 all-gather.19
  180.4 65.7 all-gather.21
  248.1 65.7 all-gather.23
  315.8 65.7 all-gather.25
  713.8 27.7 reduce-scatter.12
  745.1 27.7 reduce-scatter.14
  775.9 35.1 reduce-scatter.22
  814.8 35.1 reduce-scatter.16
  852.9 35.1 reduce-scatter.18
  891.3 65.8 reduce-scatter.24
  960.2 65.7 reduce-scatter.26
  1029.2 65.7 reduce-scatter.28
  1098.4 23.3 reduce-scatter.30
  1124.9 22.4 reduce-scatter.20
  1150.4 141.6 all-reduce.10
where the time goes:
time: 1320 us; the launch traced here: 1310 us
  waiting for transfers between devices  470 us (36%)
  matrix products  359 us (27%)
  local copies, waits for them, and re-layouts  218 us (17%)
  other arithmetic  130 us (10%)
  blocking collectives  71.1 us (5%)
  loops' own time  44.2 us (3%)
  between operations  17.6 us (1%)
    psum x1, waiting for transfers between devices, local(): lax.psum(mixer_rows[1].astype(jnp.bfloat16), 'rep').astype(jnp.float32)  116 us
    dot_general x10, matrix products, right_trans(): lax.dot_general(left, right, (((1,), (1,)), ((), ())), preferred_element_...  72.9 us
    reduce_scatter x1, waiting for transfers between devices, local(): lax.psum_scatter(part_gate.astype(jnp.bfloat16), 'shard', scatter_dimensi...  69 us
    reduce_scatter x1, waiting for transfers between devices, local(): lax.psum_scatter(part_down.astype(jnp.bfloat16), 'shard', scatter_dimensi...  68.9 us
    reduce_scatter x1, waiting for transfers between devices, local(): lax.psum_scatter(part_up.astype(jnp.bfloat16), 'shard', scatter_dimension...  68.9 us
    dot_general x10, matrix products, matmul(): return jnp.dot(left, right, preferred_element_type=jnp.float32)  66.4 us
    squeeze x96, local copies, waits for them, and re-layouts, block_pass(): lax.scan(jax.checkpoint(advance), start, (shaped(query), shaped(keys), sh...  61.5 us
    dynamic_slice x80, local copies, waits for them, and re-layouts, block_pass(): lax.scan(jax.checkpoint(advance), start, (shaped(query), shaped(keys), sh...  59.3 us
  transfers between devices with their start and end apart: 19, of which 10 were waited for; matrix products, arithmetic and copies ran while one was open for 29% of the time, Pallas kernels for 0%

commit v1 on v0

v1 whole, which is shorter than its diff:
```python
import functools
import numpy as np
import jax, jax.numpy as jnp
from jax import lax
from jax.experimental import pallas as pl
from jax.experimental.pallas import tpu as pltpu
from jax.sharding import PartitionSpec as P
HEADS=4; KH=128; VH=256; C=128
SCALE=KH**-0.5
LEVELS=(64,32,16,8,4,2,1)
F32=jnp.float32; BF=jnp.bfloat16

def level_sums():
    t=np.arange(C)[:,None]; u=np.arange(C)[None,:]
    rows=[]
    for h in LEVELS:
        ref=(t//(2*h))*(2*h)+h-1
        second=t>ref
        rows.append(np.where(second,(u>ref)&(u<=t),(u>t)&(u<=ref)))
    rows.append(u<=t); rows.append(u>t)
    return np.concatenate(rows,0).astype(np.float32)

def dot(a,b): return lax.dot_general(a,b,(((1,),(0,)),((),())),preferred_element_type=F32)
def dot_nt(a,b): return lax.dot_general(a,b,(((1,),(1,)),((),())),preferred_element_type=F32)
def dot_tn(a,b): return lax.dot_general(a,b,(((0,),(0,)),((),())),preferred_element_type=F32)

def gate_in(r_ref,wh_ref,bias_ref):
    return dot(r_ref[...],wh_ref[...])+bias_ref[...]

def log_rate(zb):
    return (jnp.minimum(zb,0.0)-jnp.log1p(jnp.exp(-jnp.abs(zb))))*(1.0/16.0)

def level_map(segc,segr):
    t=lax.broadcasted_iota(jnp.int32,(C,C),0); s=lax.broadcasted_iota(jnp.int32,(C,C),1)
    x=t^s
    return jnp.where(segc==segr,x,-1),t,s

def fwd_body(q_ref,k_ref,v_ref,g_ref,r_ref,wh_ref,bias_ref,gain_ref,cols_ref,segr_ref,m_ref,y_ref,o_ref,st_ref,state,esc):
    i=pl.program_id(0)
    @pl.when(i==0)
    def _(): state[...]=jnp.zeros_like(state)
    f=log_rate(gate_in(r_ref,wh_ref,bias_ref)).astype(BF)
    esc[...]=jnp.exp(dot(m_ref[...],f))
    segc=cols_ref[:,0:1]; segr=segr_ref[i]
    lv,t,s=level_map(segc,segr)
    lv=jnp.where(t>=s,lv,-1)
    prev=jnp.where(i==0,-1,segr_ref[jnp.maximum(i-1,0)][:,C-1:C])
    last=segr[:,C-1:C]
    keep=(segc==prev).astype(F32); tail=(segc==last).astype(F32)
    stay=(prev==last).astype(F32)
    row=lax.broadcasted_iota(jnp.int32,(C,KH),0)
    nl=len(LEVELS)
    for h in range(HEADS):
        ks=slice(h*KH,(h+1)*KH); vs=slice(h*VH,(h+1)*VH)
        q=q_ref[:,ks].astype(F32)*SCALE; k=k_ref[:,ks].astype(F32); v=v_ref[:,vs]
        a=jnp.where(lv==0,dot_nt(q.astype(BF),k_ref[:,ks]),0.0)
        for l,hs in enumerate(LEVELS):
            x=(jnp.where((row&hs)!=0,q,k)*esc[l*C:(l+1)*C,ks]).astype(BF)
            a=jnp.where((lv>=hs)&(lv<2*hs),dot_nt(x,x),a)
        ec=esc[nl*C:(nl+1)*C,ks]; es=esc[(nl+1)*C:(nl+2)*C,ks]
        st=state[h]
        stb=st.astype(BF)
        st_ref[0,h]=stb
        o=dot(a.astype(BF),v)+dot_nt((q*ec*keep).astype(BF),stb)
        state[h]=st*(ec[C-1:C,:]*stay)+dot_tn(v,(k*es*tail).astype(BF))
        o_ref[:,vs]=o.astype(BF)
        m=lax.rsqrt(jnp.mean(o*o,axis=-1,keepdims=True)+1.0)
        g=g_ref[:,vs].astype(F32)
        y_ref[:,vs]=(o*m*gain_ref[...]*(g*jax.nn.sigmoid(g))).astype(BF)

def bwd_body(q_ref,k_ref,v_ref,g_ref,r_ref,o_ref,st_ref,dy_ref,wh_ref,bias_ref,gain_ref,cols_ref,segr_ref,m_ref,u_ref,
             dq_ref,dk_ref,dv_ref,dg_ref,dz_ref,gb_ref,gg_ref,dstate,rcar,esc,dcs):
    nc=pl.num_programs(0); step=pl.program_id(0); i=nc-1-step
    @pl.when(step==0)
    def _():
        dstate[...]=jnp.zeros_like(dstate); rcar[...]=jnp.zeros_like(rcar)
        gb_ref[...]=jnp.zeros_like(gb_ref); gg_ref[...]=jnp.zeros_like(gg_ref)
    zb=gate_in(r_ref,wh_ref,bias_ref)
    f=log_rate(zb).astype(BF)
    esc[...]=jnp.exp(dot(m_ref[...],f))
    segc=cols_ref[:,0:1]; segr=segr_ref[i]
    lv,t,s=level_map(segc,segr)
    lvu=jnp.where(t<=s,lv,-1)
    lower=t>=s
    prev=jnp.where(i==0,-1,segr_ref[jnp.maximum(i-1,0)][:,C-1:C])
    last=segr[:,C-1:C]
    keep=(segc==prev).astype(F32); tail=(segc==last).astype(F32)
    stay=(prev==last).astype(F32)
    row=lax.broadcasted_iota(jnp.int32,(C,KH),0)
    nl=len(LEVELS)
    gain=gain_ref[...]
    ggacc=jnp.zeros((1,VH),F32)
    for h in range(HEADS):
        ks=slice(h*KH,(h+1)*KH); vs=slice(h*VH,(h+1)*VH)
        o=o_ref[:,vs].astype(F32); g=g_ref[:,vs].astype(F32); dy=dy_ref[:,vs].astype(F32)
        m=lax.rsqrt(jnp.mean(o*o,axis=-1,keepdims=True)+1.0)
        sg=jax.nn.sigmoid(g); om=o*m
        u=dy*(g*sg)
        dg_ref[:,vs]=(dy*om*gain*(sg*(1.0+g*(1.0-sg)))).astype(BF)
        ggacc=ggacc+jnp.sum(u*om,axis=0,keepdims=True)
        ug=u*gain
        do=(m*ug-om*(m*m)*jnp.mean(ug*o,axis=-1,keepdims=True)).astype(BF)
        q=q_ref[:,ks].astype(F32)*SCALE; k=k_ref[:,ks].astype(F32); v=v_ref[:,vs]
        qb=q.astype(BF); kb=k_ref[:,ks]
        das=jnp.where(lower,dot_nt(do,v),dot_nt(v,do))
        dd=jnp.sum(jnp.where(t==s,das,0.0),axis=1,keepdims=True)
        at=jnp.where(lvu==0,dot_nt(kb,qb),0.0)
        ec=esc[nl*C:(nl+1)*C,ks]; es=esc[(nl+1)*C:(nl+2)*C,ks]
        stb=st_ref[0,h]
        ds=dstate[h]; dsb=ds.astype(BF)
        qe=(q*ec*keep).astype(BF); ke=(k*es*tail).astype(BF)
        dq=dd*k+dot(do,stb)*(ec*keep)
        dk=dd*q+dot(v,dsb)*(es*tail)
        for l,hs in enumerate(LEVELS):
            e=esc[l*C:(l+1)*C,ks]
            sec=(row&hs)!=0
            x=(jnp.where(sec,q,k)*e).astype(BF)
            sx=dot_nt(x,x)
            at=jnp.where((lvu>=hs)&(lvu<2*hs),sx,at)
            gl=jnp.where((lv>=hs)&(lv<2*hs),das,0.0).astype(BF)
            tt=dot(gl,x)*e
            dq=dq+jnp.where(sec,tt,0.0)
            dk=dk+jnp.where(sec,0.0,tt)
        dv_ref[:,vs]=(dot(at.astype(BF),do)+dot_nt(ke,dsb)).astype(BF)
        dq_ref[:,ks]=(dq*SCALE).astype(BF)
        dk_ref[:,ks]=dk.astype(BF)
        dsn=ds*(ec[C-1:C,:]*stay)+dot_tn(do,qe)
        dstate[h]=dsn
        dc=q*dq-k*dk
        hi=dc.astype(BF)
        dcs[:,ks]=hi; dcs[:,HEADS*KH+h*KH:HEADS*KH+(h+1)*KH]=(dc-hi.astype(F32)).astype(BF)
        rold=rcar[:,ks]
        rcar[:,ks]=jnp.sum(stb.astype(F32)*dsn,axis=0,keepdims=True)
        dcs2=rold
        um=jnp.where((lv>=0)&(t<=s),1.0,0.0).astype(BF)
        df=dot(um,dcs[:,ks])+dot(um,dcs[:,HEADS*KH+h*KH:HEADS*KH+(h+1)*KH])+tail*dcs2
        start=cols_ref[:,1:2]!=segc
        dp=jnp.where(start,0.0,df)*(jax.nn.sigmoid(-zb[:,ks])*(1.0/16.0))
        dz_ref[:,ks]=dp.astype(BF)
        gb_ref[:,ks]+=jnp.sum(dp,axis=0,keepdims=True)
    gg_ref[...]+=ggacc

def seg_views(segments):
    b,l=segments.shape
    seg=(segments+8*lax.broadcasted_iota(jnp.int32,(b,l),0)).reshape(-1)
    prev=jnp.concatenate([jnp.full((1,),-1,jnp.int32),seg[:-1]])
    cols=jnp.stack([seg,prev],axis=1)
    return cols,seg.reshape(-1,1,C)

def forward(q,k,v,g,r,wh,bias,gain,cols,segr):
    T=q.shape[0]; nc=T//C
    M=jnp.asarray(level_sums(),BF); nr=M.shape[0]
    blk=lambda w: pl.BlockSpec((C,w),lambda i:(i,0))
    full=lambda *sh: pl.BlockSpec(sh,lambda i:(0,)*len(sh))
    return pl.pallas_call(fwd_body,grid=(nc,),
        in_specs=[blk(512),blk(512),blk(1024),blk(1024),blk(16),full(16,512),full(1,512),full(1,256),blk(2),full(nc,1,C),full(nr,C)],
        out_specs=[blk(1024),blk(1024),pl.BlockSpec((1,HEADS,VH,KH),lambda i:(i,0,0,0))],
        out_shape=[jax.ShapeDtypeStruct((T,1024),BF),jax.ShapeDtypeStruct((T,1024),BF),jax.ShapeDtypeStruct((nc,HEADS,VH,KH),BF)],
        scratch_shapes=[pltpu.VMEM((HEADS,VH,KH),F32),pltpu.VMEM((nr,512),F32)],
        compiler_params=pltpu.CompilerParams(vmem_limit_bytes=48<<20),
        cost_estimate=pl.CostEstimate(flops=20_000_000_000,bytes_accessed=16_000_000,transcendentals=0),
        name="gla_fwd")(q,k,v,g,r,wh,bias,gain,cols,segr,M)

def backward(q,k,v,g,r,o,st,dy,wh,bias,gain,cols,segr):
    T=q.shape[0]; nc=T//C
    M=jnp.asarray(level_sums(),BF); nr=M.shape[0]
    blk=lambda w: pl.BlockSpec((C,w),lambda i:(nc-1-i,0))
    full=lambda *sh: pl.BlockSpec(sh,lambda i:(0,)*len(sh))
    sd=jax.ShapeDtypeStruct
    return pl.pallas_call(bwd_body,grid=(nc,),
        in_specs=[blk(512),blk(512),blk(1024),blk(1024),blk(16),blk(1024),pl.BlockSpec((1,HEADS,VH,KH),lambda i:(nc-1-i,0,0,0)),blk(1024),
                  full(16,512),full(1,512),full(1,256),blk(2),full(nc,1,C),full(nr,C),full(8,128)],
        out_specs=[blk(512),blk(512),blk(1024),blk(1024),blk(512),full(1,512),full(1,256)],
        out_shape=[sd((T,512),BF),sd((T,512),BF),sd((T,1024),BF),sd((T,1024),BF),sd((T,512),BF),sd((1,512),F32),sd((1,256),F32)],
        scratch_shapes=[pltpu.VMEM((HEADS,VH,KH),F32),pltpu.VMEM((1,512),F32),pltpu.VMEM((nr,512),F32),pltpu.VMEM((C,1024),BF)],
        compiler_params=pltpu.CompilerParams(vmem_limit_bytes=48<<20),
        cost_estimate=pl.CostEstimate(flops=40_000_000_000,bytes_accessed=24_000_000,transcendentals=0),
        name="gla_bwd")(q,k,v,g,r,o,st,dy,wh,bias,gain,cols,segr,M,jnp.zeros((8,128),F32))

MESH = pl.DeviceIdType.MESH


class Place:
    def __init__(self, n, reps):
        self.n, self.z = n, reps // 2
        self.rep = lax.axis_index("rep")
        self.me = lax.axis_index("shard")
        self.core = lax.rem(self.rep, 2)
        self.chip = self.rep // 2
        self.sib = (self.rep + 1 - 2 * self.core, self.me)

    def peer(self, step):
        return lax.rem(self.me + step, self.n)

    def flip(self, bit):
        if bit == 1:
            return self.me + 1 - 2 * lax.rem(self.me, 2)
        return lax.rem(self.me + 2, 4)

    def first(self):
        return jnp.where(self.core == 0, self.flip(1), self.flip(2))

    def second(self):
        return jnp.where(self.core == 0, self.flip(2), self.flip(1))


def greet(ids):
    barrier = pltpu.get_barrier_semaphore()
    for d in ids:
        pl.semaphore_signal(barrier, inc=1, device_id=d, device_id_type=MESH)
    pl.semaphore_wait(barrier, len(ids))


def remote(src, dst, ssem, rsem, device):
    return pltpu.make_async_remote_copy(
        src_ref=src, dst_ref=dst, send_sem=ssem, recv_sem=rsem, device_id=device, device_id_type=MESH
    )


def gather_sems(n, count):
    kinds = 2 * (n - 1)
    return [
        pltpu.SemaphoreType.DMA((count, kinds)),
        pltpu.SemaphoreType.DMA((count, kinds)),
        pltpu.SemaphoreType.DMA((count,)),
    ]


class Gather:
    def __init__(self, place, owns, fulls, sems):
        self.p, self.owns, self.fulls = place, owns, fulls
        self.ssem, self.rsem, self.lsem = sems

    def peers(self):
        p = self.p
        return [(p.rep, p.peer(j)) for j in range(1, p.n)] + [p.sib]

    def local(self, i):
        return pltpu.make_async_copy(self.owns[i], self.fulls[i].at[self.p.me], self.lsem.at[i])

    def direct(self, i, kind, target):
        p = self.p
        return remote(
            self.owns[i].at[p.core],
            self.fulls[i].at[p.me, p.core],
            self.ssem.at[i, kind],
            self.rsem.at[i, kind],
            (p.rep, target),
        )

    def onward(self, i, kind, block, device):
        p = self.p
        view = self.fulls[i].at[block, p.core]
        return remote(view, view, self.ssem.at[i, kind], self.rsem.at[i, kind], device)

    def start(self):
        p = self.p
        for i in range(len(self.owns)):
            if p.n == 4:
                self.direct(i, 0, p.first()).start()
                self.direct(i, 1, p.second()).start()
            else:
                for j in range(1, p.n):
                    self.direct(i, j - 1, p.peer(j)).start()
            self.local(i).start()

    def finish(self):
        p = self.p
        count = len(self.owns)
        last = p.n - 1
        if p.n == 4:
            blocks = [p.first(), p.second(), 3 - p.me]
            for i in range(count):
                self.direct(i, 1, blocks[1]).wait_recv()
                self.onward(i, 2, blocks[1], (p.rep, blocks[0])).start()
                self.onward(i, last + 1, blocks[1], p.sib).start()
                self.direct(i, 0, blocks[0]).wait_recv()
                self.onward(i, last, blocks[0], p.sib).start()
            for i in range(count):
                self.onward(i, 2, blocks[2], (p.rep, blocks[0])).wait_recv()
                self.onward(i, last + 2, blocks[2], p.sib).start()
        else:
            blocks = [p.peer(p.n - j) for j in range(1, p.n)]
            for i in range(count):
                for j in range(last):
                    self.direct(i, j, p.me).wait_recv()
                    self.onward(i, last + j, blocks[j], p.sib).start()
        for i in range(count):
            self.local(i).wait()
            for j in range(last):
                self.direct(i, j, p.me).wait_send()
                arrival = self.onward(i, last + j, blocks[j], p.sib)
                arrival.wait_send()
                arrival.wait_recv()


def halves(w):
    return w.reshape(2, w.shape[0] // 2, w.shape[1])


def gather_kernel(n, reps, count, *refs):
    pack = refs[0]
    owns = refs[1 : 1 + count]
    packs = refs[1 + count]
    fulls = refs[2 + count : 2 + 2 * count]
    psend, precv, plocal, *sems = refs[2 + 2 * count :]
    p = Place(n, reps)
    gather = Gather(p, owns, fulls, sems)
    greet(gather.peers())

    def small(j):
        return remote(pack, packs.at[p.me], psend.at[j - 1], precv.at[j - 1], (p.rep, p.peer(j)))

    for j in range(1, n):
        small(j).start()
    gather.start()
    here = pltpu.make_async_copy(pack, packs.at[p.me], plocal)
    here.start()
    gather.finish()
    here.wait()
    for j in range(1, n):
        small(j).wait()


def gather_weights(n, reps, pack, weights):
    count = len(weights)
    owns = [halves(w) for w in weights]
    outs = pl.pallas_call(
        functools.partial(gather_kernel, n, reps, count),
        out_shape=[jax.ShapeDtypeStruct((n,) + pack.shape, pack.dtype)]
        + [jax.ShapeDtypeStruct((n,) + o.shape, o.dtype) for o in owns],
        in_specs=[pl.BlockSpec(memory_space=pl.ANY)] * (1 + count),
        out_specs=[pl.BlockSpec(memory_space=pl.ANY)] * (1 + count),
        scratch_shapes=[
            pltpu.SemaphoreType.DMA((n - 1,)),
            pltpu.SemaphoreType.DMA((n - 1,)),
            pltpu.SemaphoreType.DMA,
        ]
        + gather_sems(n, count),
        compiler_params=pltpu.CompilerParams(collective_id=0, has_side_effects=True),
        name="gather_mixer",
    )(pack, *owns)
    return outs[0], [o.reshape(-1, w.shape[1]) for o, w in zip(outs[1:], weights)]


def add_rows(dst, a, b):
    rows, width = dst.shape
    slab = 32 if rows % 32 == 0 else 16

    def step(j, _):
        at = pl.ds(pl.multiple_of(j * slab, slab), slab)
        dst[at, :] = (a[at, :].astype(F32) + b[at, :].astype(F32)).astype(dst.dtype)
        return 0

    lax.fori_loop(0, rows // slab, step, 0)


class Reduce:
    STAGES = 7

    def __init__(self, place, part, out, cols, bufs, sems):
        self.p, self.part, self.out, self.cols = place, part, out, cols
        self.mine, self.other, self.group, self.ring = bufs
        self.ssem, self.rsem, self.lsem = sems
        self.square = place.n == 4
        self.line = place.z == 4
        self.zbase = place.n
        self.end = self.zbase + (3 if self.line else place.z - 1)
        self.total = self.ring.at[self.ring.shape[0] - 1]

    def copy(self, kind, src, dst, device):
        return remote(src, dst, self.ssem.at[kind], self.rsem.at[kind], device)

    def load(self):
        return pltpu.make_async_copy(self.part.at[:, self.p.core, :, self.cols], self.mine, self.lsem.at[0])

    def swap(self):
        return self.copy(0, self.part.at[:, 1 - self.p.core, :, self.cols], self.other, self.p.sib)

    def start(self):
        self.swap().start()
        self.load().start()

    def group_sends(self):
        p = self.p
        if self.square:
            to = (p.rep, p.first())
            return [
                self.copy(1, self.mine.at[p.first()], self.group.at[0], to),
                self.copy(2, self.mine.at[3 - p.me], self.group.at[1], to),
            ]
        return [
            self.copy(j, self.mine.at[p.peer(j)], self.group.at[j - 1], (p.rep, p.peer(j)))
            for j in range(1, p.n)
        ]

    def second_send(self):
        p = self.p
        return self.copy(3, self.mine.at[p.second()], self.group.at[2], (p.rep, p.second()))

    def line_send(self, step):
        p, own = self.p, self.mine.at[self.p.me]
        if step == 0:
            return self.copy(self.zbase, own, self.ring.at[0], (jnp.where(p.chip == 0, p.rep + 2, p.rep - 2), p.me))
        if step == 1:
            return self.copy(self.zbase + 1, own, self.ring.at[1], (jnp.where(p.chip == 1, p.rep + 2, p.rep - 2), p.me))
        return self.copy(
            self.zbase + 2, self.total, self.total, (jnp.where(p.chip == 1, p.rep - 2, p.rep + 2), p.me)
        )

    def ring_sends(self):
        p = self.p
        return [
            self.copy(
                self.zbase + j - 1, self.mine.at[p.me], self.ring.at[p.chip], (lax.rem(p.rep + 2 * j, 2 * p.z), p.me)
            )
            for j in range(1, p.z)
        ]

    def last_swap(self):
        half = self.out.at[self.p.core, :, self.cols]
        return self.copy(self.end, self.total, half, self.p.sib)

    def store(self):
        return pltpu.make_async_copy(self.total, self.out.at[self.p.core, :, self.cols], self.lsem.at[1])

    def stage(self, k):
        p = self.p
        own = self.mine.at[p.me]
        outer = (p.chip == 0) | (p.chip == 3)
        if k == 0:
            self.load().wait()
            self.swap().wait_recv()
            for b in range(p.n):
                add_rows(self.mine.at[b], self.mine.at[b], self.other.at[b])
            for c in self.group_sends():
                c.start()
        elif k == 1:
            sends = self.group_sends()
            for c in sends:
                c.wait_recv()
            add_rows(own, own, self.group.at[0])
            if self.square:
                rest = self.mine.at[p.second()]
                add_rows(rest, rest, self.group.at[1])
                self.second_send().start()
            else:
                for j in range(1, p.n - 1):
                    add_rows(own, own, self.group.at[j])
        elif k == 2:
            if self.square:
                self.second_send().wait_recv()
                add_rows(own, own, self.group.at[2])
            if self.line:

                @pl.when(outer)
                def _():
                    self.line_send(0).start()

            else:
                for c in self.ring_sends():
                    c.start()
        elif k == 3:
            if self.line:

                @pl.when(jnp.logical_not(outer))
                def _():
                    self.line_send(0).wait_recv()
                    add_rows(own, own, self.ring.at[0])
                    self.line_send(1).start()

            else:
                for c in self.ring_sends():
                    c.wait_recv()
                self.ring[p.chip] = self.mine[p.me]
                add_rows(self.total, self.ring.at[0], self.ring.at[1])
                for j in range(2, p.z):
                    add_rows(self.total, self.total, self.ring.at[j])
        elif k == 4:
            if self.line:

                @pl.when(jnp.logical_not(outer))
                def _():
                    self.line_send(1).wait_recv()
                    add_rows(self.total, own, self.ring.at[1])
                    self.line_send(2).start()

        elif k == 5:
            if self.line:

                @pl.when(outer)
                def _():
                    self.line_send(2).wait_recv()

            self.last_swap().start()
            self.store().start()
        else:
            self.last_swap().wait_recv()
            self.store().wait()

    def settle(self):
        p = self.p
        outer = (p.chip == 0) | (p.chip == 3)
        self.swap().wait_send()
        for c in self.group_sends():
            c.wait_send()
        if self.square:
            self.second_send().wait_send()
        if self.line:

            @pl.when(outer)
            def _():
                self.line_send(0).wait_send()

            @pl.when(jnp.logical_not(outer))
            def _():
                self.line_send(1).wait_send()
                self.line_send(2).wait_send()

        else:
            for c in self.ring_sends():
                c.wait_send()
        self.last_swap().wait_send()

    @staticmethod
    def peers(p):
        group = [(p.rep, p.peer(j)) for j in range(1, p.n)]
        along = [(lax.rem(p.rep + 2 * j, 2 * p.z), p.me) for j in range(1, p.z)]
        return group + along + [p.sib]

    @staticmethod
    def scratch(n, z, half, width):
        slots = 3 if z == 4 else z + 1
        kinds = n + (3 if z == 4 else z - 1) + 1
        return [
            pltpu.VMEM((n, half, width), BF),
            pltpu.VMEM((n, half, width), BF),
            pltpu.VMEM((n - 1, half, width), BF),
            pltpu.VMEM((slots, half, width), BF),
            pltpu.SemaphoreType.DMA((kinds,)),
            pltpu.SemaphoreType.DMA((kinds,)),
            pltpu.SemaphoreType.DMA((2,)),
        ]


class Small:
    def __init__(self, place, part, out, bufs, sems):
        self.p, self.part, self.out = place, part, out
        self.pair, self.other, self.group, self.ring = bufs
        self.ssem, self.rsem = sems

    def copy(self, kind, src, dst, device):
        return remote(src, dst, self.ssem.at[kind], self.rsem.at[kind], device)

    def swap(self):
        return self.copy(0, self.part, self.other, self.p.sib)

    def sends(self):
        p = self.p
        return [
            self.copy(j, self.pair.at[p.peer(j)], self.group.at[j - 1], (p.rep, p.peer(j))) for j in range(1, p.n)
        ]

    def along(self):
        p = self.p
        return [
            self.copy(p.n + j - 1, self.pair.at[p.me], self.ring.at[p.chip], (lax.rem(p.rep + 2 * j, 2 * p.z), p.me))
            for j in range(1, p.z)
        ]

    def stage(self, k):
        p = self.p
        if k == 0:
            self.swap().wait_recv()
            self.pair[...] = self.part[...] + self.other[...]
            for c in self.sends():
                c.start()
        elif k == 1:
            for c in self.sends():
                c.wait_recv()
            own = self.pair[p.me]
            for j in range(p.n - 1):
                own = own + self.group[j]
            self.pair[p.me] = own
            self.ring[p.chip] = own
            for c in self.along():
                c.start()
        else:
            for c in self.along():
                c.wait_recv()
            own = self.ring[0]
            for j in range(1, p.z):
                own = own + self.ring[j]
            self.out[...] = own

    def settle(self):
        self.swap().wait_send()
        for c in self.sends() + self.along():
            c.wait_send()

    @staticmethod
    def scratch(n, z, rows):
        return [
            pltpu.VMEM((n, rows, 128), F32),
            pltpu.VMEM((n, rows, 128), F32),
            pltpu.VMEM((n - 1, rows, 128), F32),
            pltpu.VMEM((z, rows, 128), F32),
            pltpu.SemaphoreType.DMA((n + z - 1,)),
            pltpu.SemaphoreType.DMA((n + z - 1,)),
        ]


def waves(items, small=None):
    stages = Reduce.STAGES
    for t in range(len(items) + stages - 1):
        for k in reversed(range(stages)):
            if 0 <= t - k < len(items):
                items[t - k].stage(k)
        if small is not None and t < 3:
            small.stage(t)


def reduce_kernel(n, reps, cuts, *refs):
    count = 1 + max(c[0] for c in cuts)
    parts, pack = refs[:count], refs[count]
    outs, packed = refs[count + 1 : 2 * count + 1], refs[2 * count + 1]
    scratch = refs[2 * count + 2 :]
    p = Place(n, reps)
    items = []
    for j, (which, at, width) in enumerate(cuts):
        mem = scratch[7 * j : 7 * j + 7]
        items.append(Reduce(p, parts[which], outs[which], pl.ds(at, width), mem[:4], mem[4:]))
    mem = scratch[7 * len(cuts) :]
    small = Small(p, pack, packed, mem[:4], mem[4:])
    greet(Reduce.peers(p))
    small.swap().start()
    for item in items:
        item.start()
    waves(items, small)
    for item in items:
        item.settle()
    small.settle()


def reduce_all(n, reps, partials, pieces, pack):
    z = reps // 2
    views = [q.reshape(n, 2, q.shape[0] // (2 * n), q.shape[1]) for q in partials]
    cuts, scratch = [], []
    for which, (view, cut) in enumerate(zip(views, pieces)):
        width = view.shape[3] // cut
        for j in range(cut):
            cuts.append((which, j * width, width))
            scratch += Reduce.scratch(n, z, view.shape[2], width)
    scratch += Small.scratch(n, z, pack.shape[1])
    anywhere = pl.BlockSpec(memory_space=pl.ANY)
    vmem = pl.BlockSpec(memory_space=pltpu.VMEM)
    outs = pl.pallas_call(
        functools.partial(reduce_kernel, n, reps, tuple(cuts)),
        out_shape=[jax.ShapeDtypeStruct(v.shape[1:], BF) for v in views]
        + [jax.ShapeDtypeStruct(pack.shape[1:], F32)],
        in_specs=[anywhere] * len(views) + [vmem],
        out_specs=[anywhere] * len(views) + [vmem],
        scratch_shapes=scratch,
        compiler_params=pltpu.CompilerParams(collective_id=2, has_side_effects=True, vmem_limit_bytes=60 << 20),
        name="reduce_grads",
    )(*views, pack)
    return [o.reshape(-1, o.shape[2]) for o in outs[:-1]], outs[-1]


def matmul(left, right):
    return jnp.dot(left, right, preferred_element_type=F32)


def rms_parts(values):
    return lax.rsqrt(jnp.mean(values * values, axis=-1, keepdims=True) + 1e-05)


def local(
    shards,
    reps,
    tokens,
    segments,
    cotangent,
    norm_mix,
    w_query,
    w_key,
    w_value,
    w_outgate,
    w_low,
    w_high,
    decay_bias,
    head_gain,
    w_out,
    norm_mlp,
    w_gate,
    w_up,
    w_down,
):
    small = (norm_mix, norm_mlp, decay_bias, head_gain, w_low, w_high)
    sizes = [a.size for a in small]
    rows = -(-sum(sizes) // 2048) * 16
    packed = jnp.concatenate([a.reshape(-1) for a in small])
    packed = jnp.pad(packed, (0, rows * 128 - sum(sizes))).reshape(rows, 128)
    packs, (query_w, key_w, value_w, outgate_w, out_w, gate_w, up_w, down_w) = gather_weights(
        shards, reps, packed, (w_query, w_key, w_value, w_outgate, w_out, w_gate, w_up, w_down)
    )
    packs = packs.reshape(shards, -1)
    offsets = np.cumsum([0] + sizes)
    cut = [packs[:, offsets[i] : offsets[i + 1]] for i in range(len(small))]
    gain_mix = cut[0].reshape(-1).astype(F32)
    gain_feed = cut[1].reshape(-1).astype(F32)
    bias = cut[2].reshape(1, -1).astype(F32)
    gain_head = cut[3].reshape(1, -1).astype(F32)
    low_w = cut[4].reshape(-1, w_low.shape[1])
    high_w = cut[5].reshape(shards, w_high.shape[0], -1).transpose(1, 0, 2).reshape(w_high.shape[0], -1)
    total = tokens.shape[0] * tokens.shape[1]
    width = tokens.shape[2]
    cols, segr = seg_views(segments)
    inputs = tokens.reshape(total, width).astype(F32)
    inv_mix = rms_parts(inputs)
    first = (inputs * inv_mix * gain_mix).astype(BF)
    query = matmul(first, query_w).astype(BF)
    keys = matmul(first, key_w).astype(BF)
    values = matmul(first, value_w).astype(BF)
    outgate = matmul(first, outgate_w).astype(BF)
    lowrank = matmul(first, low_w).astype(BF)
    mixed, heads, states = forward(
        query, keys, values, outgate, lowrank, high_w, bias, gain_head, cols, segr
    )
    resid = inputs + matmul(mixed, out_w)
    inv_feed = rms_parts(resid)
    second = (resid * inv_feed * gain_feed).astype(BF)
    gate = matmul(second, gate_w)
    upward = matmul(second, up_w)
    sigma = jax.nn.sigmoid(gate)
    swish = gate * sigma
    hidden = (swish * upward).astype(BF)
    result = (resid + matmul(hidden, down_w)).astype(BF)
    grad_out = cotangent.reshape(total, width)
    part_down = dot_tn(hidden, grad_out)
    grad_hidden = dot_nt(grad_out, down_w)
    slope = sigma * (1.0 + gate * (1.0 - sigma))
    grad_gate = (grad_hidden * upward * slope).astype(BF)
    grad_up = (grad_hidden * swish).astype(BF)
    part_gate = dot_tn(second, grad_gate)
    part_up = dot_tn(second, grad_up)
    grad_second = dot_nt(grad_gate, gate_w) + dot_nt(grad_up, up_w)
    part_norm_mlp = jnp.sum(grad_second * resid * inv_feed, axis=0)
    scaled = grad_second * gain_feed
    grad_resid = (
        grad_out.astype(F32)
        + inv_feed * scaled
        - resid * inv_feed**3 * jnp.mean(scaled * resid, axis=-1, keepdims=True)
    )
    branch = grad_resid.astype(BF)
    part_out = dot_tn(mixed, branch)
    grad_mixed = dot_nt(branch, out_w).astype(BF)
    grad_q, grad_k, grad_v, grad_g, grad_z, part_bias, part_head = backward(
        query, keys, values, outgate, lowrank, heads, states, grad_mixed, high_w, bias, gain_head, cols, segr
    )
    part_high = dot_tn(lowrank, grad_z)
    grad_low = dot_nt(grad_z, high_w).astype(BF)
    part_low = dot_tn(first, grad_low)
    part_query = dot_tn(first, grad_q)
    part_key = dot_tn(first, grad_k)
    part_value = dot_tn(first, grad_v)
    part_outgate = dot_tn(first, grad_g)
    grad_first = (
        dot_nt(grad_q, query_w)
        + dot_nt(grad_k, key_w)
        + dot_nt(grad_v, value_w)
        + dot_nt(grad_g, outgate_w)
        + dot_nt(grad_low, low_w)
    )
    part_norm_mix = jnp.sum(grad_first * inputs * inv_mix, axis=0)
    scaled_mix = grad_first * gain_mix
    grad_inputs = (
        grad_resid
        + inv_mix * scaled_mix
        - inputs * inv_mix**3 * jnp.mean(scaled_mix * inputs, axis=-1, keepdims=True)
    )
    parts = (
        part_norm_mix,
        part_norm_mlp,
        part_bias,
        part_head,
        part_low,
        part_high.reshape(w_high.shape[0], shards, -1).transpose(1, 0, 2),
    )
    pack = jnp.concatenate([p.reshape(shards, -1) for p in parts], axis=1)
    pack = jnp.pad(pack, ((0, 0), (0, rows * 128 - sum(sizes)))).reshape(shards, rows, 128)
    partials = (part_down, part_gate, part_up, part_out, part_query, part_key, part_value, part_outgate)
    sums, mine = reduce_all(shards, reps, [p.astype(BF) for p in partials], (2, 2, 2, 1, 1, 1, 1, 1), pack)
    sum_down, sum_gate, sum_up, sum_out, sum_query, sum_key, sum_value, sum_outgate = [s.astype(F32) for s in sums]
    mine = mine.reshape(-1)
    own = [mine[offsets[i] : offsets[i + 1]].reshape(small[i].shape) for i in range(len(small))]
    return (
        result.reshape(tokens.shape),
        grad_inputs.reshape(tokens.shape),
        own[0],
        sum_query,
        sum_key,
        sum_value,
        sum_outgate,
        own[4],
        own[5],
        own[2],
        own[3],
        sum_out,
        own[1],
        sum_gate,
        sum_up,
        sum_down,
    )


def solution(mesh):
    in_specs = (
        P(("rep", "shard"), None, None),
        P(("rep", "shard"), None),
        P(("rep", "shard"), None, None),
        P("shard"),
        P("shard", None),
        P("shard", None),
        P("shard", None),
        P("shard", None),
        P("shard", None),
        P(None, "shard"),
        P("shard"),
        P("shard"),
        P("shard", None),
        P("shard"),
        P("shard", None),
        P("shard", None),
        P("shard", None),
    )
    out_specs = (
        P(("rep", "shard"), None, None),
        P(("rep", "shard"), None, None),
        P("shard"),
        P("shard", None),
        P("shard", None),
        P("shard", None),
        P("shard", None),
        P("shard", None),
        P(None, "shard"),
        P("shard"),
        P("shard"),
        P("shard", None),
        P("shard"),
        P("shard", None),
        P("shard", None),
        P("shard", None),
    )
    return jax.shard_map(
        functools.partial(local, mesh.shape["shard"], mesh.shape["rep"]), mesh=mesh, in_specs=in_specs, out_specs=out_specs, check_vma=False)
```

time: 1320 us -> 619 us (0.47)
  waiting for transfers between devices: 470 us -> 0 us
  Pallas kernels: 0 us -> 410 us
  matrix products: 359 us -> 149 us
  local copies, waits for them, and re-layouts: 218 us -> 25.1 us
  other arithmetic: 130 us -> 24.4 us
  blocking collectives: 71.1 us -> 0 us
  loops' own time: 44.2 us -> 0 us
  between operations: 17.6 us -> 2.01 us
    pallas_call x0 -> x4, Pallas kernels: none -> 410 us  [the longest x1 200 us: gather_weights(): pl.pallas_call(functools.partial(gather_kernel, n, reps, count), out_shap...]
    reduce_scatter x9 -> x0, waiting for transfers between devices: 302 us -> none  [the longest x1 69 us: local(): lax.psum_scatter(part_gate.astype(jnp.bfloat16), 'shard', scatter_dimensi...]
    dot_general x238 -> x29, matrix products: 359 us -> 149 us  [the longest x10 57.9 us: dot_nt(): lax.dot_general(a, b, (((1,), (1,)), ((), ())), preferred_element_type=F32)]
    psum x1 -> x0, waiting for transfers between devices: 116 us -> none  [local(): lax.psum(mixer_rows[1].astype(jnp.bfloat16), 'rep').astype(jnp.float32)]
    squeeze x96 -> x0, local copies, waits for them, and re-layouts: 61.5 us -> none  [block_pass(): lax.scan(jax.checkpoint(advance), start, (shaped(query), shaped(keys), sh...]
    dynamic_slice x80 -> x0, local copies, waits for them, and re-layouts: 59.3 us -> none  [block_pass(): lax.scan(jax.checkpoint(advance), start, (shaped(query), shaped(keys), sh...]
    all_gather x8 -> x0, waiting for transfers between devices: 46.5 us -> none  [the longest x1 31.1 us: local(): lax.all_gather(w_down, 'shard', axis=0, tiled=True)]
    another operation x2 -> x0, loops' own time: 44.2 us -> none  [block_pass(): lax.scan(jax.checkpoint(advance), start, (shaped(query), shaped(keys), sh...]
  transfers between devices with their start and end apart: 19 -> 0, of which waited for: 10 -> 0; matrix products, arithmetic and copies ran while one was open for 29% -> 0% of each run, Pallas kernels for 0% -> 0%
where the time goes in v1:
time: 619 us; the launch traced here: 610 us
  Pallas kernels  410 us (66%)
  matrix products  149 us (24%)
  local copies, waits for them, and re-layouts  25.1 us (4%)
  other arithmetic  24.4 us (4%)
    pallas_call x1, Pallas kernels, gather_weights(): pl.pallas_call(functools.partial(gather_kernel, n, reps, count), out_shap...  200 us
    pallas_call x1, Pallas kernels, reduce_all(): pl.pallas_call(functools.partial(reduce_kernel, n, reps, tuple(cuts)), ou...  163 us
    dot_general x10, matrix products, dot_nt(): lax.dot_general(a, b, (((1,), (1,)), ((), ())), preferred_element_type=F32)  57.9 us
    dot_general x10, matrix products, dot_tn(): lax.dot_general(a, b, (((0,), (0,)), ((), ())), preferred_element_type=F32)  46.2 us
    dot_general x9, matrix products, matmul(): return jnp.dot(left, right, preferred_element_type=F32)  45.1 us
    pallas_call x1, Pallas kernels, backward(): pl.pallas_call(bwd_body, grid=(nc,), in_specs=[blk(512), blk(512), blk(10...  28.5 us
    unnamed x146, local copies, waits for them, and re-layouts  18.9 us
    pallas_call x1, Pallas kernels, forward(): pl.pallas_call(fwd_body, grid=(nc,), in_specs=[blk(512), blk(512), blk(10...  17.9 us

profile of v1, /device:TPU:1, one launch (start us, length us, event | category | flops | bytes accessed | tf_op | source)
XLA Modules:
  0.0 610.3 jit_solution(2066347296223723407)
XLA Ops:
  0.7 2.9 copy.71
  3.6 0.5 fusion.10
  4.1 0.8 multiply_multiply_fusion
  5.3 0.6 pad_bitcast_fusion.1.refs_0_
  5.9 200.2 %gather_mixer.1 = (bf16[4,64,128]{2,1,0:T(8,128)(2,1)}, bf16[4,2,128,512]{3,2,1,0:T(8,128)(2,1)}, bf16[4,2,128,512]{3,2,1,0:T(8,128)(2,1)}, bf16[4,2,128,1024]{3...) custom-call(bf16[64,128]{1,0:T(8,128)(2,1)} %pad_bitcast_fusion.1.re, ...), custom_call_target="tpu_custom_call" | custom-call | tf_op jit(solution)/shard_map/gather_mixer/pallas_call | solution.py:328
  206.0 0.9 copy.112
  207.1 0.2 reshape.367
  207.3 1.0 convolution_convert_fusion.13.r_ref
  208.3 0.7 copy-done.46
  209.0 3.9 convolution_convert_fusion.7.g_ref
  212.9 3.9 convolution_convert_fusion.8.v_ref
  216.9 1.4 convolution_convert_fusion.11.k_ref
  218.4 3.4 convolution_convert_fusion.12.q_ref
  222.1 0.5 copy-done.32
  222.9 17.9 %gla_fwd.1 = (bf16[1024,1024]{1,0:T(8,128)(2,1)S(1)}, bf16[1024,1024]{1,0:T(8,128)(2,1)}, bf16[8,4,256,128]{3,2,1,0:T(8,128)(2,1)}) custom-call(bf16[1024,512]{1,0:T(8,128)(2,1)S(1)} %convolution_convert_fusion.12.q_ref, bf16[1024,512]{1,0:T(8,128)(2,1)S(1)} %convolution_convert_fusion.11.k_ref, bf16[1024,1024]{1,0:T(8,128)(2,1)} %convolution_convert_fusion.8.v_ref, ...), custom_call_target="tpu_custom_call" | custom-call | flops 20000000000 | bytes 16000000 | tf_op jit(solution)/shard_map/gla_fwd/pallas_call | solution.py:155
  240.9 2.6 multiply_reduce_fusion.2
  243.6 0.4 multiply_convert_fusion.1
  244.0 0.3 slice-done.1
  244.3 9.1 %fusion.40 = f32[1024,2816]{1,0:T(8,128)} fusion(bf16[1024,1024]{0,1:T(8,128)(2,1)S(1)} %multiply_convert_fusion.1, bf16[1024,2816]{1,0:T(8,128)(2,1)S(1)} %bitcast.266), kind=kOutput, calls=%fused_computation.88 | convolution fusion | flops 5905580032 | bytes 19398656 | tf_op jit(solution)/shard_map/dot_general | solution.py:671
  253.5 9.1 %fusion.39 = f32[1024,2816]{1,0:T(8,128)} fusion(bf16[1024,1024]{0,1:T(8,128)(2,1)S(1)} %multiply_convert_fusion.1, bf16[1024,2816]{1,0:T(8,128)(2,1)S(1)} %bitcast.270), kind=kOutput, calls=%fused_computation.87 | convolution fusion | flops 5905580032 | bytes 19398656 | tf_op jit(solution)/shard_map/dot_general | solution.py:671
  262.6 21.5 %fusion.2 = (bf16[1024,2816]{1,0:T(8,128)(2,1)}, bf16[1024,2816]{1,0:T(8,128)(2,1)}, bf16[1024,2816]{1,0:T(8,128)(2,1)}) fusion(f32[1024,2816]{1,0:T(8,128)} %fusion.39, f32[1024,2816]{1,0:T(8,128)} %fusion.40, bf16[2816,1024]{1,0:T(8,128)(2,1)} %bitcast.261, bf16[1,1024,1024]{2,1,0:T(8,128)(2,1)S(1)} %copy-done.17), kind=kOutput, calls=%fused_computation.4 | convolution fusion | flops 5948833792 | bytes 48234496 | tf_op jit(solution)/shard_map/dot_general | solution.py:24
  284.2 10.0 %fusion.41 = f32[1024,1024]{0,1:T(8,128)S(1)} fusion(bf16[1024,2816]{1,0:T(8,128)(2,1)} %get-tuple-element.125, bf16[1024,2816]{1,0:T(8,128)(2,1)} %bitcast.267), kind=kOutput, calls=%fused_computation.89 | convolution fusion | flops 5905580032 | bytes 15728640 | tf_op jit(solution)/shard_map/dot_general | solution.py:24
  294.2 10.1 %multiply_reduce_fusion = (f32[1024]{0:T(1024)S(1)}, f32[1024]{0:T(1024)S(1)}, f32[1024,1024]{0,1:T(8,128)}) fusion(f32[1024,1024]{0,1:T(8,128)S(1)} %copy-done.15, f32[1024]{0:T(1024)S(1)} %get-tuple-element.134, f32[1024]{0:T(1024)S(1)} %bitcast.257, f32[1024,1024]{0,1:T(8,128)S(1)} %fusion.41, bf16[1024,2816]{1,0:T(8,128)(2,1)S(1)} %copy-done.56, ...), kind=kOutput, calls=%fused_computation.30 | convolution fusion | flops 5912918016 | bytes 24133632 | tf_op jit(solution)/shard_map/dot_general | solution.py:24
  304.4 2.9 copy.77
  307.2 4.7 multiply_subtract_fusion
  312.0 3.7 convolution_convert_fusion.6.dy_ref
  315.7 28.5 %gla_bwd.1 = (bf16[1024,512]{1,0:T(8,128)(2,1)S(1)}, bf16[1024,512]{1,0:T(8,128)(2,1)S(1)}, bf16[1024,1024]{1,0:T(8,128)(2,1)}, bf16[1024,1024]{1,0:T(8,128)(2,1...) custom-call(bf16[1024,512]{1,0:T(8,128)(2,1)S(1)} %copy-done.8, ...), custom_call_target="tpu_custom_call" | custom-call | flops 40000000000 | bytes 24000000 | tf_op jit(solution)/shard_map/gla_bwd/pallas_call | solution.py:170
  344.2 0.3 fusion.46
  344.6 0.4 convolution_convert_fusion.14
  345.0 3.2 fusion.33
  348.1 1.4 reshape.389
  349.5 2.5 fusion.43
  352.1 1.3 fusion.42
  353.4 0.3 copy-done.49
  353.6 0.6 copy-done.54
  354.3 2.4 fusion.44
  356.7 2.4 fusion.45
  359.1 3.6 fusion.18
  362.7 0.5 broadcast.120
  363.2 0.7 reduce.3
  364.2 0.7 copy.111
  364.8 6.7 %convolution_convert_fusion.5 = bf16[1024,1024]{1,0:T(8,128)(2,1)} fusion(bf16[1024,1024]{1,0:T(8,128)(2,1)} %copy-done.5, f32[1024,1024]{0,1:T(8,128)} %copy-done.16), kind=kOutput, calls=%fused_computation.45 | convolution fusion | flops 2149580800 | bytes 8388608 | tf_op jit(solution)/shard_map/dot_general | solution.py:25
  371.5 3.7 convolution_convert_fusion.4
  375.2 3.7 convolution_convert_fusion.3
  378.9 2.3 convolution_convert_fusion.10
  381.2 2.3 convolution_convert_fusion.9
  383.5 8.0 %convolution_convert_fusion.1 = bf16[1024,2816]{1,0:T(8,128)(2,1)} fusion(bf16[1024,1024]{0,1:T(8,128)(2,1)S(1)} %copy-done.20, bf16[1024,2816]{1,0:T(8,128)(2,1)S(1)} %bitcast.280), kind=kOutput, calls=%fused_computation.9 | convolution fusion | flops 5908463616 | bytes 13631488 | tf_op jit(solution)/shard_map/dot_general | solution.py:25
  391.5 8.1 %convolution_convert_fusion = bf16[1024,2816]{1,0:T(8,128)(2,1)} fusion(bf16[1024,1024]{0,1:T(8,128)(2,1)S(1)} %copy-done.20, bf16[1024,2816]{1,0:T(8,128)(2,1)S(1)} %bitcast.278), kind=kOutput, calls=%fused_computation.8 | convolution fusion | flops 5908463616 | bytes 13631488 | tf_op jit(solution)/shard_map/dot_general | solution.py:25
  399.6 8.1 %convolution_convert_fusion.2 = bf16[2816,1024]{1,0:T(8,128)(2,1)} fusion(bf16[1024,2816]{1,0:T(8,128)(2,1)S(1)} %bitcast.282, bf16[1,1024,1024]{2,1,0:T(8,128)(2,1)S(1)} %copy-done.18), kind=kOutput, calls=%fused_computation.10 | convolution fusion | flops 5908463616 | bytes 13631488 | tf_op jit(solution)/shard_map/dot_general | solution.py:25
  407.7 162.9 %reduce_grads.1 = (bf16[2,352,1024]{2,1,0:T(8,128)(2,1)}, bf16[2,128,2816]{2,1,0:T(8,128)(2,1)}, bf16[2,128,2816]{2,1,0:T(8,128)(2,1)}, bf16[2,128,1024]{2,1,0:T...) custom-call(bf16[4,2,352,1024]{3,2,1,0:T(8,128)(2,1)} %bitcast.214, ...), custom_call_target="tpu_custom_call" | custom-call | tf_op jit(solution)/shard_map/reduce_grads/pallas_call | solution.py:657
  570.7 4.9 bitcast_convert_fusion.1
  575.6 1.6 bitcast_convert_fusion.3
  577.3 2.0 bitcast_convert_fusion
  579.3 1.1 bitcast_convert_fusion.6
  580.5 1.1 bitcast_convert_fusion.5
  581.7 0.7 copy.90
  582.4 0.7 slice_bitcast_fusion
  583.1 0.6 slice_bitcast_fusion.1
  583.6 0.5 slice.80
  584.2 0.5 slice_bitcast_fusion.3
  584.7 6.5 %fusion.13 = f32[1,1024,1024]{1,2,0:T(8,128)} fusion(bf16[1,1024,1024]{1,2,0:T(8,128)(2,1)S(1)} %copy-done.13, f32[1024,1024]{0,1:T(8,128)} %copy-done.16, f32[1024,1024]{0,1:T(8,128)} %get-tuple-element.138, f32[1024]{0:T(1024)S(1)} %broadcast_multiply_fusion, f32[1024]{0:T(1024)S(1)} %copy-done.39, f32[1024]{0:T(1024)S(1)} %bitcast.255, f32[1024]{0:T(1024)S(1)} %copy-done.36), kind=kLoop, calls=%fused_computation.22 | loop fusion | flops 7340032 | bytes 14696448 | tf_op jit(solution)/shard_map/reshape | solution.py:799
  591.1 5.6 copy.89
  596.7 10.6 %fusion.21 = bf16[1,1024,1024]{1,2,0:T(8,128)(2,1)S(1)} fusion(f32[1024,1024]{0,1:T(8,128)} %copy-done.14, bf16[1024,2816]{1,0:T(8,128)(2,1)} %get-tuple-element.126, bf16[2816,1024]{1,0:T(8,128)(2,1)} %bitcast.262), kind=kOutput, calls=%fused_computation.37 | convolution fusion | flops 5907677184 | bytes 17825792 | tf_op jit(solution)/shard_map/dot_general | solution.py:671
  607.3 2.6 copy.88
  (161 shorter events, 1.7 us)
Async XLA Ops:
  0.6 4.2 copy-start.40
  0.7 4.5 copy-start.41
  0.7 4.5 copy-start.42
  0.7 4.5 copy-start.44
  0.7 4.5 copy-start.45
  0.7 4.5 copy-start.43
  3.6 213.3 %copy-start.9 = (bf16[1,1024,1024]{1,2,0:T(8,128)(2,1)}, bf16[1,1024,1024]{1,2,0:T(8,128)(2,1)S(1)}, u32[]{:S(2)}) copy-start(bf16[1,1024,1024]{1,2,0:T(8,128)(2,1)S(1)} %copy.71) | copy-start | bytes 6291460
  4.9 213.5 %copy-start.35 = (f32[1024]{0:T(1024)}, f32[1024]{0:T(1024)S(1)}, u32[]{:S(2)}) copy-start(f32[1024]{0:T(1024)S(1)} %get-tuple-element.132) | copy-start | bytes 12292
  207.0 11.4 %copy-start.37 = (f32[1,2,4,128]{3,1,2,0:T(2,128)}, f32[1,2,4,128]{3,1,2,0:T(2,128)S(1)}, u32[]{:S(2)}) copy-start(f32[1,2,4,128]{3,1,2,0:T(2,128)S(1)} %copy.103) | copy-start | bytes 12292
  207.3 5.6 copy-start.22
  207.3 1.7 copy-start.46
  209.0 3.9 copy-start.48
  212.9 3.9 copy-start.26
  218.3 4.5 copy-start.6
  218.4 3.6 copy-start.2
  218.4 4.5 copy-start.3
  221.8 19.1 %copy-start.7 = (bf16[1024,512]{1,0:T(8,128)(2,1)}, bf16[1024,512]{1,0:T(8,128)(2,1)S(1)}, u32[]{:S(2)}) copy-start(bf16[1024,512]{1,0:T(8,128)(2,1)S(1)} %convolution_convert_fusion.12.q_ref) | copy-start | bytes 3145732
  222.8 18.0 %copy-start = (s32[1024,2]{1,0:T(8,128)}, s32[1024,2]{1,0:T(8,128)S(1)}, u32[]{:S(2)}) copy-start(s32[1024,2]{1,0:T(8,128)S(1)} %copy.75.cols_ref) | copy-start | bytes 24580
  222.9 18.0 %copy-start.10 = (bf16[1,1024,1024]{1,2,0:T(8,128)(2,1)S(1)}, bf16[1,1024,1024]{1,2,0:T(8,128)(2,1)}, u32[]{:S(2)}) copy-start(bf16[1,1024,1024]{1,2,0:T(8,128)(2,1)} %copy-done.9) | copy-start | bytes 6291460
  222.9 18.0 %copy-start.50 = (bf16[4,2,128,1024]{3,2,1,0:T(8,128)(2,1)S(1)}, bf16[4,2,128,1024]{3,2,1,0:T(8,128)(2,1)}, u32[]{:S(2)}) copy-start(bf16[4,2,128,1024]{3,2,1,0:T(8,128)(2,1)} %get-tuple-element.50) | copy-start | bytes 6291460
  240.9 2.7 copy-start.5
  240.9 3.1 slice-start
  240.9 3.4 slice-start.1
  243.5 9.9 %copy-start.14 = (f32[1024,1024]{0,1:T(8,128)}, f32[1024,1024]{0,1:T(8,128)S(1)}, u32[]{:S(2)}) copy-start(f32[1024,1024]{0,1:T(8,128)S(1)} %get-tuple-element.136) | copy-start | bytes 12582916
  243.6 9.9 %slice-start.2 = ((s8[5767168]{0:T(1024)(128)(4,1)}), s8[4194304]{0:T(1024)(128)(4,1)S(1)}, s32[]{:S(2)}) async-start(s8[5767168]{0:T(1024)(128)(4,1)} %bitcast.268), calls=%async_computation.2 | async-start | bytes 8388608
  244.0 9.5 %copy-start.19 = (bf16[1024,1024]{0,1:T(8,128)(2,1)}, bf16[1024,1024]{0,1:T(8,128)(2,1)S(1)}, u32[]{:S(2)}) copy-start(bf16[1024,1024]{0,1:T(8,128)(2,1)S(1)} %multiply_convert_fusion.1) | copy-start | bytes 6291460
  244.3 9.2 %slice-start.3 = ((s8[5767168]{0:T(1024)(128)(4,1)}), s8[1572864]{0:T(1024)(128)(4,1)S(1)}, s32[]{:S(2)}) async-start(s8[5767168]{0:T(1024)(128)(4,1)} %bitcast.268), calls=%async_computation.3 | async-start | bytes 3145728
  253.5 9.1 %copy-start.17 = (bf16[1,1024,1024]{2,1,0:T(8,128)(2,1)S(1)}, bf16[1,1024,1024]{2,1,0:T(8,128)(2,1)}, u32[]{:S(2)}) copy-start(bf16[1,1024,1024]{2,1,0:T(8,128)(2,1)} %param.21) | copy-start | bytes 6291460
  284.2 10.0 %copy-start.15 = (f32[1024,1024]{0,1:T(8,128)S(1)}, f32[1024,1024]{0,1:T(8,128)}, u32[]{:S(2)}) copy-start(f32[1024,1024]{0,1:T(8,128)} %copy-done.14) | copy-start | bytes 12582916
  284.2 10.1 %copy-start.56 = (bf16[1024,2816]{1,0:T(8,128)(2,1)S(1)}, bf16[1024,2816]{1,0:T(8,128)(2,1)}, u32[]{:S(2)}) copy-start(bf16[1024,2816]{1,0:T(8,128)(2,1)} %get-tuple-element.124) | copy-start | bytes 17301508
  307.2 4.7 copy-start.51
  311.9 3.7 copy-start.16
  311.9 3.7 copy-start.1
  311.9 3.7 copy-start.4
  312.0 3.7 copy-start.8
  315.7 28.9 %copy-start.33 = (bf16[4,2048]{1,0:T(4,128)(2,1)S(1)}, bf16[4,2048]{1,0:T(4,128)(2,1)}, u32[]{:S(2)}) copy-start(bf16[4,2048]{1,0:T(4,128)(2,1)} %copy-done.32) | copy-start | bytes 49156
  315.7 29.2 %copy-start.36 = (f32[1024]{0:T(1024)S(1)}, f32[1024]{0:T(1024)}, u32[]{:S(2)}) copy-start(f32[1024]{0:T(1024)} %copy-done.35) | copy-start | bytes 12292
  315.7 29.2 %copy-start.38 = (f32[1,2,4,128]{3,1,2,0:T(2,128)S(1)}, f32[1,2,4,128]{3,1,2,0:T(2,128)}, u32[]{:S(2)}) copy-start(f32[1,2,4,128]{3,1,2,0:T(2,128)} %copy-done.37) | copy-start | bytes 12292
  348.1 4.0 copy-start.25
  352.1 2.2 copy-start.54
  354.3 2.4 copy-start.47
  354.3 2.4 copy-start.52
  356.7 2.4 copy-start.11
  356.7 2.4 copy-start.23
  364.8 6.7 %copy-start.12 = (bf16[1,1024,1024]{1,2,0:T(8,128)(2,1)S(1)}, bf16[1,1024,1024]{1,2,0:T(8,128)(2,1)}, u32[]{:S(2)}) copy-start(bf16[1,1024,1024]{1,2,0:T(8,128)(2,1)} %copy-done.9) | copy-start | bytes 6291460
  364.8 6.7 %copy-start.55 = (bf16[1024,1024]{1,0:T(8,128)(2,1)S(1)}, bf16[1024,1024]{1,0:T(8,128)(2,1)}, u32[]{:S(2)}) copy-start(bf16[1024,1024]{1,0:T(8,128)(2,1)} %get-tuple-element.58) | copy-start | bytes 6291460
  371.5 3.7 copy-start.53
  375.2 8.3 %slice-start.6 = ((s8[5767168]{0:T(1024)(128)(4,1)}), s8[4194304]{0:T(1024)(128)(4,1)S(1)}, s32[]{:S(2)}) async-start(s8[5767168]{0:T(1024)(128)(4,1)} %bitcast.279), calls=%async_computation.6 | async-start | bytes 8388608
  378.9 4.6 slice-start.7
  381.2 2.3 copy-start.20
  381.2 10.3 %slice-start.4 = ((s8[5767168]{0:T(1024)(128)(4,1)}), s8[4194304]{0:T(1024)(128)(4,1)S(1)}, s32[]{:S(2)}) async-start(s8[5767168]{0:T(1024)(128)(4,1)} %bitcast.277), calls=%async_computation.4 | async-start | bytes 8388608
  383.5 8.0 %slice-start.5 = ((s8[5767168]{0:T(1024)(128)(4,1)}), s8[1572864]{0:T(1024)(128)(4,1)S(1)}, s32[]{:S(2)}) async-start(s8[5767168]{0:T(1024)(128)(4,1)} %bitcast.277), calls=%async_computation.5 | async-start | bytes 3145728
  383.5 16.1 %slice-start.8 = ((s8[5767168]{0:T(1024)(128)(4,1)}), s8[1572864]{0:T(1024)(128)(4,1)S(1)}, s32[]{:S(2)}) async-start(s8[5767168]{0:T(1024)(128)(4,1)} %bitcast.281), calls=%async_computation.8 | async-start | bytes 3145728
  391.5 8.1 %copy-start.18 = (bf16[1,1024,1024]{2,1,0:T(8,128)(2,1)S(1)}, bf16[1,1024,1024]{2,1,0:T(8,128)(2,1)}, u32[]{:S(2)}) copy-start(bf16[1,1024,1024]{2,1,0:T(8,128)(2,1)} %param.21) | copy-start | bytes 6291460
  391.5 8.1 %slice-start.9 = ((s8[5767168]{0:T(1024)(128)(4,1)}), s8[4194304]{0:T(1024)(128)(4,1)S(1)}, s32[]{:S(2)}) async-start(s8[5767168]{0:T(1024)(128)(4,1)} %bitcast.281), calls=%async_computation.9 | async-start | bytes 8388608
  570.7 4.9 copy-start.28
  570.7 4.9 copy-start.29
  570.7 6.6 %copy-start.21 = (bf16[2,352,1024]{2,1,0:T(8,128)(2,1)S(1)}, bf16[2,352,1024]{2,1,0:T(8,128)(2,1)}, u32[]{:S(2)}) copy-start(bf16[2,352,1024]{2,1,0:T(8,128)(2,1)} %get-tuple-element.71) | copy-start | bytes 4325380
  575.6 3.7 copy-start.30
  575.6 3.7 copy-start.31
  575.6 4.8 copy-start.27
  577.3 4.3 copy-start.34
  577.3 7.4 %copy-start.13 = (bf16[1,1024,1024]{1,2,0:T(8,128)(2,1)S(1)}, bf16[1,1024,1024]{1,2,0:T(8,128)(2,1)}, u32[]{:S(2)}) copy-start(bf16[1,1024,1024]{1,2,0:T(8,128)(2,1)} %copy-done.9) | copy-start | bytes 6291460
  577.3 7.4 %copy-start.39 = (f32[1024]{0:T(1024)S(1)}, f32[1024]{0:T(1024)}, u32[]{:S(2)}) copy-start(f32[1024]{0:T(1024)} %get-tuple-element.131) | copy-start | bytes 12292
  (3 other events, 3.8 us)

commit v2 on v1

--- a/solution.py
+++ b/solution.py
@@ -68,13 +68,8 @@
         g=g_ref[:,vs].astype(F32)
         y_ref[:,vs]=(o*m*gain_ref[...]*(g*jax.nn.sigmoid(g))).astype(BF)
 
-def bwd_body(q_ref,k_ref,v_ref,g_ref,r_ref,o_ref,st_ref,dy_ref,wh_ref,bias_ref,gain_ref,cols_ref,segr_ref,m_ref,u_ref,
+def bwd_chunk(i,q_ref,k_ref,v_ref,g_ref,r_ref,o_ref,st_ref,dy_ref,wh_ref,bias_ref,gain_ref,cols_ref,segr_ref,m_ref,
              dq_ref,dk_ref,dv_ref,dg_ref,dz_ref,gb_ref,gg_ref,dstate,rcar,esc,dcs):
-    nc=pl.num_programs(0); step=pl.program_id(0); i=nc-1-step
-    @pl.when(step==0)
-    def _():
-        dstate[...]=jnp.zeros_like(dstate); rcar[...]=jnp.zeros_like(rcar)
-        gb_ref[...]=jnp.zeros_like(gb_ref); gg_ref[...]=jnp.zeros_like(gg_ref)
     zb=gate_in(r_ref,wh_ref,bias_ref)
     f=log_rate(zb).astype(BF)
     esc[...]=jnp.exp(dot(m_ref[...],f))
@@ -161,21 +156,6 @@
         cost_estimate=pl.CostEstimate(flops=20_000_000_000,bytes_accessed=16_000_000,transcendentals=0),
         name="gla_fwd")(q,k,v,g,r,wh,bias,gain,cols,segr,M)
 
-def backward(q,k,v,g,r,o,st,dy,wh,bias,gain,cols,segr):
-    T=q.shape[0]; nc=T//C
-    M=jnp.asarray(level_sums(),BF); nr=M.shape[0]
-    blk=lambda w: pl.BlockSpec((C,w),lambda i:(nc-1-i,0))
-    full=lambda *sh: pl.BlockSpec(sh,lambda i:(0,)*len(sh))
-    sd=jax.ShapeDtypeStruct
-    return pl.pallas_call(bwd_body,grid=(nc,),
-        in_specs=[blk(512),blk(512),blk(1024),blk(1024),blk(16),blk(1024),pl.BlockSpec((1,HEADS,VH,KH),lambda i:(nc-1-i,0,0,0)),blk(1024),
-                  full(16,512),full(1,512),full(1,256),blk(2),full(nc,1,C),full(nr,C),full(8,128)],
-        out_specs=[blk(512),blk(512),blk(1024),blk(1024),blk(512),full(1,512),full(1,256)],
-        out_shape=[sd((T,512),BF),sd((T,512),BF),sd((T,1024),BF),sd((T,1024),BF),sd((T,512),BF),sd((1,512),F32),sd((1,256),F32)],
-        scratch_shapes=[pltpu.VMEM((HEADS,VH,KH),F32),pltpu.VMEM((1,512),F32),pltpu.VMEM((nr,512),F32),pltpu.VMEM((C,1024),BF)],
-        compiler_params=pltpu.CompilerParams(vmem_limit_bytes=48<<20),
-        cost_estimate=pl.CostEstimate(flops=40_000_000_000,bytes_accessed=24_000_000,transcendentals=0),
-        name="gla_bwd")(q,k,v,g,r,o,st,dy,wh,bias,gain,cols,segr,M,jnp.zeros((8,128),F32))
 
 MESH = pl.DeviceIdType.MESH
 
@@ -218,25 +198,24 @@
 
 
 def gather_sems(n, count):
-    kinds = 2 * (n - 1)
-    return [
-        pltpu.SemaphoreType.DMA((count, kinds)),
-        pltpu.SemaphoreType.DMA((count, kinds)),
-        pltpu.SemaphoreType.DMA((count,)),
-    ]
+    kinds = 2 * (n - 1) + 1
+    return [pltpu.SemaphoreType.DMA((count, kinds)), pltpu.SemaphoreType.DMA((count, kinds))]
 
 
 class Gather:
     def __init__(self, place, owns, fulls, sems):
         self.p, self.owns, self.fulls = place, owns, fulls
-        self.ssem, self.rsem, self.lsem = sems
+        self.ssem, self.rsem = sems
 
     def peers(self):
         p = self.p
         return [(p.rep, p.peer(j)) for j in range(1, p.n)] + [p.sib]
 
-    def local(self, i):
-        return pltpu.make_async_copy(self.owns[i], self.fulls[i].at[self.p.me], self.lsem.at[i])
+    def same(self, i):
+        kind = 2 * (self.p.n - 1)
+        return remote(
+            self.owns[i], self.fulls[i].at[self.p.me], self.ssem.at[i, kind], self.rsem.at[i, kind], self.p.sib
+        )
 
     def direct(self, i, kind, target):
         p = self.p
@@ -262,7 +241,7 @@
             else:
                 for j in range(1, p.n):
                     self.direct(i, j - 1, p.peer(j)).start()
-            self.local(i).start()
+            self.same(i).start()
 
     def finish(self):
         p = self.p
@@ -286,7 +265,7 @@
                     self.direct(i, j, p.me).wait_recv()
                     self.onward(i, last + j, blocks[j], p.sib).start()
         for i in range(count):
-            self.local(i).wait()
+            self.same(i).wait()
             for j in range(last):
                 self.direct(i, j, p.me).wait_send()
                 arrival = self.onward(i, last + j, blocks[j], p.sib)
@@ -344,7 +323,7 @@
 
 
 def add_rows(dst, a, b):
-    rows, width = dst.shape
+    rows = dst.shape[0]
     slab = 32 if rows % 32 == 0 else 16
 
     def step(j, _):
@@ -358,99 +337,114 @@
 class Reduce:
     STAGES = 7
 
-    def __init__(self, place, part, out, cols, bufs, sems):
-        self.p, self.part, self.out, self.cols = place, part, out, cols
-        self.mine, self.other, self.group, self.ring = bufs
-        self.ssem, self.rsem, self.lsem = sems
+    def __init__(self, place, out, bufs, sems, mine=None, give=None, paired=None):
+        self.p, self.out = place, out
+        self.mine, self.give, self.paired = mine, give, paired
         self.square = place.n == 4
         self.line = place.z == 4
+        bufs = list(bufs)
+        if paired is None:
+            self.other = bufs.pop(0)
+            self.own, self.rest = mine.at[place.me], mine.at[place.second()]
+        else:
+            self.kept = bufs.pop(0)
+            self.own, self.rest = self.kept.at[0], self.kept.at[1 if self.square else 0]
+        self.group, self.ring = bufs
+        self.ssem, self.rsem, self.lsem = sems
         self.zbase = place.n
         self.end = self.zbase + (3 if self.line else place.z - 1)
-        self.total = self.ring.at[self.ring.shape[0] - 1]
+        self.total = self.ring.at[2] if self.line else self.group.at[0]
 
     def copy(self, kind, src, dst, device):
         return remote(src, dst, self.ssem.at[kind], self.rsem.at[kind], device)
 
-    def load(self):
-        return pltpu.make_async_copy(self.part.at[:, self.p.core, :, self.cols], self.mine, self.lsem.at[0])
+    def loads(self):
+        p = self.p
+        which = [p.me, p.second()] if self.square else [p.me]
+        return [
+            pltpu.make_async_copy(self.paired.at[b], self.kept.at[j], self.lsem.at[j]) for j, b in enumerate(which)
+        ]
 
     def swap(self):
-        return self.copy(0, self.part.at[:, 1 - self.p.core, :, self.cols], self.other, self.p.sib)
+        return self.copy(0, self.give, self.other, self.p.sib)
 
     def start(self):
-        self.swap().start()
-        self.load().start()
+        if self.paired is None:
+            self.swap().start()
+        else:
+            for c in self.loads() + self.group_sends():
+                c.start()
+
+    def source(self, b):
+        return self.mine.at[b] if self.paired is None else self.paired.at[b]
 
     def group_sends(self):
         p = self.p
         if self.square:
             to = (p.rep, p.first())
             return [
-                self.copy(1, self.mine.at[p.first()], self.group.at[0], to),
-                self.copy(2, self.mine.at[3 - p.me], self.group.at[1], to),
+                self.copy(1, self.source(p.first()), self.group.at[0], to),
+                self.copy(2, self.source(3 - p.me), self.group.at[1], to),
             ]
         return [
-            self.copy(j, self.mine.at[p.peer(j)], self.group.at[j - 1], (p.rep, p.peer(j)))
-            for j in range(1, p.n)
+            self.copy(j, self.source(p.peer(j)), self.group.at[j - 1], (p.rep, p.peer(j))) for j in range(1, p.n)
         ]
 
     def second_send(self):
         p = self.p
-        return self.copy(3, self.mine.at[p.second()], self.group.at[2], (p.rep, p.second()))
+        return self.copy(3, self.rest, self.group.at[2], (p.rep, p.second()))
 
     def line_send(self, step):
-        p, own = self.p, self.mine.at[self.p.me]
+        p = self.p
         if step == 0:
-            return self.copy(self.zbase, own, self.ring.at[0], (jnp.where(p.chip == 0, p.rep + 2, p.rep - 2), p.me))
+            to = jnp.where(p.chip == 0, p.rep + 2, p.rep - 2)
+            return self.copy(self.zbase, self.own, self.ring.at[0], (to, p.me))
         if step == 1:
-            return self.copy(self.zbase + 1, own, self.ring.at[1], (jnp.where(p.chip == 1, p.rep + 2, p.rep - 2), p.me))
-        return self.copy(
-            self.zbase + 2, self.total, self.total, (jnp.where(p.chip == 1, p.rep - 2, p.rep + 2), p.me)
-        )
+            to = jnp.where(p.chip == 1, p.rep + 2, p.rep - 2)
+            return self.copy(self.zbase + 1, self.own, self.ring.at[1], (to, p.me))
+        to = jnp.where(p.chip == 1, p.rep - 2, p.rep + 2)
+        return self.copy(self.zbase + 2, self.total, self.total, (to, p.me))
 
     def ring_sends(self):
         p = self.p
         return [
-            self.copy(
-                self.zbase + j - 1, self.mine.at[p.me], self.ring.at[p.chip], (lax.rem(p.rep + 2 * j, 2 * p.z), p.me)
-            )
+            self.copy(self.zbase + j - 1, self.own, self.ring.at[p.chip], (lax.rem(p.rep + 2 * j, 2 * p.z), p.me))
             for j in range(1, p.z)
         ]
 
     def last_swap(self):
-        half = self.out.at[self.p.core, :, self.cols]
-        return self.copy(self.end, self.total, half, self.p.sib)
+        return self.copy(self.end, self.total, self.out(self.p.core), self.p.sib)
 
     def store(self):
-        return pltpu.make_async_copy(self.total, self.out.at[self.p.core, :, self.cols], self.lsem.at[1])
+        return pltpu.make_async_copy(self.total, self.out(self.p.core), self.lsem.at[2])
 
     def stage(self, k):
         p = self.p
-        own = self.mine.at[p.me]
         outer = (p.chip == 0) | (p.chip == 3)
         if k == 0:
-            self.load().wait()
-            self.swap().wait_recv()
-            for b in range(p.n):
-                add_rows(self.mine.at[b], self.mine.at[b], self.other.at[b])
+            if self.paired is None:
+                self.swap().wait_recv()
+                for b in range(p.n):
+                    add_rows(self.mine.at[b], self.mine.at[b], self.other.at[b])
+                for c in self.group_sends():
+                    c.start()
+        elif k == 1:
+            if self.paired is not None:
+                for c in self.loads():
+                    c.wait()
             for c in self.group_sends():
-                c.start()
-        elif k == 1:
-            sends = self.group_sends()
-            for c in sends:
                 c.wait_recv()
-            add_rows(own, own, self.group.at[0])
+            add_rows(self.own, self.own, self.group.at[0])
             if self.square:
-                rest = self.mine.at[p.second()]
-                add_rows(rest, rest, self.group.at[1])
+                add_rows(self.rest, self.rest, self.group.at[1])
                 self.second_send().start()
             else:
                 for j in range(1, p.n - 1):
-                    add_rows(own, own, self.group.at[j])
+                    add_rows(self.own, self.own, self.group.at[j])
         elif k == 2:
             if self.square:
                 self.second_send().wait_recv()
-                add_rows(own, own, self.group.at[2])
+                add_rows(self.own, self.own, self.group.at[2])
             if self.line:
 
                 @pl.when(outer)
@@ -466,13 +460,13 @@
                 @pl.when(jnp.logical_not(outer))
                 def _():
                     self.line_send(0).wait_recv()
-                    add_rows(own, own, self.ring.at[0])
+                    add_rows(self.own, self.own, self.ring.at[0])
                     self.line_send(1).start()
 
             else:
                 for c in self.ring_sends():
                     c.wait_recv()
-                self.ring[p.chip] = self.mine[p.me]
+                self.ring[p.chip] = self.own[...]
                 add_rows(self.total, self.ring.at[0], self.ring.at[1])
                 for j in range(2, p.z):
                     add_rows(self.total, self.total, self.ring.at[j])
@@ -482,7 +476,7 @@
                 @pl.when(jnp.logical_not(outer))
                 def _():
                     self.line_send(1).wait_recv()
-                    add_rows(self.total, own, self.ring.at[1])
+                    add_rows(self.total, self.own, self.ring.at[1])
                     self.line_send(2).start()
 
         elif k == 5:
@@ -501,7 +495,8 @@
     def settle(self):
         p = self.p
         outer = (p.chip == 0) | (p.chip == 3)
-        self.swap().wait_send()
+        if self.paired is None:
+            self.swap().wait_send()
         for c in self.group_sends():
             c.wait_send()
         if self.square:
@@ -529,17 +524,16 @@
         return group + along + [p.sib]
 
     @staticmethod
-    def scratch(n, z, half, width):
-        slots = 3 if z == 4 else z + 1
+    def scratch(n, z, half, width, paired):
+        slots = 3 if z == 4 else z
         kinds = n + (3 if z == 4 else z - 1) + 1
         return [
-            pltpu.VMEM((n, half, width), BF),
-            pltpu.VMEM((n, half, width), BF),
+            pltpu.VMEM(((2 if n == 4 else 1) if paired else n, half, width), BF),
             pltpu.VMEM((n - 1, half, width), BF),
             pltpu.VMEM((slots, half, width), BF),
             pltpu.SemaphoreType.DMA((kinds,)),
             pltpu.SemaphoreType.DMA((kinds,)),
-            pltpu.SemaphoreType.DMA((2,)),
+            pltpu.SemaphoreType.DMA((3,)),
         ]
 
 
@@ -599,72 +593,188 @@
             c.wait_send()
 
     @staticmethod
-    def scratch(n, z, rows):
+    def scratch(n, z, rows, width):
         return [
-            pltpu.VMEM((n, rows, 128), F32),
-            pltpu.VMEM((n, rows, 128), F32),
-            pltpu.VMEM((n - 1, rows, 128), F32),
-            pltpu.VMEM((z, rows, 128), F32),
+            pltpu.VMEM((n, rows, width), F32),
+            pltpu.VMEM((n, rows, width), F32),
+            pltpu.VMEM((n - 1, rows, width), F32),
+            pltpu.VMEM((z, rows, width), F32),
             pltpu.SemaphoreType.DMA((n + z - 1,)),
             pltpu.SemaphoreType.DMA((n + z - 1,)),
         ]
 
 
-def waves(items, small=None):
-    stages = Reduce.STAGES
-    for t in range(len(items) + stages - 1):
-        for k in reversed(range(stages)):
-            if 0 <= t - k < len(items):
-                items[t - k].stage(k)
-        if small is not None and t < 3:
-            small.stage(t)
-
-
-def reduce_kernel(n, reps, cuts, *refs):
-    count = 1 + max(c[0] for c in cuts)
-    parts, pack = refs[:count], refs[count]
-    outs, packed = refs[count + 1 : 2 * count + 1], refs[2 * count + 1]
-    scratch = refs[2 * count + 2 :]
+def pair_kernel(n, reps, count, *refs):
+    parts, outs = refs[:count], refs[count : 2 * count]
+    scratch = refs[2 * count :]
     p = Place(n, reps)
-    items = []
-    for j, (which, at, width) in enumerate(cuts):
-        mem = scratch[7 * j : 7 * j + 7]
-        items.append(Reduce(p, parts[which], outs[which], pl.ds(at, width), mem[:4], mem[4:]))
-    mem = scratch[7 * len(cuts) :]
-    small = Small(p, pack, packed, mem[:4], mem[4:])
-    greet(Reduce.peers(p))
-    small.swap().start()
-    for item in items:
-        item.start()
-    waves(items, small)
-    for item in items:
-        item.settle()
-    small.settle()
-
-
-def reduce_all(n, reps, partials, pieces, pack):
-    z = reps // 2
+    greet([p.sib])
+    work = []
+    for i in range(count):
+        mine, other, sems, lsem = scratch[4 * i : 4 * i + 4]
+        swap = remote(parts[i].at[:, 1 - p.core], other, sems.at[0], sems.at[1], p.sib)
+        load = pltpu.make_async_copy(parts[i].at[:, p.core], mine, lsem.at[0])
+        store = pltpu.make_async_copy(mine, outs[i], lsem.at[1])
+        swap.start()
+        load.start()
+        work.append((mine, other, swap, load, store))
+    for mine, other, swap, load, store in work:
+        load.wait()
+        swap.wait_recv()
+        for b in range(n):
+            add_rows(mine.at[b], mine.at[b], other.at[b])
+        store.start()
+    for mine, other, swap, load, store in work:
+        store.wait()
+        swap.wait_send()
+
+
+def pair_sums(n, reps, partials):
     views = [q.reshape(n, 2, q.shape[0] // (2 * n), q.shape[1]) for q in partials]
-    cuts, scratch = [], []
-    for which, (view, cut) in enumerate(zip(views, pieces)):
-        width = view.shape[3] // cut
-        for j in range(cut):
-            cuts.append((which, j * width, width))
-            scratch += Reduce.scratch(n, z, view.shape[2], width)
-    scratch += Small.scratch(n, z, pack.shape[1])
+    scratch = []
+    for v in views:
+        shape = (n,) + v.shape[2:]
+        scratch += [pltpu.VMEM(shape, BF), pltpu.VMEM(shape, BF), pltpu.SemaphoreType.DMA((2,)), pltpu.SemaphoreType.DMA((2,))]
     anywhere = pl.BlockSpec(memory_space=pl.ANY)
-    vmem = pl.BlockSpec(memory_space=pltpu.VMEM)
-    outs = pl.pallas_call(
-        functools.partial(reduce_kernel, n, reps, tuple(cuts)),
-        out_shape=[jax.ShapeDtypeStruct(v.shape[1:], BF) for v in views]
-        + [jax.ShapeDtypeStruct(pack.shape[1:], F32)],
-        in_specs=[anywhere] * len(views) + [vmem],
-        out_specs=[anywhere] * len(views) + [vmem],
+    return pl.pallas_call(
+        functools.partial(pair_kernel, n, reps, len(views)),
+        out_shape=[jax.ShapeDtypeStruct((n,) + v.shape[2:], BF) for v in views],
+        in_specs=[anywhere] * len(views),
+        out_specs=[anywhere] * len(views),
         scratch_shapes=scratch,
-        compiler_params=pltpu.CompilerParams(collective_id=2, has_side_effects=True, vmem_limit_bytes=60 << 20),
-        name="reduce_grads",
-    )(*views, pack)
-    return [o.reshape(-1, o.shape[2]) for o in outs[:-1]], outs[-1]
+        compiler_params=pltpu.CompilerParams(collective_id=1, has_side_effects=True, vmem_limit_bytes=40 << 20),
+        name="pair_sums",
+    )(*views)
+
+
+def backward_kernel(n,reps,plan,half,*refs):
+    (q_ref,k_ref,v_ref,g_ref,r_ref,o_ref,st_ref,dy_ref,a_ref,x_ref,dx_ref,cols_ref,
+     wh_ref,bias_ref,gain_ref,gmix_ref,nmlp_ref,segr_ref,m_ref,wq_ref,wk_ref,wv_ref,wg_ref,wl_ref)=refs[:24]
+    paired=refs[24:28]
+    gt_ref,small_ref=refs[28:30]
+    outs=refs[30:38]
+    dstate,rcar,esc,dcs,dall,at_ref,dz_ref,low_acc,high_acc,gb_ref,gg_ref,nmix_ref,smb,both=refs[38:52]
+    rest=refs[52:]
+    steps=pl.num_programs(0); step=pl.program_id(0); nc=steps-1
+    p=Place(n,reps)
+    items=[]
+    for j,(which,at,width,source) in enumerate(plan):
+        mem=rest[6*j:6*j+6]
+        cols=pl.ds(at,width)
+        out=lambda c,which=which,cols=cols: outs[which].at[c,:,cols]
+        if source is None:
+            items.append(Reduce(p,out,mem[:3],mem[3:],paired=paired[which].at[:,:,cols]))
+        else:
+            cols=pl.ds(source,width)
+            items.append(Reduce(p,out,mem[:3],mem[3:],mine=both.at[0,:,:,cols],give=both.at[1,:,:,cols]))
+    mem=rest[6*len(plan):]
+    small=Small(p,smb,small_ref,mem[:4],mem[4:])
+    ready=[it for it in items if it.paired is not None]
+    fresh=[it for it in items if it.paired is None]
+
+    def slot(t):
+        for k in range(Reduce.STAGES):
+            if 0<=t-k<len(items): items[t-k].stage(k)
+
+    @pl.when(step==0)
+    def _():
+        greet(Reduce.peers(p))
+        for it in ready: it.start()
+        for ref in (dstate,rcar,gb_ref,gg_ref,low_acc,high_acc,nmix_ref,smb): ref[...]=jnp.zeros_like(ref)
+
+    @pl.when(step<nc)
+    def _():
+        i=nc-1-step
+        rows=pl.ds(pl.multiple_of(i*C,C),C)
+        bwd_chunk(i,q_ref,k_ref,v_ref,g_ref,r_ref,o_ref,st_ref,dy_ref,wh_ref,bias_ref,gain_ref,cols_ref,segr_ref,m_ref,
+                  dall.at[rows,0:512],dall.at[rows,512:1024],dall.at[rows,1024:2048],dall.at[rows,2048:3072],dz_ref,gb_ref,gg_ref,dstate,rcar,esc,dcs)
+        dz=dz_ref[...]; a=a_ref[...]
+        dr=dot_nt(dz,wh_ref[...]).astype(BF)
+        high_acc[...]+=dot_tn(r_ref[...],dz)
+        low_acc[...]+=dot_tn(dr,a)
+        at_ref[:,rows]=jnp.transpose(a)
+        da=dot_nt(dall[rows,0:512],wq_ref[...])+dot_nt(dall[rows,512:1024],wk_ref[...])
+        da=da+dot_nt(dall[rows,1024:2048],wv_ref[...])+dot_nt(dall[rows,2048:3072],wg_ref[...])+dot_nt(dr,wl_ref[...])
+        x=x_ref[...].astype(F32)
+        n1=lax.rsqrt(jnp.mean(x*x,axis=-1,keepdims=True)+1e-5)
+        xn=x*n1
+        nmix_ref[...]+=jnp.sum(da*xn,axis=0,keepdims=True)
+        dm=da*gmix_ref[...]
+        gt_ref[...]=dx_ref[...]+n1*(dm-xn*jnp.mean(dm*xn,axis=-1,keepdims=True))
+
+    for t in range(8):
+        @pl.when(step==t)
+        def _(): slot(t)
+
+    @pl.when(step==nc)
+    def _():
+        rs=2*half
+        smb[:,16:32,:]=jnp.broadcast_to(high_acc[...][None],(n,16,512))
+        smb[:,32:33,:]=jnp.broadcast_to(gb_ref[...][None],(n,1,512))
+        smb[:,33:34,0:256]=jnp.broadcast_to(gg_ref[...][None],(n,1,256))
+        for s in range(n):
+            at=slice(s*rs,(s+1)*rs)
+            smb[s,0:16,0:rs]=low_acc[:,at]
+            smb[s,34:35,0:rs]=nmix_ref[:,at]
+            smb[s,35:36,0:rs]=nmlp_ref[:,at]
+        small.swap().start()
+
+        def product(at,width):
+            cols=slice(at,at+width)
+            def one(s,_):
+                rows=pl.ds(pl.multiple_of(s*rs,rs),rs)
+                w=dot(at_ref[rows,:],dall[:,cols]).astype(BF)
+                both[p.core,s,:,cols]=w[:half]
+                both[1-p.core,s,:,cols]=w[half:]
+                return 0
+            lax.fori_loop(0,n,one,0)
+
+        t=8; f=0
+        for at,width,count in ((2048,1024,2),(1024,1024,2),(0,1024,2)):
+            product(at,width)
+            for it in fresh[f:f+count]: it.start()
+            f+=count
+            slot(t); t+=1
+            small.stage((t-9))
+        last=len(items)+Reduce.STAGES-1
+        while t<last:
+            slot(t); t+=1
+        for it in items: it.settle()
+        small.settle()
+
+def backward(n,reps,q,k,v,g,r,o,st,dy,first,tokens,dx2,wh,bias,gain,gmix,nmlp,cols,segr,weights,pairs):
+    T=q.shape[0]; nc=T//C; z=reps//2
+    assert nc==8
+    M=jnp.asarray(level_sums(),BF); nr=M.shape[0]
+    blk=lambda w: pl.BlockSpec((C,w),lambda i:(jnp.maximum(nc-1-i,0),0))
+    full=lambda *sh: pl.BlockSpec(sh,lambda i:(0,)*len(sh),pipeline_mode=pl.Buffered(1))
+    sd=jax.ShapeDtypeStruct
+    anywhere=pl.BlockSpec(memory_space=pl.ANY)
+    half=first.shape[1]//(2*n)
+    plan,scratch=[],[]
+    for which,(pair,cut) in enumerate(zip(pairs,(4,4,4,2))):
+        tiles=pair.shape[2]//128
+        edges=[128*(tiles*j//cut) for j in range(cut+1)]
+        for at,end in zip(edges[:-1],edges[1:]):
+            plan.append((which,at,end-at,None)); scratch+=Reduce.scratch(n,z,pair.shape[1],end-at,True)
+    for which,at,width,source in ((7,0,512,2048),(7,512,512,2560),(6,0,512,1024),(6,512,512,1536),(4,0,512,0),(5,0,512,512)):
+        plan.append((which,at,width,source)); scratch+=Reduce.scratch(n,z,half,width,False)
+    scratch+=Small.scratch(n,z,40,512)
+    out=lambda h,w: sd((2,h,w),BF)
+    res=pl.pallas_call(functools.partial(backward_kernel,n,reps,tuple(plan),half),grid=(nc+1,),
+        in_specs=[blk(512),blk(512),blk(1024),blk(1024),blk(16),blk(1024),pl.BlockSpec((1,HEADS,VH,KH),lambda i:(jnp.maximum(nc-1-i,0),0,0,0)),blk(1024),
+                  blk(1024),blk(1024),blk(1024),blk(2),
+                  full(16,512),full(1,512),full(1,256),full(1,1024),full(1,1024),full(nc,1,C),full(nr,C),
+                  full(1024,512),full(1024,512),full(1024,1024),full(1024,1024),full(1024,16)]+[anywhere]*4,
+        out_specs=[blk(1024),pl.BlockSpec((40,512),lambda i:(0,0))]+[anywhere]*8,
+        out_shape=[sd((T,1024),F32),sd((40,512),F32)]+[out(q.shape[1],q.shape[2]) for q in pairs]+[out(half,512),out(half,512),out(half,1024),out(half,1024)],
+        scratch_shapes=[pltpu.VMEM((HEADS,VH,KH),F32),pltpu.VMEM((1,512),F32),pltpu.VMEM((nr,512),F32),pltpu.VMEM((C,1024),BF),
+                        pltpu.VMEM((T,3072),BF),pltpu.VMEM((1024,T),BF),pltpu.VMEM((C,512),BF),pltpu.VMEM((16,1024),F32),pltpu.VMEM((16,512),F32),
+                        pltpu.VMEM((1,512),F32),pltpu.VMEM((1,256),F32),pltpu.VMEM((1,1024),F32),pltpu.VMEM((n,40,512),F32),
+                        pltpu.VMEM((2,n,half,3072),BF)]+scratch,
+        compiler_params=pltpu.CompilerParams(collective_id=2,has_side_effects=True,vmem_limit_bytes=63<<20),
+        name="gla_bwd_reduce")(q,k,v,g,r,o,st,dy,first,tokens,dx2,cols,wh,bias,gain,gmix,nmlp,segr,M,*weights,*pairs)
+    return res[0],res[1],[x.reshape(-1,x.shape[2]) for x in res[2:]]
 
 
 def matmul(left, right):
@@ -755,45 +865,48 @@
     branch = grad_resid.astype(BF)
     part_out = dot_tn(mixed, branch)
     grad_mixed = dot_nt(branch, out_w).astype(BF)
-    grad_q, grad_k, grad_v, grad_g, grad_z, part_bias, part_head = backward(
-        query, keys, values, outgate, lowrank, heads, states, grad_mixed, high_w, bias, gain_head, cols, segr
+    pairs = pair_sums(
+        shards, reps, [q.astype(BF) for q in (part_down, part_gate, part_up, part_out)]
     )
-    part_high = dot_tn(lowrank, grad_z)
-    grad_low = dot_nt(grad_z, high_w).astype(BF)
-    part_low = dot_tn(first, grad_low)
-    part_query = dot_tn(first, grad_q)
-    part_key = dot_tn(first, grad_k)
-    part_value = dot_tn(first, grad_v)
-    part_outgate = dot_tn(first, grad_g)
-    grad_first = (
-        dot_nt(grad_q, query_w)
-        + dot_nt(grad_k, key_w)
-        + dot_nt(grad_v, value_w)
-        + dot_nt(grad_g, outgate_w)
-        + dot_nt(grad_low, low_w)
+    grad_inputs, small_sums, sums = backward(
+        shards,
+        reps,
+        query,
+        keys,
+        values,
+        outgate,
+        lowrank,
+        heads,
+        states,
+        grad_mixed,
+        first,
+        tokens.reshape(total, width),
+        grad_resid,
+        high_w,
+        bias,
+        gain_head,
+        gain_mix[None],
+        part_norm_mlp[None],
+        cols,
+        segr,
+        (query_w, key_w, value_w, outgate_w, low_w),
+        pairs,
     )
-    part_norm_mix = jnp.sum(grad_first * inputs * inv_mix, axis=0)
-    scaled_mix = grad_first * gain_mix
-    grad_inputs = (
-        grad_resid
-        + inv_mix * scaled_mix
-        - inputs * inv_mix**3 * jnp.mean(scaled_mix * inputs, axis=-1, keepdims=True)
+    sum_down, sum_gate, sum_up, sum_out, sum_query, sum_key, sum_value, sum_outgate = [s.astype(F32) for s in sums]
+    me = lax.axis_index("shard")
+    rs = w_low.shape[0]
+
+    def across(block, width):
+        return lax.dynamic_slice_in_dim(block, me * width, width, axis=1)
+
+    own = (
+        small_sums[34, :rs],
+        small_sums[35, :rs],
+        across(small_sums[32:33], decay_bias.shape[0]).reshape(-1),
+        across(small_sums[33:34, :VH], head_gain.shape[0]).reshape(-1),
+        small_sums[:16, :rs].T,
+        across(small_sums[16:32], w_high.shape[1]),
     )
-    parts = (
-        part_norm_mix,
-        part_norm_mlp,
-        part_bias,
-        part_head,
-        part_low,
-        part_high.reshape(w_high.shape[0], shards, -1).transpose(1, 0, 2),
-    )
-    pack = jnp.concatenate([p.reshape(shards, -1) for p in parts], axis=1)
-    pack = jnp.pad(pack, ((0, 0), (0, rows * 128 - sum(sizes)))).reshape(shards, rows, 128)
-    partials = (part_down, part_gate, part_up, part_out, part_query, part_key, part_value, part_outgate)
-    sums, mine = reduce_all(shards, reps, [p.astype(BF) for p in partials], (2, 2, 2, 1, 1, 1, 1, 1), pack)
-    sum_down, sum_gate, sum_up, sum_out, sum_query, sum_key, sum_value, sum_outgate = [s.astype(F32) for s in sums]
-    mine = mine.reshape(-1)
-    own = [mine[offsets[i] : offsets[i + 1]].reshape(small[i].shape) for i in range(len(small))]
     return (
         result.reshape(tokens.shape),
         grad_inputs.reshape(tokens.shape),

time: 619 us -> 462 us (0.75)
  Pallas kernels: 410 us -> 304 us
  matrix products: 149 us -> 117 us
  other arithmetic: 24.4 us -> 15.4 us
  local copies, waits for them, and re-layouts: 25.1 us -> 17 us
    pallas_call x1, Pallas kernels: 200 us -> 112 us  [gather_weights(): pl.pallas_call(functools.partial(gather_kernel, n, reps, count), out_shap...]
    dot_general x10 -> x4, matrix products: 46.2 us -> 27.1 us  [dot_tn(): lax.dot_general(a, b, (((0,), (0,)), ((), ())), preferred_element_type=F32)]
    pallas_call x2, Pallas kernels: 191 us -> 174 us  [the longest x1 157 us: backward(): pl.pallas_call(functools.partial(backward_kernel, n, reps, tuple(plan), h...]
    dot_general x10 -> x4, matrix products: 57.9 us -> 47.6 us  [dot_nt(): lax.dot_general(a, b, (((1,), (1,)), ((), ())), preferred_element_type=F32)]
    unnamed x146 -> x113, local copies, waits for them, and re-layouts: 18.9 us -> 9.24 us
    reshape x1 -> x0, other arithmetic: 6.45 us -> none  [local(): grad_inputs.reshape(tokens.shape)]
where the time goes in v2:
time: 462 us; the launch traced here: 455 us
  Pallas kernels  304 us (66%)
  matrix products  117 us (25%)
  local copies, waits for them, and re-layouts  17 us (4%)
  other arithmetic  15.4 us (3%)
    pallas_call x1, Pallas kernels, backward(): pl.pallas_call(functools.partial(backward_kernel, n, reps, tuple(plan), h...  157 us
    pallas_call x1, Pallas kernels, gather_weights(): pl.pallas_call(functools.partial(gather_kernel, n, reps, count), out_shap...  112 us
    dot_general x4, matrix products, dot_nt(): lax.dot_general(a, b, (((1,), (1,)), ((), ())), preferred_element_type=F32)  47.6 us
    dot_general x9, matrix products, matmul(): return jnp.dot(left, right, preferred_element_type=F32)  42.5 us
    dot_general x4, matrix products, dot_tn(): lax.dot_general(a, b, (((0,), (0,)), ((), ())), preferred_element_type=F32)  27.1 us
    pallas_call x1, Pallas kernels, forward(): pl.pallas_call(fwd_body, grid=(nc,), in_specs=[blk(512), blk(512), blk(10...  18.5 us
    pallas_call x1, Pallas kernels, pair_sums(): pl.pallas_call(functools.partial(pair_kernel, n, reps, len(views)), out_s...  16.8 us
    convert_element_type x5, other arithmetic, local(): s.astype(F32)  10.8 us

profile of v2, /device:TPU:1, one launch (start us, length us, event | category | flops | bytes accessed | tf_op | source)
XLA Modules:
  0.0 455.4 jit_solution(2589626321489874395)
XLA Ops:
  0.6 0.0 copy-start.15
  0.7 1.0 copy.46
  1.6 0.1 reshape.309
  1.7 3.4 concatenate.6
  5.2 0.6 pad_bitcast_fusion.refs_0_
  5.8 112.3 %gather_mixer.1 = (bf16[4,64,128]{2,1,0:T(8,128)(2,1)}, bf16[4,2,128,512]{3,2,1,0:T(8,128)(2,1)}, bf16[4,2,128,512]{3,2,1,0:T(8,128)(2,1)}, bf16[4,2,128,1024]{3...) custom-call(bf16[64,128]{1,0:T(8,128)(2,1)} %pad_bitcast_fusion.refs, ...), custom_call_target="tpu_custom_call" | custom-call | tf_op jit(solution)/shard_map/gather_mixer/pallas_call | solution.py:307
  118.1 0.9 copy.63
  119.0 0.6 convert_bitcast_fusion
  119.6 0.1 slice.57
  119.6 0.2 reshape.325.refs_23_
  119.9 0.5 fusion.4
  120.4 0.8 convolution_convert_fusion.9.r_ref.refs_4_
  121.2 0.0 copy-start.8
  121.2 0.4 copy-done.25
  121.6 3.8 convolution_convert_fusion.5.g_ref.refs_3_
  125.4 3.7 convolution_convert_fusion.6.v_ref.refs_2_
  129.1 1.3 convolution_convert_fusion.7.k_ref.refs_1_
  130.4 0.0 copy-start.4
  130.4 0.0 copy-start.10
  130.5 0.0 copy-start.7
  130.5 1.3 convolution_convert_fusion.8.q_ref.refs_0_
  131.8 0.0 copy-start.5
  131.8 0.1 slice.58
  131.9 0.1 reshape.343.gain_ref.refs_14_
  132.0 0.1 pad_add_fusion.1
  132.1 0.2 copy.49.cols_ref.refs_11_
  132.4 18.5 %gla_fwd.1 = (bf16[1024,1024]{1,0:T(8,128)(2,1)S(1)}, bf16[1024,1024]{1,0:T(8,128)(2,1)}, bf16[8,4,256,128]{3,2,1,0:T(8,128)(2,1)}) custom-call(bf16[1024,512]{1,0:T(8,128)(2,1)S(1)} %convolution_convert_fusion.8.q_ref.refs_0_, bf16[1024,512]{1,0:T(8,128)(2,1)S(1)} %convolution_convert_fusion.7.k_ref.refs_1_, ...), custom_call_target="tpu_custom_call" | custom-call | flops 20000000000 | bytes 16000000 | tf_op jit(solution)/shard_map/gla_fwd/pallas_call | solution.py:150
  150.9 0.0 copy-start.13
  150.9 2.5 multiply_reduce_fusion.2
  153.4 2.0 copy-done.19
  155.4 0.4 multiply_convert_fusion.1
  155.9 8.8 %fusion.23 = f32[1024,2816]{1,0:T(8,128)} fusion(bf16[1024,1024]{1,0:T(8,128)(2,1)S(1)} %multiply_convert_fusion.1, bf16[1024,2816]{1,0:T(8,128)(2,1)S(1)} %bitcast.196), kind=kOutput, calls=%fused_computation.69 | convolution fusion | flops 5905580032 | bytes 19398656 | tf_op jit(solution)/shard_map/dot_general | solution.py:781
  164.7 8.8 %fusion.22 = f32[1024,2816]{1,0:T(8,128)} fusion(bf16[1024,1024]{1,0:T(8,128)(2,1)S(1)} %multiply_convert_fusion.1, bf16[1024,2816]{1,0:T(8,128)(2,1)S(1)} %bitcast.200), kind=kOutput, calls=%fused_computation.68 | convolution fusion | flops 5905580032 | bytes 19398656 | tf_op jit(solution)/shard_map/dot_general | solution.py:781
  173.5 21.6 %fusion.2 = (bf16[1024,2816]{1,0:T(8,128)(2,1)}, bf16[1024,2816]{1,0:T(8,128)(2,1)}, bf16[1024,2816]{1,0:T(8,128)(2,1)}) fusion(f32[1024,2816]{1,0:T(8,128)} %fusion.22, f32[1024,2816]{1,0:T(8,128)} %fusion.23, bf16[2816,1024]{1,0:T(8,128)(2,1)} %bitcast.191, bf16[1,1024,1024]{2,1,0:T(8,128)(2,1)} %param.21), kind=kOutput, calls=%fused_computation.4 | convolution fusion | flops 5948833792 | bytes 48234496 | tf_op jit(solution)/shard_map/dot_general | solution.py:24
  195.1 11.4 %fusion.24 = f32[1024,1024]{1,0:T(8,128)} fusion(bf16[1024,2816]{1,0:T(8,128)(2,1)} %get-tuple-element.71, bf16[1024,2816]{1,0:T(8,128)(2,1)} %bitcast.197), kind=kOutput, calls=%fused_computation.70 | convolution fusion | flops 5905580032 | bytes 15728640 | tf_op jit(solution)/shard_map/dot_general | solution.py:24
  206.6 10.2 %multiply_reduce_fusion = (f32[1024]{0:T(1024)}, f32[1024]{0:T(1024)S(1)}, f32[1024,1024]{1,0:T(8,128)S(1)}) fusion(f32[1024,1024]{1,0:T(8,128)S(1)} %copy-done.20, f32[1024]{0:T(1024)S(1)} %get-tuple-element.80, f32[1024]{0:T(1024)S(1)} %bitcast.177, f32[1024,1024]{1,0:T(8,128)} %fusion.24, bf16[1024,2816]{1,0:T(8,128)(2,1)S(1)} %copy-done.43, ...), kind=kOutput, calls=%fused_computation.17 | convolution fusion | flops 5912918016 | bytes 24133632 | tf_op jit(solution)/shard_map/dot_general | solution.py:24
  216.8 1.2 multiply_subtract_fusion.refs_10_
  218.0 0.3 copy-done.14
  218.4 2.4 convolution_convert_fusion.3
  220.8 1.8 copy-done.44
  222.5 8.4 %convolution_convert_fusion = bf16[1024,2816]{1,0:T(8,128)(2,1)} fusion(bf16[1024,1024]{1,0:T(8,128)(2,1)S(1)} %multiply_convert_fusion.1, bf16[1024,2816]{1,0:T(8,128)(2,1)S(1)} %copy-done.44), kind=kOutput, calls=%fused_computation.11 | convolution fusion | flops 5908463616 | bytes 13631488 | tf_op jit(solution)/shard_map/dot_general | solution.py:25
  231.0 8.3 %convolution_convert_fusion.1 = bf16[1024,2816]{1,0:T(8,128)(2,1)} fusion(bf16[1024,1024]{1,0:T(8,128)(2,1)S(1)} %multiply_convert_fusion.1, bf16[1024,2816]{1,0:T(8,128)(2,1)S(1)} %bitcast.204), kind=kOutput, calls=%fused_computation.12 | convolution fusion | flops 5908463616 | bytes 13631488 | tf_op jit(solution)/shard_map/dot_general | solution.py:25
  239.2 8.1 %convolution_convert_fusion.2 = bf16[2816,1024]{1,0:T(8,128)(2,1)} fusion(bf16[1024,2816]{1,0:T(8,128)(2,1)S(1)} %bitcast.206, bf16[1,1024,1024]{2,1,0:T(8,128)(2,1)S(1)} %copy-done.23), kind=kOutput, calls=%fused_computation.13 | convolution fusion | flops 5908463616 | bytes 13631488 | tf_op jit(solution)/shard_map/dot_general | solution.py:25
  247.3 16.8 %pair_sums.1 = (bf16[4,352,1024]{2,1,0:T(8,128)(2,1)S(1)}, bf16[4,128,2816]{2,1,0:T(8,128)(2,1)S(1)}, bf16[4,128,2816]{2,1,0:T(8,128)(2,1)S(1)}, bf16[4,128,1024]{2,1,0:T(8,128)(2,1)S(1)}) custom-call(bf16[4,2,352,1024]{3,2,1,0:T(8,128)(2,1)} %bitcast.151, bf16[4,2,128,2816]{3,2,1,0:T(8,128)(2,1)} %bitcast.150, bf16[4,2,128,2816]{3,2,1,0:T(8,128)(2,1)} %bitcast.149, ...), custom_call_target="tpu_custom_call" | custom-call | tf_op jit(solution)/shard_map/pair_sums/pallas_call | solution.py:639
  264.1 0.0 copy-start
  264.1 0.0 copy-start.1
  264.2 0.0 copy-start.18
  264.2 4.4 convolution_convert_fusion.4.refs_7_
  268.6 0.1 copy-done.6
  268.6 1.8 fusion.6.refs_8_
  270.5 0.6 copy.60
  271.1 156.8 %gla_bwd_reduce.1 = (f32[1024,1024]{1,0:T(8,128)}, f32[40,512]{1,0:T(8,128)}, bf16[2,352,1024]{2,1,0:T(8,128)(2,1)}, bf16[2,128,2816]{2,1,0:T(8,128)(2,1)}, bf16...) custom-call(bf16[1024,512]{1,0:T(8,128)(2,1)} %copy-done.5, ...), custom_call_target="tpu_custom_call" | custom-call | tf_op jit(solution)/shard_map/gla_bwd_reduce/pallas_call | solution.py:764
  428.0 4.8 %bitcast_convert_fusion.1 = (f32[256,2816]{1,0:T(8,128)}, f32[256,2816]{1,0:T(8,128)}) fusion(bf16[2,128,2816]{2,1,0:T(8,128)(2,1)} %get-tuple-element.66, bf16[2,128,2816]{2,1,0:T(8,128)(2,1)} %get-tuple-element.65), kind=kLoop, calls=%fused_computation.37 | loop fusion | flops 1441792 | bytes 8650752 | tf_op jit(solution)/shard_map/convert_element_type | solution.py:895
  432.8 1.6 bitcast_convert_fusion.3
  434.5 1.1 bitcast_convert_fusion.6
  435.6 2.0 bitcast_convert_fusion
  437.6 1.1 bitcast_convert_fusion.5
  438.8 0.6 constant_dynamic-slice_fusion.2
  439.4 0.6 slice_bitcast_fusion
  440.0 0.6 fusion.21
  440.5 0.6 fusion.15
  441.1 0.5 fusion.14
  441.6 11.5 %fusion.8 = bf16[1,1024,1024]{2,1,0:T(8,128)(2,1)} fusion(f32[1024,1024]{1,0:T(8,128)} %copy-done.19, bf16[1024,2816]{1,0:T(8,128)(2,1)} %get-tuple-element.72, bf16[2816,1024]{1,0:T(8,128)(2,1)} %bitcast.192), kind=kOutput, calls=%fused_computation.25 | convolution fusion | flops 5907677184 | bytes 17825792 | tf_op jit(solution)/shard_map/dot_general | solution.py:781
  453.2 2.0 copy.66
  (106 shorter events, 0.2 us)
Async XLA Ops:
  0.6 119.2 %copy-start.15 = (bf16[1,1024,1024]{2,1,0:T(8,128)(2,1)S(1)}, bf16[1,1024,1024]{2,1,0:T(8,128)(2,1)}, u32[]{:S(2)}) copy-start(bf16[1,1024,1024]{2,1,0:T(8,128)(2,1)} %param.19) | copy-start | bytes 6291460
  119.6 10.9 %copy-start.37 = (f32[1,2,4,128]{3,1,2,0:T(2,128)}, f32[1,2,4,128]{3,1,2,0:T(2,128)S(1)}, u32[]{:S(2)}) copy-start(f32[1,2,4,128]{3,1,2,0:T(2,128)S(1)} %copy.57) | copy-start | bytes 12292
  119.9 5.5 %copy-start.27 = (bf16[1024,16]{1,0:T(8,128)(2,1)}, bf16[1024,16]{1,0:T(8,128)(2,1)S(1)}, u32[]{:S(2)}) copy-start(bf16[1024,16]{1,0:T(8,128)(2,1)S(1)} %reshape.325.refs_23_) | copy-start | bytes 98308
  119.9 1.7 copy-start.25
  120.4 10.0 %copy-start.39 = (f32[1024]{0:T(1024)}, f32[1024]{0:T(1024)S(1)}, u32[]{:S(2)}) copy-start(f32[1024]{0:T(1024)S(1)} %add_rsqrt_fusion.1) | copy-start | bytes 12292
  121.2 11.2 %copy-start.8 = (bf16[1024,16]{1,0:T(8,128)(2,1)}, bf16[1024,16]{1,0:T(8,128)(2,1)S(1)}, u32[]{:S(2)}) copy-start(bf16[1024,16]{1,0:T(8,128)(2,1)S(1)} %convolution_convert_fusion.9.r_ref.refs_4_) | copy-start | bytes 98308
  121.6 3.8 copy-start.24
  125.4 3.7 copy-start.16
  125.4 3.7 copy-start.29
  129.1 1.3 copy-start.28
  130.4 2.0 copy-start.4
  130.4 1.6 copy-start.10
  130.5 1.9 copy-start.7
  131.8 19.1 %copy-start.5 = (bf16[1024,512]{1,0:T(8,128)(2,1)}, bf16[1024,512]{1,0:T(8,128)(2,1)S(1)}, u32[]{:S(2)}) copy-start(bf16[1024,512]{1,0:T(8,128)(2,1)S(1)} %convolution_convert_fusion.8.q_ref.refs_0_) | copy-start | bytes 3145732
  131.9 19.0 %copy-start.9 = (bf16[2,8,4,128]{3,1,2,0:T(8,128)(2,1)}, bf16[2,8,4,128]{3,1,2,0:T(8,128)(2,1)S(1)}, u32[]{:S(2)}) copy-start(bf16[2,8,4,128]{3,1,2,0:T(8,128)(2,1)S(1)} %copy.64) | copy-start | bytes 49156
  132.0 18.9 %copy-start.12 = (f32[1,256]{1,0:T(1,128)}, f32[1,256]{1,0:T(1,128)S(1)}, u32[]{:S(2)}) copy-start(f32[1,256]{1,0:T(1,128)S(1)} %reshape.343.gain_ref.refs_14_) | copy-start | bytes 3076
  132.0 18.9 %copy-start.11 = (f32[4,128]{1,0:T(4,128)}, f32[4,128]{1,0:T(4,128)S(1)}, u32[]{:S(2)}) copy-start(f32[4,128]{1,0:T(4,128)S(1)} %slice_convert_fusion.1) | copy-start | bytes 6148
  132.3 18.5 %copy-start.3 = (s32[1024,2]{1,0:T(8,128)}, s32[1024,2]{1,0:T(8,128)S(1)}, u32[]{:S(2)}) copy-start(s32[1024,2]{1,0:T(8,128)S(1)} %copy.49.cols_ref.refs_11_) | copy-start | bytes 24580
  132.4 18.5 %copy-start.17 = (bf16[1,1024,1024]{2,1,0:T(8,128)(2,1)S(1)}, bf16[1,1024,1024]{2,1,0:T(8,128)(2,1)}, u32[]{:S(2)}) copy-start(bf16[1,1024,1024]{2,1,0:T(8,128)(2,1)} %param.19) | copy-start | bytes 6291460
  132.4 18.5 %copy-start.41 = (bf16[4,2,128,1024]{3,2,1,0:T(8,128)(2,1)S(1)}, bf16[4,2,128,1024]{3,2,1,0:T(8,128)(2,1)}, u32[]{:S(2)}) copy-start(bf16[4,2,128,1024]{3,2,1,0:T(8,128)(2,1)} %get-tuple-element.48) | copy-start | bytes 6291460
  150.9 2.5 copy-start.13
  150.9 5.0 %slice-start = ((s8[5767168]{0:T(1024)(128)(4,1)}), s8[4194304]{0:T(1024)(128)(4,1)S(1)}, s32[]{:S(2)}) async-start(s8[5767168]{0:T(1024)(128)(4,1)} %bitcast.194), calls=%async_computation | async-start | bytes 8388608
  150.9 4.9 %slice-start.1 = ((s8[5767168]{0:T(1024)(128)(4,1)}), s8[1572864]{0:T(1024)(128)(4,1)S(1)}, s32[]{:S(2)}) async-start(s8[5767168]{0:T(1024)(128)(4,1)} %bitcast.194), calls=%async_computation.1 | async-start | bytes 3145728
  153.4 2.0 copy-start.19
  155.4 9.3 %slice-start.2 = ((s8[5767168]{0:T(1024)(128)(4,1)}), s8[4194304]{0:T(1024)(128)(4,1)S(1)}, s32[]{:S(2)}) async-start(s8[5767168]{0:T(1024)(128)(4,1)} %bitcast.198), calls=%async_computation.2 | async-start | bytes 8388608
  155.9 8.8 %slice-start.3 = ((s8[5767168]{0:T(1024)(128)(4,1)}), s8[1572864]{0:T(1024)(128)(4,1)S(1)}, s32[]{:S(2)}) async-start(s8[5767168]{0:T(1024)(128)(4,1)} %bitcast.198), calls=%async_computation.3 | async-start | bytes 3145728
  195.1 11.4 %copy-start.20 = (f32[1024,1024]{1,0:T(8,128)S(1)}, f32[1024,1024]{1,0:T(8,128)}, u32[]{:S(2)}) copy-start(f32[1024,1024]{1,0:T(8,128)} %copy-done.19) | copy-start | bytes 12582916
  195.1 11.4 %copy-start.43 = (bf16[1024,2816]{1,0:T(8,128)(2,1)S(1)}, bf16[1024,2816]{1,0:T(8,128)(2,1)}, u32[]{:S(2)}) copy-start(bf16[1024,2816]{1,0:T(8,128)(2,1)} %get-tuple-element.70) | copy-start | bytes 17301508
  206.5 10.3 %copy-start.23 = (bf16[1,1024,1024]{2,1,0:T(8,128)(2,1)S(1)}, bf16[1,1024,1024]{2,1,0:T(8,128)(2,1)}, u32[]{:S(2)}) copy-start(bf16[1,1024,1024]{2,1,0:T(8,128)(2,1)} %param.21) | copy-start | bytes 6291460
  216.8 1.6 copy-start.14
  218.4 45.8 %copy-start.21 = (f32[1024,1024]{1,0:T(8,128)}, f32[1024,1024]{1,0:T(8,128)S(1)}, u32[]{:S(2)}) copy-start(f32[1024,1024]{1,0:T(8,128)S(1)} %multiply_subtract_fusion.refs_10_) | copy-start | bytes 12582916
  218.4 4.1 copy-start.44
  218.4 12.6 %slice-start.4 = ((s8[5767168]{0:T(1024)(128)(4,1)}), s8[4194304]{0:T(1024)(128)(4,1)S(1)}, s32[]{:S(2)}) async-start(s8[5767168]{0:T(1024)(128)(4,1)} %bitcast.203), calls=%async_computation.4 | async-start | bytes 8388608
  222.5 8.4 %slice-start.5 = ((s8[5767168]{0:T(1024)(128)(4,1)}), s8[1572864]{0:T(1024)(128)(4,1)S(1)}, s32[]{:S(2)}) async-start(s8[5767168]{0:T(1024)(128)(4,1)} %bitcast.203), calls=%async_computation.5 | async-start | bytes 3145728
  222.5 16.7 %slice-start.6 = ((s8[5767168]{0:T(1024)(128)(4,1)}), s8[1572864]{0:T(1024)(128)(4,1)S(1)}, s32[]{:S(2)}) async-start(s8[5767168]{0:T(1024)(128)(4,1)} %bitcast.205), calls=%async_computation.6 | async-start | bytes 3145728
  231.0 8.3 %slice-start.7 = ((s8[5767168]{0:T(1024)(128)(4,1)}), s8[4194304]{0:T(1024)(128)(4,1)S(1)}, s32[]{:S(2)}) async-start(s8[5767168]{0:T(1024)(128)(4,1)} %bitcast.205), calls=%async_computation.7 | async-start | bytes 8388608
  247.3 16.8 %copy-start.42 = (bf16[4,2,128,1024]{3,2,1,0:T(8,128)(2,1)S(1)}, bf16[4,2,128,1024]{3,2,1,0:T(8,128)(2,1)}, u32[]{:S(2)}) copy-start(bf16[4,2,128,1024]{3,2,1,0:T(8,128)(2,1)} %get-tuple-element.48) | copy-start | bytes 6291460
  264.1 4.5 copy-start
  264.1 4.4 copy-start.1
  264.1 4.4 copy-start.2
  264.1 4.5 copy-start.6
  264.2 4.5 copy-start.18
  264.2 4.4 copy-start.38
  264.2 4.4 copy-start.40
  268.6 1.9 copy-start.36
  427.9 4.9 %copy-start.31 = (bf16[2,128,1024]{2,1,0:T(8,128)(2,1)S(1)}, bf16[2,128,1024]{2,1,0:T(8,128)(2,1)}, u32[]{:S(2)}) copy-start(bf16[2,128,1024]{2,1,0:T(8,128)(2,1)} %get-tuple-element.64) | copy-start | bytes 1572868
  427.9 4.9 %copy-start.32 = (bf16[2,128,1024]{2,1,0:T(8,128)(2,1)S(1)}, bf16[2,128,1024]{2,1,0:T(8,128)(2,1)}, u32[]{:S(2)}) copy-start(bf16[2,128,1024]{2,1,0:T(8,128)(2,1)} %get-tuple-element.63) | copy-start | bytes 1572868
  427.9 6.5 %copy-start.33 = (bf16[2,128,512]{2,1,0:T(8,128)(2,1)S(1)}, bf16[2,128,512]{2,1,0:T(8,128)(2,1)}, u32[]{:S(2)}) copy-start(bf16[2,128,512]{2,1,0:T(8,128)(2,1)} %get-tuple-element.60) | copy-start | bytes 786436
  427.9 6.5 %copy-start.34 = (bf16[2,128,512]{2,1,0:T(8,128)(2,1)S(1)}, bf16[2,128,512]{2,1,0:T(8,128)(2,1)}, u32[]{:S(2)}) copy-start(bf16[2,128,512]{2,1,0:T(8,128)(2,1)} %get-tuple-element.61) | copy-start | bytes 786436
  432.8 2.8 copy-start.26
  432.8 4.8 %copy-start.30 = (bf16[2,128,1024]{2,1,0:T(8,128)(2,1)S(1)}, bf16[2,128,1024]{2,1,0:T(8,128)(2,1)}, u32[]{:S(2)}) copy-start(bf16[2,128,1024]{2,1,0:T(8,128)(2,1)} %get-tuple-element.62) | copy-start | bytes 1572868
  434.4 4.3 copy-start.35
  441.6 11.6 %copy-start.22 = (f32[1024,1024]{1,0:T(8,128)S(1)}, f32[1024,1024]{1,0:T(8,128)}, u32[]{:S(2)}) copy-start(f32[1024,1024]{1,0:T(8,128)} %get-tuple-element.58) | copy-start | bytes 12582916

commit v3 on v2

--- a/solution.py
+++ b/solution.py
@@ -35,10 +35,7 @@
     x=t^s
     return jnp.where(segc==segr,x,-1),t,s
 
-def fwd_body(q_ref,k_ref,v_ref,g_ref,r_ref,wh_ref,bias_ref,gain_ref,cols_ref,segr_ref,m_ref,y_ref,o_ref,st_ref,state,esc):
-    i=pl.program_id(0)
-    @pl.when(i==0)
-    def _(): state[...]=jnp.zeros_like(state)
+def fwd_chunk(i,q_ref,k_ref,v_ref,g_ref,r_ref,wh_ref,bias_ref,gain_ref,cols_ref,segr_ref,m_ref,y_ref,o_ref,st_ref,state,esc):
     f=log_rate(gate_in(r_ref,wh_ref,bias_ref)).astype(BF)
     esc[...]=jnp.exp(dot(m_ref[...],f))
     segc=cols_ref[:,0:1]; segr=segr_ref[i]
@@ -142,20 +139,6 @@
     cols=jnp.stack([seg,prev],axis=1)
     return cols,seg.reshape(-1,1,C)
 
-def forward(q,k,v,g,r,wh,bias,gain,cols,segr):
-    T=q.shape[0]; nc=T//C
-    M=jnp.asarray(level_sums(),BF); nr=M.shape[0]
-    blk=lambda w: pl.BlockSpec((C,w),lambda i:(i,0))
-    full=lambda *sh: pl.BlockSpec(sh,lambda i:(0,)*len(sh))
-    return pl.pallas_call(fwd_body,grid=(nc,),
-        in_specs=[blk(512),blk(512),blk(1024),blk(1024),blk(16),full(16,512),full(1,512),full(1,256),blk(2),full(nc,1,C),full(nr,C)],
-        out_specs=[blk(1024),blk(1024),pl.BlockSpec((1,HEADS,VH,KH),lambda i:(i,0,0,0))],
-        out_shape=[jax.ShapeDtypeStruct((T,1024),BF),jax.ShapeDtypeStruct((T,1024),BF),jax.ShapeDtypeStruct((nc,HEADS,VH,KH),BF)],
-        scratch_shapes=[pltpu.VMEM((HEADS,VH,KH),F32),pltpu.VMEM((nr,512),F32)],
-        compiler_params=pltpu.CompilerParams(vmem_limit_bytes=48<<20),
-        cost_estimate=pl.CostEstimate(flops=20_000_000_000,bytes_accessed=16_000_000,transcendentals=0),
-        name="gla_fwd")(q,k,v,g,r,wh,bias,gain,cols,segr,M)
-
 
 MESH = pl.DeviceIdType.MESH
 
@@ -232,94 +215,53 @@
         view = self.fulls[i].at[block, p.core]
         return remote(view, view, self.ssem.at[i, kind], self.rsem.at[i, kind], device)
 
-    def start(self):
-        p = self.p
-        for i in range(len(self.owns)):
-            if p.n == 4:
-                self.direct(i, 0, p.first()).start()
-                self.direct(i, 1, p.second()).start()
-            else:
-                for j in range(1, p.n):
-                    self.direct(i, j - 1, p.peer(j)).start()
-            self.same(i).start()
-
-    def finish(self):
-        p = self.p
-        count = len(self.owns)
-        last = p.n - 1
+    def start(self, i):
+        p = self.p
         if p.n == 4:
-            blocks = [p.first(), p.second(), 3 - p.me]
-            for i in range(count):
-                self.direct(i, 1, blocks[1]).wait_recv()
-                self.onward(i, 2, blocks[1], (p.rep, blocks[0])).start()
-                self.onward(i, last + 1, blocks[1], p.sib).start()
-                self.direct(i, 0, blocks[0]).wait_recv()
-                self.onward(i, last, blocks[0], p.sib).start()
-            for i in range(count):
-                self.onward(i, 2, blocks[2], (p.rep, blocks[0])).wait_recv()
-                self.onward(i, last + 2, blocks[2], p.sib).start()
+            self.direct(i, 0, p.first()).start()
+            self.direct(i, 1, p.second()).start()
         else:
-            blocks = [p.peer(p.n - j) for j in range(1, p.n)]
-            for i in range(count):
-                for j in range(last):
-                    self.direct(i, j, p.me).wait_recv()
-                    self.onward(i, last + j, blocks[j], p.sib).start()
-        for i in range(count):
-            self.same(i).wait()
+            for j in range(1, p.n):
+                self.direct(i, j - 1, p.peer(j)).start()
+        self.same(i).start()
+
+    def blocks(self):
+        p = self.p
+        if p.n == 4:
+            return [p.first(), p.second(), 3 - p.me]
+        return [p.peer(p.n - j) for j in range(1, p.n)]
+
+    def relay(self, i):
+        p, blocks, last = self.p, self.blocks(), self.p.n - 1
+        if p.n == 4:
+            self.direct(i, 1, blocks[1]).wait_recv()
+            self.onward(i, 2, blocks[1], (p.rep, blocks[0])).start()
+            self.onward(i, last + 1, blocks[1], p.sib).start()
+            self.direct(i, 0, blocks[0]).wait_recv()
+            self.onward(i, last, blocks[0], p.sib).start()
+        else:
             for j in range(last):
-                self.direct(i, j, p.me).wait_send()
-                arrival = self.onward(i, last + j, blocks[j], p.sib)
-                arrival.wait_send()
-                arrival.wait_recv()
+                self.direct(i, j, p.me).wait_recv()
+                self.onward(i, last + j, blocks[j], p.sib).start()
+
+    def pass_on(self, i):
+        p, blocks, last = self.p, self.blocks(), self.p.n - 1
+        if p.n == 4:
+            self.onward(i, 2, blocks[2], (p.rep, blocks[0])).wait_recv()
+            self.onward(i, last + 2, blocks[2], p.sib).start()
+
+    def done(self, i):
+        p, blocks, last = self.p, self.blocks(), self.p.n - 1
+        self.same(i).wait()
+        for j in range(last):
+            self.direct(i, j, p.me).wait_send()
+            arrival = self.onward(i, last + j, blocks[j], p.sib)
+            arrival.wait_send()
+            arrival.wait_recv()
 
 
 def halves(w):
     return w.reshape(2, w.shape[0] // 2, w.shape[1])
-
-
-def gather_kernel(n, reps, count, *refs):
-    pack = refs[0]
-    owns = refs[1 : 1 + count]
-    packs = refs[1 + count]
-    fulls = refs[2 + count : 2 + 2 * count]
-    psend, precv, plocal, *sems = refs[2 + 2 * count :]
-    p = Place(n, reps)
-    gather = Gather(p, owns, fulls, sems)
-    greet(gather.peers())
-
-    def small(j):
-        return remote(pack, packs.at[p.me], psend.at[j - 1], precv.at[j - 1], (p.rep, p.peer(j)))
-
-    for j in range(1, n):
-        small(j).start()
-    gather.start()
-    here = pltpu.make_async_copy(pack, packs.at[p.me], plocal)
-    here.start()
-    gather.finish()
-    here.wait()
-    for j in range(1, n):
-        small(j).wait()
-
-
-def gather_weights(n, reps, pack, weights):
-    count = len(weights)
-    owns = [halves(w) for w in weights]
-    outs = pl.pallas_call(
-        functools.partial(gather_kernel, n, reps, count),
-        out_shape=[jax.ShapeDtypeStruct((n,) + pack.shape, pack.dtype)]
-        + [jax.ShapeDtypeStruct((n,) + o.shape, o.dtype) for o in owns],
-        in_specs=[pl.BlockSpec(memory_space=pl.ANY)] * (1 + count),
-        out_specs=[pl.BlockSpec(memory_space=pl.ANY)] * (1 + count),
-        scratch_shapes=[
-            pltpu.SemaphoreType.DMA((n - 1,)),
-            pltpu.SemaphoreType.DMA((n - 1,)),
-            pltpu.SemaphoreType.DMA,
-        ]
-        + gather_sems(n, count),
-        compiler_params=pltpu.CompilerParams(collective_id=0, has_side_effects=True),
-        name="gather_mixer",
-    )(pack, *owns)
-    return outs[0], [o.reshape(-1, w.shape[1]) for o, w in zip(outs[1:], weights)]
 
 
 def add_rows(dst, a, b):
@@ -328,7 +270,7 @@
 
     def step(j, _):
         at = pl.ds(pl.multiple_of(j * slab, slab), slab)
-        dst[at, :] = (a[at, :].astype(F32) + b[at, :].astype(F32)).astype(dst.dtype)
+        dst[at, :] = a[at, :] + b[at, :]
         return 0
 
     lax.fori_loop(0, rows // slab, step, 0)
@@ -337,19 +279,18 @@
 class Reduce:
     STAGES = 7
 
-    def __init__(self, place, out, bufs, sems, mine=None, give=None, paired=None):
+    def __init__(self, place, out, bufs, sems, mine=None, give=None, part=None):
         self.p, self.out = place, out
-        self.mine, self.give, self.paired = mine, give, paired
+        self.part = part
         self.square = place.n == 4
         self.line = place.z == 4
         bufs = list(bufs)
-        if paired is None:
-            self.other = bufs.pop(0)
-            self.own, self.rest = mine.at[place.me], mine.at[place.second()]
-        else:
-            self.kept = bufs.pop(0)
-            self.own, self.rest = self.kept.at[0], self.kept.at[1 if self.square else 0]
-        self.group, self.ring = bufs
+        if part is not None:
+            mine, give = bufs.pop(0), part.at[:, 1 - place.core]
+        self.mine, self.give = mine, give
+        self.other, self.group, self.ring = bufs
+        self.own = mine.at[place.me]
+        self.rest = mine.at[place.second()] if self.square else None
         self.ssem, self.rsem, self.lsem = sems
         self.zbase = place.n
         self.end = self.zbase + (3 if self.line else place.z - 1)
@@ -358,36 +299,27 @@
     def copy(self, kind, src, dst, device):
         return remote(src, dst, self.ssem.at[kind], self.rsem.at[kind], device)
 
-    def loads(self):
-        p = self.p
-        which = [p.me, p.second()] if self.square else [p.me]
-        return [
-            pltpu.make_async_copy(self.paired.at[b], self.kept.at[j], self.lsem.at[j]) for j, b in enumerate(which)
-        ]
+    def load(self):
+        return pltpu.make_async_copy(self.part.at[:, self.p.core], self.mine, self.lsem.at[0])
 
     def swap(self):
         return self.copy(0, self.give, self.other, self.p.sib)
 
     def start(self):
-        if self.paired is None:
-            self.swap().start()
-        else:
-            for c in self.loads() + self.group_sends():
-                c.start()
-
-    def source(self, b):
-        return self.mine.at[b] if self.paired is None else self.paired.at[b]
+        self.swap().start()
+        if self.part is not None:
+            self.load().start()
 
     def group_sends(self):
         p = self.p
         if self.square:
             to = (p.rep, p.first())
             return [
-                self.copy(1, self.source(p.first()), self.group.at[0], to),
-                self.copy(2, self.source(3 - p.me), self.group.at[1], to),
+                self.copy(1, self.mine.at[p.first()], self.group.at[0], to),
+                self.copy(2, self.mine.at[3 - p.me], self.group.at[1], to),
             ]
         return [
-            self.copy(j, self.source(p.peer(j)), self.group.at[j - 1], (p.rep, p.peer(j))) for j in range(1, p.n)
+            self.copy(j, self.mine.at[p.peer(j)], self.group.at[j - 1], (p.rep, p.peer(j))) for j in range(1, p.n)
         ]
 
     def second_send(self):
@@ -412,26 +344,30 @@
             for j in range(1, p.z)
         ]
 
-    def last_swap(self):
-        return self.copy(self.end, self.total, self.out(self.p.core), self.p.sib)
-
-    def store(self):
-        return pltpu.make_async_copy(self.total, self.out(self.p.core), self.lsem.at[2])
+    def last_swaps(self):
+        return [
+            self.copy(self.end + j, self.total.at[:, lanes], half(self.p.core), self.p.sib)
+            for j, (half, lanes) in enumerate(self.out)
+        ]
+
+    def stores(self):
+        return [
+            pltpu.make_async_copy(self.total.at[:, lanes], half(self.p.core), self.lsem.at[2 + j])
+            for j, (half, lanes) in enumerate(self.out)
+        ]
 
     def stage(self, k):
         p = self.p
         outer = (p.chip == 0) | (p.chip == 3)
         if k == 0:
-            if self.paired is None:
-                self.swap().wait_recv()
-                for b in range(p.n):
-                    add_rows(self.mine.at[b], self.mine.at[b], self.other.at[b])
-                for c in self.group_sends():
-                    c.start()
+            if self.part is not None:
+                self.load().wait()
+            self.swap().wait_recv()
+            for b in range(p.n):
+                add_rows(self.mine.at[b], self.mine.at[b], self.other.at[b])
+            for c in self.group_sends():
+                c.start()
         elif k == 1:
-            if self.paired is not None:
-                for c in self.loads():
-                    c.wait()
             for c in self.group_sends():
                 c.wait_recv()
             add_rows(self.own, self.own, self.group.at[0])
@@ -486,17 +422,18 @@
                 def _():
                     self.line_send(2).wait_recv()
 
-            self.last_swap().start()
-            self.store().start()
+            for c in self.last_swaps() + self.stores():
+                c.start()
         else:
-            self.last_swap().wait_recv()
-            self.store().wait()
+            for c in self.last_swaps():
+                c.wait_recv()
+            for c in self.stores():
+                c.wait()
 
     def settle(self):
         p = self.p
         outer = (p.chip == 0) | (p.chip == 3)
-        if self.paired is None:
-            self.swap().wait_send()
+        self.swap().wait_send()
         for c in self.group_sends():
             c.wait_send()
         if self.square:
@@ -515,7 +452,8 @@
         else:
             for c in self.ring_sends():
                 c.wait_send()
-        self.last_swap().wait_send()
+        for c in self.last_swaps():
+            c.wait_send()
 
     @staticmethod
     def peers(p):
@@ -524,16 +462,20 @@
         return group + along + [p.sib]
 
     @staticmethod
-    def scratch(n, z, half, width, paired):
-        slots = 3 if z == 4 else z
-        kinds = n + (3 if z == 4 else z - 1) + 1
-        return [
-            pltpu.VMEM(((2 if n == 4 else 1) if paired else n, half, width), BF),
-            pltpu.VMEM((n - 1, half, width), BF),
-            pltpu.VMEM((slots, half, width), BF),
-            pltpu.SemaphoreType.DMA((kinds,)),
-            pltpu.SemaphoreType.DMA((kinds,)),
-            pltpu.SemaphoreType.DMA((3,)),
+    def kinds(n, z):
+        return n + (3 if z == 4 else z - 1) + 2
+
+    @staticmethod
+    def scratch(n, z, half, width, loaded, lead=()):
+        lead = tuple(lead)
+        kinds = Reduce.kinds(n, z)
+        return ([pltpu.VMEM(lead + (n, half, width), BF)] if loaded else []) + [
+            pltpu.VMEM(lead + (n, half, width), BF),
+            pltpu.VMEM(lead + (n - 1, half, width), BF),
+            pltpu.VMEM(lead + (3 if z == 4 else z, half, width), BF),
+            pltpu.SemaphoreType.DMA(lead + (kinds,)),
+            pltpu.SemaphoreType.DMA(lead + (kinds,)),
+            pltpu.SemaphoreType.DMA(lead + (4,)),
         ]
 
 
@@ -604,77 +546,409 @@
         ]
 
 
-def pair_kernel(n, reps, count, *refs):
-    parts, outs = refs[:count], refs[count : 2 * count]
-    scratch = refs[2 * count :]
+def feed_kernel(n, reps, half, tile, *refs):
+    (b_ref, e_ref, x_ref, gain_ref, wg_ref, wu_ref, wd_ref) = refs[:7]
+    res_out, dx_out, dm_out, norm_ref, down_out, gate_out, up_out = refs[7:14]
+    bt, acc, hid, dgate, dup, both, other, group, ring, ssem, rsem, lsem = refs[14:26]
+    xs, res_ref, dx_ref, dm_ref, down_ref, moved = refs[26:]
+    step, tiles = pl.program_id(0), pl.num_programs(0) - 1
     p = Place(n, reps)
-    greet([p.sib])
-    work = []
-    for i in range(count):
-        mine, other, sems, lsem = scratch[4 * i : 4 * i + 4]
-        swap = remote(parts[i].at[:, 1 - p.core], other, sems.at[0], sems.at[1], p.sib)
-        load = pltpu.make_async_copy(parts[i].at[:, p.core], mine, lsem.at[0])
-        store = pltpu.make_async_copy(mine, outs[i], lsem.at[1])
-        swap.start()
-        load.start()
-        work.append((mine, other, swap, load, store))
-    for mine, other, swap, load, store in work:
-        load.wait()
-        swap.wait_recv()
-        for b in range(n):
-            add_rows(mine.at[b], mine.at[b], other.at[b])
-        store.start()
-    for mine, other, swap, load, store in work:
-        store.wait()
-        swap.wait_send()
-
-
-def pair_sums(n, reps, partials):
-    views = [q.reshape(n, 2, q.shape[0] // (2 * n), q.shape[1]) for q in partials]
-    scratch = []
-    for v in views:
-        shape = (n,) + v.shape[2:]
-        scratch += [pltpu.VMEM(shape, BF), pltpu.VMEM(shape, BF), pltpu.SemaphoreType.DMA((2,)), pltpu.SemaphoreType.DMA((2,))]
+    total = b_ref.shape[0]
+    rs = 2 * half
+    rows_at = lambda j, size: pl.ds(pl.multiple_of(j * size, size), size)
+
+    def fetch():
+        return pltpu.make_async_copy(x_ref, xs, moved.at[0])
+
+    def write(k, ref, out, rows):
+        return pltpu.make_async_copy(ref.at[rows], out.at[rows], moved.at[k])
+
+    def item(j):
+        cols = pl.ds(pl.multiple_of(j * tile, tile), tile)
+        out = [
+            (lambda c: gate_out.at[c, :, cols], pl.ds(0, tile)),
+            (lambda c: up_out.at[c, :, cols], pl.ds(tile, tile)),
+        ]
+        return Reduce(
+            p,
+            out,
+            [other.at[j], group.at[j], ring.at[j]],
+            [ssem.at[j], rsem.at[j], lsem.at[j]],
+            mine=both.at[j, 0],
+            give=both.at[j, 1],
+        )
+
+    def slot(t):
+        for k in range(Reduce.STAGES):
+
+            @pl.when((t >= k) & (t - k < tiles))
+            def _():
+                item(t - k).stage(k)
+
+    @pl.when(step == 0)
+    def _():
+        greet(Reduce.peers(p))
+        fetch().start()
+        acc[...] = jnp.zeros_like(acc)
+        dx_ref[...] = jnp.zeros_like(dx_ref)
+
+        def turn(j, _):
+            rows = rows_at(j, 128)
+            bt[:, rows] = jnp.transpose(b_ref[rows, :])
+            return 0
+
+        lax.fori_loop(0, total // 128, turn, 0)
+
+    @pl.when(step < tiles)
+    def _():
+        def rows_step(j, _):
+            rows = rows_at(j, 512)
+            b, e = b_ref[rows, :], e_ref[rows, :]
+            gate = dot(b, wg_ref[...])
+            up = dot(b, wu_ref[...])
+            dh = dot_nt(e, wd_ref[...])
+            sig = jax.nn.sigmoid(gate)
+            swish = gate * sig
+            h = (swish * up).astype(BF)
+            dg = (dh * up * (sig * (1.0 + gate * (1.0 - sig)))).astype(BF)
+            du = (dh * swish).astype(BF)
+            down_ref[rows_at(step, tile), rows] = jnp.transpose(h)
+            hid[rows, :] = h
+            dgate[rows, :] = dg
+            dup[rows, :] = du
+            return 0
+
+        def sums_step(j, _):
+            rows = rows_at(j, 512)
+            acc[rows, :] += dot(hid[rows, :], wd_ref[...])
+            dx_ref[rows, :] += dot_nt(dgate[rows, :], wg_ref[...]) + dot_nt(dup[rows, :], wu_ref[...])
+            return 0
+
+        lax.fori_loop(0, total // 512, rows_step, 0)
+
+        @pl.when(step > 0)
+        def _():
+            slot(step - 1)
+
+        for at, d in ((0, dgate), (tile, dup)):
+            w = dot(bt[...], d[...]).astype(BF)
+            for s in range(n):
+                both[step, p.core, s, :, at : at + tile] = w[s * rs : s * rs + half]
+                both[step, 1 - p.core, s, :, at : at + tile] = w[s * rs + half : (s + 1) * rs]
+        item(step).start()
+        lax.fori_loop(0, total // 512, sums_step, 0)
+
+    @pl.when(step == tiles)
+    def _():
+        norm_ref[...] = jnp.zeros_like(norm_ref)
+
+        def finish(j, _):
+            rows = rows_at(j, 128)
+            x = xs[rows, :]
+            res_ref[rows, :] = (x + acc[rows, :]).astype(BF)
+            inv = lax.rsqrt(jnp.mean(x * x, axis=-1, keepdims=True) + 1e-5)
+            xn = x * inv
+            db = dx_ref[rows, :]
+            norm_ref[...] += jnp.sum(db * xn, axis=0, keepdims=True)
+            dbg = db * gain_ref[...]
+            dx = e_ref[rows, :].astype(F32) + inv * (dbg - xn * jnp.mean(dbg * xn, axis=-1, keepdims=True))
+            dx_ref[rows, :] = dx
+            dm_ref[rows, :] = dx.astype(BF)
+            return 0
+
+        fetch().wait()
+
+        def turn_down(j, _):
+            slot(tiles - 1 + j)
+            rows = rows_at(j, down_ref.shape[0] // 4)
+            down_ref[rows, :] = dot(down_ref[rows, :], e_ref[...]).astype(BF)
+            write(1 + j, down_ref, down_out, rows).start()
+            return 0
+
+        lax.fori_loop(0, 4, turn_down, 0)
+        slot(tiles + 3)
+        lax.fori_loop(0, total // 128, finish, 0)
+        every = pl.ds(0, total)
+        results = [
+            write(5, res_ref, res_out, every),
+            write(6, dx_ref, dx_out, every),
+            write(7, dm_ref, dm_out, every),
+        ]
+        for c in results:
+            c.start()
+
+        def tail(t, _):
+            slot(t)
+            return 0
+
+        lax.fori_loop(tiles + 4, tiles + Reduce.STAGES - 1, tail, 0)
+
+        def settle(j, _):
+            item(j).settle()
+            return 0
+
+        lax.fori_loop(0, tiles, settle, 0)
+        for j in range(4):
+            write(1 + j, down_ref, down_out, rows_at(j, down_ref.shape[0] // 4)).wait()
+        for c in results:
+            c.wait()
+
+
+def feed(n, reps, b, e, x2, gain, wg, wu, wd):
+    total, width = b.shape
+    ff = wg.shape[1]
+    tile, z = 256, reps // 2
+    tiles, half = ff // tile, width // (2 * n)
+    once = lambda *sh: pl.BlockSpec(sh, lambda j: (0,) * len(sh), pipeline_mode=pl.Buffered(1))
+    col = lambda: pl.BlockSpec((width, tile), lambda j: (0, jnp.minimum(j, tiles - 1)))
+    row = lambda: pl.BlockSpec((tile, width), lambda j: (jnp.minimum(j, tiles - 1), 0))
     anywhere = pl.BlockSpec(memory_space=pl.ANY)
+    sd = jax.ShapeDtypeStruct
     return pl.pallas_call(
-        functools.partial(pair_kernel, n, reps, len(views)),
-        out_shape=[jax.ShapeDtypeStruct((n,) + v.shape[2:], BF) for v in views],
-        in_specs=[anywhere] * len(views),
-        out_specs=[anywhere] * len(views),
-        scratch_shapes=scratch,
-        compiler_params=pltpu.CompilerParams(collective_id=1, has_side_effects=True, vmem_limit_bytes=40 << 20),
-        name="pair_sums",
-    )(*views)
+        functools.partial(feed_kernel, n, reps, half, tile),
+        grid=(tiles + 1,),
+        in_specs=[once(total, width)] * 2 + [anywhere, once(1, width), col(), col(), row()],
+        out_specs=[anywhere] * 3 + [once(1, width), anywhere, anywhere, anywhere],
+        out_shape=[
+            sd((total, width), BF),
+            sd((total, width), F32),
+            sd((total, width), BF),
+            sd((1, width), F32),
+            sd((ff, total), BF),
+            sd((2, half, ff), BF),
+            sd((2, half, ff), BF),
+        ],
+        scratch_shapes=[
+            pltpu.VMEM((width, total), BF),
+            pltpu.VMEM((total, width), F32),
+            pltpu.VMEM((total, tile), BF),
+            pltpu.VMEM((total, tile), BF),
+            pltpu.VMEM((total, tile), BF),
+            pltpu.VMEM((tiles, 2, n, half, 2 * tile), BF),
+        ]
+        + Reduce.scratch(n, z, half, 2 * tile, False, (tiles,))
+        + [
+            pltpu.VMEM((total, width), F32),
+            pltpu.VMEM((total, width), BF),
+            pltpu.VMEM((total, width), F32),
+            pltpu.VMEM((total, width), BF),
+            pltpu.VMEM((ff, total), BF),
+            pltpu.SemaphoreType.DMA((8,)),
+        ],
+        compiler_params=pltpu.CompilerParams(collective_id=1, has_side_effects=True, vmem_limit_bytes=63 << 20),
+        name="feed_forward",
+    )(b, e, x2, gain, wg, wu, wd)
+
+
+def forward_kernel(n, reps, width, *refs):
+    x_ref, cols_ref, segr_ref, m_ref, vec_ref, high_ref, low_ref = refs[:7]
+    owns = refs[7:15]
+    a_ref, q_ref, k_ref, v_ref, g_ref, r_ref, y_ref, o_ref, st_ref = refs[15:24]
+    x2_ref, b_ref, vec_out, high_out, low_out = refs[24:29]
+    outs = refs[29:37]
+    state, esc, xs, ys, vecs, highs, lows = refs[37:44]
+    kept = refs[44:49]
+    small_send, small_recv, ssem, rsem, lsem = refs[49:]
+    step, nc = pl.program_id(0), pl.num_programs(0) - 1
+    p = Place(n, reps)
+    gather = Gather(p, owns, list(kept) + list(outs[5:]), [ssem, rsem])
+    smalls = [(vec_ref, vecs), (high_ref, highs), (low_ref, lows)]
+
+    def small(k, j):
+        src, dst = smalls[k]
+        return remote(src, dst.at[p.me], small_send.at[k, j - 1], small_recv.at[k, j - 1], (p.rep, p.peer(j)))
+
+    def keep(i):
+        return pltpu.make_async_copy(kept[i], outs[i], lsem.at[i])
+
+    def whole(i):
+        w = kept[i][...]
+        return w.reshape(-1, w.shape[-1])
+
+    @pl.when(step == 0)
+    def _():
+        greet(gather.peers())
+        for i in range(4):
+            gather.start(i)
+        for k in range(3):
+            for j in range(1, n):
+                small(k, j).start()
+            src, dst = smalls[k]
+            dst[p.me] = src[...]
+        for i in range(4):
+            gather.relay(i)
+        for i in range(4, 8):
+            gather.start(i)
+        for k in range(3):
+            for j in range(1, n):
+                small(k, j).wait()
+        rs = low_ref.shape[0]
+        for s in range(n):
+            at = slice(s * rs, (s + 1) * rs)
+            vec_out[0:2, at] = vecs[s, 0:2, 0:rs]
+            low_out[at, :] = lows[s]
+
+        def spread(part, out_width):
+            own = part(0).shape[1]
+            total = None
+            for s in range(n):
+                col = lax.broadcasted_iota(jnp.int32, (own, out_width), 1)
+                row = lax.broadcasted_iota(jnp.int32, (own, out_width), 0)
+                piece = dot(part(s), (col == row + s * own).astype(F32).astype(BF))
+                total = piece if total is None else total + piece
+            return total
+
+        nb, ng = 512 // n, VH // n
+        vec_out[2:3, 0:512] = spread(lambda s: vecs[s, 2:3, 0:nb].astype(BF), 512)
+        vec_out[3:4, 0:VH] = spread(lambda s: vecs[s, 3:4, 0:ng].astype(BF), VH)
+        high_out[...] = spread(lambda s: highs[s], 512).astype(BF)
+        for i in range(4):
+            gather.pass_on(i)
+        for i in range(4):
+            gather.done(i)
+            keep(i).start()
+        state[...] = jnp.zeros_like(state)
+
+    @pl.when(step < nc)
+    def _():
+        rows = pl.ds(pl.multiple_of(step * C, C), C)
+        xb = x_ref[...]
+        xs[rows, :] = xb
+        x = xb.astype(F32)
+        inv = lax.rsqrt(jnp.mean(x * x, axis=-1, keepdims=True) + 1e-5)
+        a = (x * inv * vec_out[0:1, :]).astype(BF)
+        a_ref[...] = a
+        q_ref[...] = dot(a, whole(0)).astype(BF)
+        k_ref[...] = dot(a, whole(1)).astype(BF)
+        v_ref[...] = dot(a, whole(2)).astype(BF)
+        g_ref[...] = dot(a, whole(3)).astype(BF)
+        r_ref[...] = dot(a, low_out[...]).astype(BF)
+        fwd_chunk(
+            step, q_ref, k_ref, v_ref, g_ref, r_ref, high_out, vec_out.at[2:3, 0:512], vec_out.at[3:4, 0:VH],
+            cols_ref, segr_ref, m_ref, y_ref, o_ref, st_ref, state, esc,
+        )
+        ys[rows, :] = y_ref[...]
+
+    @pl.when(step == 2)
+    def _():
+        gather.relay(4)
+
+    @pl.when(step == 4)
+    def _():
+        gather.pass_on(4)
+
+    @pl.when(step == nc)
+    def _():
+        gather.relay(5)
+        gather.done(4)
+        keep(4).start()
+
+        def join(j, _):
+            rows = pl.ds(pl.multiple_of(j * 256, 256), 256)
+            x2 = xs[rows, :].astype(F32) + dot(ys[rows, :], whole(4))
+            x2_ref[rows, :] = x2
+            inv = lax.rsqrt(jnp.mean(x2 * x2, axis=-1, keepdims=True) + 1e-5)
+            b_ref[rows, :] = (x2 * inv * vec_out[1:2, :]).astype(BF)
+            return 0
+
+        lax.fori_loop(0, xs.shape[0] // 256, join, 0)
+        gather.pass_on(5)
+        gather.relay(6)
+        gather.pass_on(6)
+        gather.relay(7)
+        gather.pass_on(7)
+        for i in range(5, 8):
+            gather.done(i)
+        for i in range(5):
+            keep(i).wait()
+
+
+def forward(n, reps, x, cols, segr, vec, high, low, weights):
+    T, width = x.shape
+    nc = T // C
+    M = jnp.asarray(level_sums(), BF)
+    nr = M.shape[0]
+    owns = [halves(w) for w in weights]
+    last = lambda i: jnp.minimum(i, nc - 1)
+    blk = lambda w: pl.BlockSpec((C, w), lambda i: (last(i), 0))
+    full = lambda *sh: pl.BlockSpec(sh, lambda i: (0,) * len(sh), pipeline_mode=pl.Buffered(1))
+    anywhere = pl.BlockSpec(memory_space=pl.ANY)
+    sd = jax.ShapeDtypeStruct
+    shapes = [(n,) + o.shape for o in owns]
+    kinds = 2 * (n - 1) + 1
+    res = pl.pallas_call(
+        functools.partial(forward_kernel, n, reps, width),
+        grid=(nc + 1,),
+        in_specs=[blk(width), blk(2), full(nc, 1, C), full(nr, C), full(*vec.shape), full(*high.shape), full(*low.shape)]
+        + [anywhere] * 8,
+        out_specs=[blk(w) for w in (width, 512, 512, 1024, 1024, 16, 1024, 1024)]
+        + [pl.BlockSpec((1, HEADS, VH, KH), lambda i: (last(i), 0, 0, 0))]
+        + [full(T, width), full(T, width), full(8, width), full(16, 512), full(width, 16)]
+        + [anywhere] * 8,
+        out_shape=[sd((T, w), BF) for w in (width, 512, 512, 1024, 1024, 16, 1024, 1024)]
+        + [
+            sd((nc, HEADS, VH, KH), BF),
+            sd((T, width), F32),
+            sd((T, width), BF),
+            sd((8, width), F32),
+            sd((16, 512), BF),
+            sd((width, 16), BF),
+        ]
+        + [sd(shape, BF) for shape in shapes],
+        scratch_shapes=[
+            pltpu.VMEM((HEADS, VH, KH), F32),
+            pltpu.VMEM((nr, 512), F32),
+            pltpu.VMEM((T, width), BF),
+            pltpu.VMEM((T, 1024), BF),
+            pltpu.VMEM((n,) + vec.shape, F32),
+            pltpu.VMEM((n,) + high.shape, BF),
+            pltpu.VMEM((n,) + low.shape, BF),
+        ]
+        + [pltpu.VMEM(shape, BF) for shape in shapes[:5]]
+        + [
+            pltpu.SemaphoreType.DMA((3, n - 1)),
+            pltpu.SemaphoreType.DMA((3, n - 1)),
+            pltpu.SemaphoreType.DMA((8, kinds)),
+            pltpu.SemaphoreType.DMA((8, kinds)),
+            pltpu.SemaphoreType.DMA((5,)),
+        ],
+        compiler_params=pltpu.CompilerParams(collective_id=0, has_side_effects=True, vmem_limit_bytes=60 << 20),
+        name="gla_fwd_gather",
+    )(x, cols, segr, M, vec, high, low, *owns)
+    return res[:14], [o.reshape(-1, o.shape[-1]) for o in res[14:]]
 
 
 def backward_kernel(n,reps,plan,half,*refs):
     (q_ref,k_ref,v_ref,g_ref,r_ref,o_ref,st_ref,dy_ref,a_ref,x_ref,dx_ref,cols_ref,
      wh_ref,bias_ref,gain_ref,gmix_ref,nmlp_ref,segr_ref,m_ref,wq_ref,wk_ref,wv_ref,wg_ref,wl_ref)=refs[:24]
-    paired=refs[24:28]
-    gt_ref,small_ref=refs[28:30]
-    outs=refs[30:38]
-    dstate,rcar,esc,dcs,dall,at_ref,dz_ref,low_acc,high_acc,gb_ref,gg_ref,nmix_ref,smb,both=refs[38:52]
-    rest=refs[52:]
+    parts=refs[24:26]
+    gt_ref,small_ref=refs[26:28]
+    outs=refs[28:34]
+    dstate,rcar,esc,dcs,dall,at_ref,dz_ref,low_acc,high_acc,gb_ref,gg_ref,nmix_ref,smb,both=refs[34:48]
+    rest=refs[48:]
     steps=pl.num_programs(0); step=pl.program_id(0); nc=steps-1
     p=Place(n,reps)
     items=[]
-    for j,(which,at,width,source) in enumerate(plan):
-        mem=rest[6*j:6*j+6]
+    for which,at,width,source in plan:
+        count=7 if source is None else 6
+        mem,rest=rest[:count],rest[count:]
         cols=pl.ds(at,width)
-        out=lambda c,which=which,cols=cols: outs[which].at[c,:,cols]
+        out=[(lambda c,which=which,cols=cols: outs[which].at[c,:,cols],pl.ds(0,width))]
         if source is None:
-            items.append(Reduce(p,out,mem[:3],mem[3:],paired=paired[which].at[:,:,cols]))
+            items.append(Reduce(p,out,mem[:4],mem[4:],part=parts[which].at[:,:,:,cols]))
         else:
             cols=pl.ds(source,width)
             items.append(Reduce(p,out,mem[:3],mem[3:],mine=both.at[0,:,:,cols],give=both.at[1,:,:,cols]))
-    mem=rest[6*len(plan):]
+    mem=rest
     small=Small(p,smb,small_ref,mem[:4],mem[4:])
-    ready=[it for it in items if it.paired is not None]
-    fresh=[it for it in items if it.paired is None]
+    ready=[it for it in items if it.part is not None]
+    fresh=[it for it in items if it.part is None]
+
+    line=ready+[None]*(8-len(ready))+fresh
 
     def slot(t):
         for k in range(Reduce.STAGES):
-            if 0<=t-k<len(items): items[t-k].stage(k)
+            if 0<=t-k<len(line) and line[t-k] is not None: line[t-k].stage(k)
 
     @pl.when(step==0)
     def _():
@@ -736,13 +1010,13 @@
             f+=count
             slot(t); t+=1
             small.stage((t-9))
-        last=len(items)+Reduce.STAGES-1
+        last=len(line)+Reduce.STAGES-1
         while t<last:
             slot(t); t+=1
         for it in items: it.settle()
         small.settle()
 
-def backward(n,reps,q,k,v,g,r,o,st,dy,first,tokens,dx2,wh,bias,gain,gmix,nmlp,cols,segr,weights,pairs):
+def backward(n,reps,q,k,v,g,r,o,st,dy,first,tokens,dx2,wh,bias,gain,gmix,nmlp,cols,segr,weights,partials):
     T=q.shape[0]; nc=T//C; z=reps//2
     assert nc==8
     M=jnp.asarray(level_sums(),BF); nr=M.shape[0]
@@ -751,13 +1025,14 @@
     sd=jax.ShapeDtypeStruct
     anywhere=pl.BlockSpec(memory_space=pl.ANY)
     half=first.shape[1]//(2*n)
+    pairs=[q.reshape(n,2,q.shape[0]//(2*n),q.shape[1]) for q in partials]
     plan,scratch=[],[]
-    for which,(pair,cut) in enumerate(zip(pairs,(4,4,4,2))):
-        tiles=pair.shape[2]//128
+    for which,(pair,cut) in enumerate(zip(pairs,(4,2))):
+        tiles=pair.shape[3]//128
         edges=[128*(tiles*j//cut) for j in range(cut+1)]
         for at,end in zip(edges[:-1],edges[1:]):
-            plan.append((which,at,end-at,None)); scratch+=Reduce.scratch(n,z,pair.shape[1],end-at,True)
-    for which,at,width,source in ((7,0,512,2048),(7,512,512,2560),(6,0,512,1024),(6,512,512,1536),(4,0,512,0),(5,0,512,512)):
+            plan.append((which,at,end-at,None)); scratch+=Reduce.scratch(n,z,pair.shape[2],end-at,True)
+    for which,at,width,source in ((5,0,512,2048),(5,512,512,2560),(4,0,512,1024),(4,512,512,1536),(2,0,512,0),(3,0,512,512)):
         plan.append((which,at,width,source)); scratch+=Reduce.scratch(n,z,half,width,False)
     scratch+=Small.scratch(n,z,40,512)
     out=lambda h,w: sd((2,h,w),BF)
@@ -765,9 +1040,9 @@
         in_specs=[blk(512),blk(512),blk(1024),blk(1024),blk(16),blk(1024),pl.BlockSpec((1,HEADS,VH,KH),lambda i:(jnp.maximum(nc-1-i,0),0,0,0)),blk(1024),
                   blk(1024),blk(1024),blk(1024),blk(2),
                   full(16,512),full(1,512),full(1,256),full(1,1024),full(1,1024),full(nc,1,C),full(nr,C),
-                  full(1024,512),full(1024,512),full(1024,1024),full(1024,1024),full(1024,16)]+[anywhere]*4,
-        out_specs=[blk(1024),pl.BlockSpec((40,512),lambda i:(0,0))]+[anywhere]*8,
-        out_shape=[sd((T,1024),F32),sd((40,512),F32)]+[out(q.shape[1],q.shape[2]) for q in pairs]+[out(half,512),out(half,512),out(half,1024),out(half,1024)],
+                  full(1024,512),full(1024,512),full(1024,1024),full(1024,1024),full(1024,16)]+[anywhere]*2,
+        out_specs=[blk(1024),pl.BlockSpec((40,512),lambda i:(0,0))]+[anywhere]*6,
+        out_shape=[sd((T,1024),F32),sd((40,512),F32)]+[out(q.shape[2],q.shape[3]) for q in pairs]+[out(half,512),out(half,512),out(half,1024),out(half,1024)],
         scratch_shapes=[pltpu.VMEM((HEADS,VH,KH),F32),pltpu.VMEM((1,512),F32),pltpu.VMEM((nr,512),F32),pltpu.VMEM((C,1024),BF),
                         pltpu.VMEM((T,3072),BF),pltpu.VMEM((1024,T),BF),pltpu.VMEM((C,512),BF),pltpu.VMEM((16,1024),F32),pltpu.VMEM((16,512),F32),
                         pltpu.VMEM((1,512),F32),pltpu.VMEM((1,256),F32),pltpu.VMEM((1,1024),F32),pltpu.VMEM((n,40,512),F32),
@@ -779,10 +1054,6 @@
 
 def matmul(left, right):
     return jnp.dot(left, right, preferred_element_type=F32)
-
-
-def rms_parts(values):
-    return lax.rsqrt(jnp.mean(values * values, axis=-1, keepdims=True) + 1e-05)
 
 
 def local(
@@ -806,68 +1077,33 @@
     w_up,
     w_down,
 ):
-    small = (norm_mix, norm_mlp, decay_bias, head_gain, w_low, w_high)
-    sizes = [a.size for a in small]
-    rows = -(-sum(sizes) // 2048) * 16
-    packed = jnp.concatenate([a.reshape(-1) for a in small])
-    packed = jnp.pad(packed, (0, rows * 128 - sum(sizes))).reshape(rows, 128)
-    packs, (query_w, key_w, value_w, outgate_w, out_w, gate_w, up_w, down_w) = gather_weights(
-        shards, reps, packed, (w_query, w_key, w_value, w_outgate, w_out, w_gate, w_up, w_down)
-    )
-    packs = packs.reshape(shards, -1)
-    offsets = np.cumsum([0] + sizes)
-    cut = [packs[:, offsets[i] : offsets[i + 1]] for i in range(len(small))]
-    gain_mix = cut[0].reshape(-1).astype(F32)
-    gain_feed = cut[1].reshape(-1).astype(F32)
-    bias = cut[2].reshape(1, -1).astype(F32)
-    gain_head = cut[3].reshape(1, -1).astype(F32)
-    low_w = cut[4].reshape(-1, w_low.shape[1])
-    high_w = cut[5].reshape(shards, w_high.shape[0], -1).transpose(1, 0, 2).reshape(w_high.shape[0], -1)
     total = tokens.shape[0] * tokens.shape[1]
     width = tokens.shape[2]
     cols, segr = seg_views(segments)
-    inputs = tokens.reshape(total, width).astype(F32)
-    inv_mix = rms_parts(inputs)
-    first = (inputs * inv_mix * gain_mix).astype(BF)
-    query = matmul(first, query_w).astype(BF)
-    keys = matmul(first, key_w).astype(BF)
-    values = matmul(first, value_w).astype(BF)
-    outgate = matmul(first, outgate_w).astype(BF)
-    lowrank = matmul(first, low_w).astype(BF)
-    mixed, heads, states = forward(
-        query, keys, values, outgate, lowrank, high_w, bias, gain_head, cols, segr
+    wide = max(norm_mix.shape[0], 128)
+    rows = [jnp.pad(v.astype(F32), (0, wide - v.shape[0])) for v in (norm_mix, norm_mlp, decay_bias, head_gain)]
+    vec = jnp.concatenate([jnp.stack(rows), jnp.zeros((4, wide), F32)])
+    (
+        (first, query, keys, values, outgate, lowrank, mixed, heads, states, resid, second, vecs, high_w, low_w),
+        (query_w, key_w, value_w, outgate_w, out_w, gate_w, up_w, down_w),
+    ) = forward(
+        shards,
+        reps,
+        tokens.reshape(total, width),
+        cols,
+        segr,
+        vec,
+        w_high,
+        w_low,
+        (w_query, w_key, w_value, w_outgate, w_out, w_gate, w_up, w_down),
     )
-    resid = inputs + matmul(mixed, out_w)
-    inv_feed = rms_parts(resid)
-    second = (resid * inv_feed * gain_feed).astype(BF)
-    gate = matmul(second, gate_w)
-    upward = matmul(second, up_w)
-    sigma = jax.nn.sigmoid(gate)
-    swish = gate * sigma
-    hidden = (swish * upward).astype(BF)
-    result = (resid + matmul(hidden, down_w)).astype(BF)
+    gain_mix, gain_feed, bias, gain_head = vecs[0:1], vecs[1:2], vecs[2:3, :512], vecs[3:4, :VH]
     grad_out = cotangent.reshape(total, width)
-    part_down = dot_tn(hidden, grad_out)
-    grad_hidden = dot_nt(grad_out, down_w)
-    slope = sigma * (1.0 + gate * (1.0 - sigma))
-    grad_gate = (grad_hidden * upward * slope).astype(BF)
-    grad_up = (grad_hidden * swish).astype(BF)
-    part_gate = dot_tn(second, grad_gate)
-    part_up = dot_tn(second, grad_up)
-    grad_second = dot_nt(grad_gate, gate_w) + dot_nt(grad_up, up_w)
-    part_norm_mlp = jnp.sum(grad_second * resid * inv_feed, axis=0)
-    scaled = grad_second * gain_feed
-    grad_resid = (
-        grad_out.astype(F32)
-        + inv_feed * scaled
-        - resid * inv_feed**3 * jnp.mean(scaled * resid, axis=-1, keepdims=True)
+    result, grad_resid, branch, part_norm_mlp, part_down, sum_gate, sum_up = feed(
+        shards, reps, second, grad_out, resid, gain_feed, gate_w, up_w, down_w
     )
-    branch = grad_resid.astype(BF)
     part_out = dot_tn(mixed, branch)
     grad_mixed = dot_nt(branch, out_w).astype(BF)
-    pairs = pair_sums(
-        shards, reps, [q.astype(BF) for q in (part_down, part_gate, part_up, part_out)]
-    )
     grad_inputs, small_sums, sums = backward(
         shards,
         reps,
@@ -885,14 +1121,15 @@
         high_w,
         bias,
         gain_head,
-        gain_mix[None],
-        part_norm_mlp[None],
+        gain_mix,
+        part_norm_mlp,
         cols,
         segr,
         (query_w, key_w, value_w, outgate_w, low_w),
-        pairs,
+        (part_down, part_out.astype(BF)),
     )
-    sum_down, sum_gate, sum_up, sum_out, sum_query, sum_key, sum_value, sum_outgate = [s.astype(F32) for s in sums]
+    sum_gate, sum_up = [s.reshape(-1, s.shape[2]).astype(F32) for s in (sum_gate, sum_up)]
+    sum_down, sum_out, sum_query, sum_key, sum_value, sum_outgate = [s.astype(F32) for s in sums]
     me = lax.axis_index("shard")
     rs = w_low.shape[0]
 

time: 462 us -> 402 us (0.87); the launches traced: 455 us -> 401 us
  matrix products: 117 us -> 9.78 us
  Pallas kernels: 304 us -> 357 us
    pallas_call x3 -> x2, Pallas kernels: 147 us -> 240 us  [the longest x1 139 us: forward(): pl.pallas_call(functools.partial(forward_kernel, n, reps, width), grid=(n...]
    dot_general x4 -> x1, matrix products: 47.6 us -> 3.7 us  [dot_nt(): lax.dot_general(a, b, (((1,), (1,)), ((), ())), preferred_element_type=F32)]
    dot_general x9 -> x0, matrix products: 42.5 us -> none  [matmul(): return jnp.dot(left, right, preferred_element_type=F32)]
    pallas_call x1, Pallas kernels: 157 us -> 116 us  [backward(): pl.pallas_call(functools.partial(backward_kernel, n, reps, tuple(plan), h...]
    dot_general x4 -> x1, matrix products: 27.1 us -> 6.08 us  [dot_tn(): lax.dot_general(a, b, (((0,), (0,)), ((), ())), preferred_element_type=F32)]
    convert_element_type x5 -> x4, other arithmetic: 10.8 us -> 8.03 us  [local(): s.astype(F32)]
where the time goes in v3:
time: 402 us; the launch traced here: 401 us
  Pallas kernels  357 us (89%)
  local copies, waits for them, and re-layouts  18.7 us (5%)
  other arithmetic  15.2 us (4%)
  matrix products  9.78 us (2%)
    pallas_call x1, Pallas kernels, forward(): pl.pallas_call(functools.partial(forward_kernel, n, reps, width), grid=(n...  139 us
    pallas_call x1, Pallas kernels, backward(): pl.pallas_call(functools.partial(backward_kernel, n, reps, tuple(plan), h...  116 us
    pallas_call x1, Pallas kernels, feed(): pl.pallas_call(functools.partial(feed_kernel, n, reps, half, tile), grid=...  102 us

profile of v3, /device:TPU:1, one launch (start us, length us, event | category | flops | bytes accessed | tf_op | source)
XLA Modules:
  0.0 401.4 jit_solution(14818725932744402077)
XLA Ops:
  0.6 0.7 stack.40
  1.3 0.7 pad_convert_fusion.1
  2.0 0.7 pad_convert_fusion
  2.6 0.7 stack.41
  3.3 0.8 pad_add_fusion.1
  4.0 0.7 pad_add_fusion
  4.8 0.6 concatenate.7.refs_4_
  5.4 1.4 copy.40.refs_6_
  6.8 1.0 copy.39.refs_1_.refs_11_
  7.8 138.6 %gla_fwd_gather.1 = (bf16[1024,1024]{1,0:T(8,128)(2,1)}, bf16[1024,512]{1,0:T(8,128)(2,1)}, bf16[1024,512]{1,0:T(8,128)(2,1)}, bf16[1024,1024]{1,0:T(8,128)(2,1)...) custom-call(bf16[1024,1024]{1,0:T(8,128)(2,1)} %bitcast.67, ...), custom_call_target="tpu_custom_call" | custom-call | tf_op jit(solution)/shard_map/gla_fwd_gather/pallas_call | solution.py:879
  146.5 1.3 slice.40.refs_14_
  147.7 1.3 slice.39.refs_13_
  149.0 1.4 fusion.3
  150.5 101.9 %feed_forward.1 = (bf16[1024,1024]{1,0:T(8,128)(2,1)}, f32[1024,1024]{1,0:T(8,128)}, bf16[1024,1024]{1,0:T(8,128)(2,1)}, f32[1,1024]{1,0:T(1,128)}, bf16[2816,10...) custom-call(bf16[1024,1024]{1,0:T(8,128)(2,1)} %get-tuple-element.53.refs_0_, ...), custom_call_target="tpu_custom_call" | custom-call | tf_op jit(solution)/shard_map/feed_forward/pallas_call | solution.py:707
  252.3 0.0 copy-start.7
  252.3 0.0 copy-start.8
  252.3 6.1 %convolution_convert_fusion = bf16[1024,1024]{1,0:T(8,128)(2,1)} fusion(bf16[1024,1024]{1,0:T(8,128)(2,1)} %get-tuple-element.79, bf16[1024,1024]{1,0:T(8,128)(2,1)} %get-tuple-element.67), kind=kOutput, calls=%fused_computation | convolution fusion | flops 2148532224 | bytes 6291456 | tf_op jit(solution)/shard_map/dot_general | solution.py:25
  258.4 0.0 copy-done.7
  258.4 0.0 copy-done.8
  258.4 3.7 convolution_convert_fusion.1.refs_7_
  262.1 116.5 %gla_bwd_reduce.1 = (f32[1024,1024]{1,0:T(8,128)}, f32[40,512]{1,0:T(8,128)}, bf16[2,352,1024]{2,1,0:T(8,128)(2,1)}, bf16[2,128,1024]{2,1,0:T(8,128)(2,1)}, bf16...) custom-call(bf16[1024,512]{1,0:T(8,128)(2,1)} %get-tuple-element.60., ...), custom_call_target="tpu_custom_call" | custom-call | tf_op jit(solution)/shard_map/gla_bwd_reduce/pallas_call | solution.py:1039
  378.6 0.0 copy-start.5
  378.6 0.0 copy-start.6
  378.6 0.8 slice.45
  379.4 0.5 fusion
  379.9 1.4 fusion.2
  381.3 0.6 fusion.1
  381.9 1.3 slice_bitcast_fusion
  383.2 0.8 slice.44
  384.0 0.6 constant_dynamic-slice_fusion.2
  384.6 2.1 bitcast_convert_fusion.5
  386.7 0.0 copy-start.2
  386.7 2.2 bitcast_convert_fusion.6
  388.9 0.0 copy-done.5
  388.9 0.0 copy-done.6
  389.0 1.6 bitcast_convert_fusion.3
  390.6 0.0 copy-done.2
  390.6 0.0 copy-start.3
  390.6 0.0 copy-start.4
  390.6 2.0 bitcast_convert_fusion
  392.6 0.0 copy-done.3
  392.6 0.7 copy-done.4
  393.4 0.0 copy-start.1
  393.4 3.1 bitcast_convert_fusion.1
  396.5 0.0 copy-done.1
  396.5 0.0 copy-start
  396.5 1.3 copy.44
  397.8 1.6 copy-done
  399.4 2.0 copy.45
  (1 shorter events, 0.0 us)
Async XLA Ops:
  252.3 6.1 %copy-start.7 = (bf16[4,2,128,1024]{3,2,1,0:T(8,128)(2,1)S(1)}, bf16[4,2,128,1024]{3,2,1,0:T(8,128)(2,1)}, u32[]{:S(2)}) copy-start(bf16[4,2,128,1024]{3,2,1,0:T(8,128)(2,1)} %get-tuple-element.68) | copy-start | bytes 6291460
  252.3 6.1 %copy-start.8 = (bf16[1024,1024]{1,0:T(8,128)(2,1)S(1)}, bf16[1024,1024]{1,0:T(8,128)(2,1)}, u32[]{:S(2)}) copy-start(bf16[1024,1024]{1,0:T(8,128)(2,1)} %get-tuple-element.67) | copy-start | bytes 6291460
  378.6 10.4 %copy-start.5 = (bf16[2,128,1024]{2,1,0:T(8,128)(2,1)S(1)}, bf16[2,128,1024]{2,1,0:T(8,128)(2,1)}, u32[]{:S(2)}) copy-start(bf16[2,128,1024]{2,1,0:T(8,128)(2,1)} %get-tuple-element.86) | copy-start | bytes 1572868
  378.6 10.3 %copy-start.6 = (bf16[2,128,1024]{2,1,0:T(8,128)(2,1)S(1)}, bf16[2,128,1024]{2,1,0:T(8,128)(2,1)}, u32[]{:S(2)}) copy-start(bf16[2,128,1024]{2,1,0:T(8,128)(2,1)} %get-tuple-element.85) | copy-start | bytes 1572868
  386.7 3.9 copy-start.2
  390.6 2.0 copy-start.3
  390.6 2.8 copy-start.4
  393.4 3.1 copy-start.1
  396.5 2.9 copy-start

commit v4 on v3

--- a/solution.py
+++ b/solution.py
@@ -30,21 +30,23 @@
 def log_rate(zb):
     return (jnp.minimum(zb,0.0)-jnp.log1p(jnp.exp(-jnp.abs(zb))))*(1.0/16.0)
 
-def level_map(segc,segr):
+def level_map(i,segr_ref):
     t=lax.broadcasted_iota(jnp.int32,(C,C),0); s=lax.broadcasted_iota(jnp.int32,(C,C),1)
-    x=t^s
-    return jnp.where(segc==segr,x,-1),t,s
-
-def fwd_chunk(i,q_ref,k_ref,v_ref,g_ref,r_ref,wh_ref,bias_ref,gain_ref,cols_ref,segr_ref,m_ref,y_ref,o_ref,st_ref,state,esc):
+    segr=segr_ref[i].astype(F32)
+    prev=jnp.where(i==0,-1.0,segr_ref[jnp.maximum(i-1,0)][:,C-1:C].astype(F32))
+    segc=jnp.sum(jnp.where(t==s,segr,0.0),axis=1,keepdims=True)
+    before=jnp.sum(jnp.where(t==s+1,segr,0.0),axis=1,keepdims=True)
+    first=lax.broadcasted_iota(jnp.int32,(C,1),0)==0
+    start=jnp.where(first,prev,before)!=segc
+    last=segr[:,C-1:C]
+    lv=jnp.where(segc==segr,t^s,-1)
+    return lv,t,s,(segc==prev).astype(F32),(segc==last).astype(F32),(prev==last).astype(F32),start
+
+def fwd_chunk(i,q_ref,k_ref,v_ref,g_ref,r_ref,wh_ref,bias_ref,gain_ref,segr_ref,m_ref,y_ref,o_ref,st_ref,state,esc):
     f=log_rate(gate_in(r_ref,wh_ref,bias_ref)).astype(BF)
     esc[...]=jnp.exp(dot(m_ref[...],f))
-    segc=cols_ref[:,0:1]; segr=segr_ref[i]
-    lv,t,s=level_map(segc,segr)
+    lv,t,s,keep,tail,stay,start=level_map(i,segr_ref)
     lv=jnp.where(t>=s,lv,-1)
-    prev=jnp.where(i==0,-1,segr_ref[jnp.maximum(i-1,0)][:,C-1:C])
-    last=segr[:,C-1:C]
-    keep=(segc==prev).astype(F32); tail=(segc==last).astype(F32)
-    stay=(prev==last).astype(F32)
     row=lax.broadcasted_iota(jnp.int32,(C,KH),0)
     nl=len(LEVELS)
     for h in range(HEADS):
@@ -65,19 +67,14 @@
         g=g_ref[:,vs].astype(F32)
         y_ref[:,vs]=(o*m*gain_ref[...]*(g*jax.nn.sigmoid(g))).astype(BF)
 
-def bwd_chunk(i,q_ref,k_ref,v_ref,g_ref,r_ref,o_ref,st_ref,dy_ref,wh_ref,bias_ref,gain_ref,cols_ref,segr_ref,m_ref,
+def bwd_chunk(i,q_ref,k_ref,v_ref,g_ref,r_ref,o_ref,st_ref,dy_ref,wh_ref,bias_ref,gain_ref,segr_ref,m_ref,
              dq_ref,dk_ref,dv_ref,dg_ref,dz_ref,gb_ref,gg_ref,dstate,rcar,esc,dcs):
     zb=gate_in(r_ref,wh_ref,bias_ref)
     f=log_rate(zb).astype(BF)
     esc[...]=jnp.exp(dot(m_ref[...],f))
-    segc=cols_ref[:,0:1]; segr=segr_ref[i]
-    lv,t,s=level_map(segc,segr)
+    lv,t,s,keep,tail,stay,start=level_map(i,segr_ref)
     lvu=jnp.where(t<=s,lv,-1)
     lower=t>=s
-    prev=jnp.where(i==0,-1,segr_ref[jnp.maximum(i-1,0)][:,C-1:C])
-    last=segr[:,C-1:C]
-    keep=(segc==prev).astype(F32); tail=(segc==last).astype(F32)
-    stay=(prev==last).astype(F32)
     row=lax.broadcasted_iota(jnp.int32,(C,KH),0)
     nl=len(LEVELS)
     gain=gain_ref[...]
@@ -126,21 +123,20 @@
         dcs2=rold
         um=jnp.where((lv>=0)&(t<=s),1.0,0.0).astype(BF)
         df=dot(um,dcs[:,ks])+dot(um,dcs[:,HEADS*KH+h*KH:HEADS*KH+(h+1)*KH])+tail*dcs2
-        start=cols_ref[:,1:2]!=segc
         dp=jnp.where(start,0.0,df)*(jax.nn.sigmoid(-zb[:,ks])*(1.0/16.0))
         dz_ref[:,ks]=dp.astype(BF)
         gb_ref[:,ks]+=jnp.sum(dp,axis=0,keepdims=True)
     gg_ref[...]+=ggacc
 
-def seg_views(segments):
+def seg_rows(segments):
     b,l=segments.shape
-    seg=(segments+8*lax.broadcasted_iota(jnp.int32,(b,l),0)).reshape(-1)
-    prev=jnp.concatenate([jnp.full((1,),-1,jnp.int32),seg[:-1]])
-    cols=jnp.stack([seg,prev],axis=1)
-    return cols,seg.reshape(-1,1,C)
+    seg=segments if b==1 else segments+8*lax.broadcasted_iota(jnp.int32,(b,l),0)
+    return seg.reshape(-1,1,C)
 
 
 MESH = pl.DeviceIdType.MESH
+TILE = 256
+EARLY = 3
 
 
 class Place:
@@ -197,7 +193,7 @@
     def same(self, i):
         kind = 2 * (self.p.n - 1)
         return remote(
-            self.owns[i], self.fulls[i].at[self.p.me], self.ssem.at[i, kind], self.rsem.at[i, kind], self.p.sib
+            self.owns[i], self.fulls[i].at[self.p.me], self.ssem[i].at[kind], self.rsem[i].at[kind], self.p.sib
         )
 
     def direct(self, i, kind, target):
@@ -205,15 +201,15 @@
         return remote(
             self.owns[i].at[p.core],
             self.fulls[i].at[p.me, p.core],
-            self.ssem.at[i, kind],
-            self.rsem.at[i, kind],
+            self.ssem[i].at[kind],
+            self.rsem[i].at[kind],
             (p.rep, target),
         )
 
     def onward(self, i, kind, block, device):
         p = self.p
         view = self.fulls[i].at[block, p.core]
-        return remote(view, view, self.ssem.at[i, kind], self.rsem.at[i, kind], device)
+        return remote(view, view, self.ssem[i].at[kind], self.rsem[i].at[kind], device)
 
     def start(self, i):
         p = self.p
@@ -547,10 +543,11 @@
 
 
 def feed_kernel(n, reps, half, tile, *refs):
-    (b_ref, e_ref, x_ref, gain_ref, wg_ref, wu_ref, wd_ref) = refs[:7]
-    res_out, dx_out, dm_out, norm_ref, down_out, gate_out, up_out = refs[7:14]
-    bt, acc, hid, dgate, dup, both, other, group, ring, ssem, rsem, lsem = refs[14:26]
-    xs, res_ref, dx_ref, dm_ref, down_ref, moved = refs[26:]
+    b_ref, e_ref, x_ref, gain_ref, wd_ref = refs[:5]
+    first, owns = refs[5:7], refs[7:9]
+    res_out, dx_out, dm_out, norm_ref, down_out, gate_out, up_out, *late = refs[9:18]
+    bt, acc, hid, dgate, dup, both, other, group, ring, ssem, rsem, lsem = refs[18:30]
+    xs, res_ref, dx_ref, dm_ref, down_ref, moved, gsend, grecv, wbuf, wsem = refs[30:]
     step, tiles = pl.program_id(0), pl.num_programs(0) - 1
     p = Place(n, reps)
     total = b_ref.shape[0]
@@ -562,6 +559,40 @@
 
     def write(k, ref, out, rows):
         return pltpu.make_async_copy(ref.at[rows], out.at[rows], moved.at[k])
+
+    def tile_gather(j):
+        at = pl.ds(pl.multiple_of(j * tile, tile), tile)
+        to = pl.ds(pl.multiple_of((j - EARLY) * tile, tile), tile)
+        return Gather(
+            p,
+            [own.at[:, :, at] for own in owns],
+            [full.at[:, :, :, to] for full in late],
+            [[sem.at[j - EARLY, i] for i in range(2)] for sem in (gsend, grecv)],
+        )
+
+    def weights(j, begin):
+        buf = lax.rem(j, 2)
+
+        def one(source, at):
+            for i in range(2):
+                c = pltpu.make_async_copy(
+                    source[i].at[:, :, :, pl.ds(pl.multiple_of(at * tile, tile), tile)], wbuf.at[buf, i], wsem.at[buf, i]
+                )
+                c.start() if begin else c.wait()
+
+        @pl.when(j < EARLY)
+        def _():
+            one(first, j)
+
+        @pl.when(j >= EARLY)
+        def _():
+            one(late, j - EARLY)
+
+    def ahead(lead, run):
+        @pl.when((step + lead >= EARLY) & (step + lead < tiles))
+        def _():
+            for i in range(2):
+                run(tile_gather(step + lead), i)
 
     def item(j):
         cols = pl.ds(pl.multiple_of(j * tile, tile), tile)
@@ -589,6 +620,10 @@
     def _():
         greet(Reduce.peers(p))
         fetch().start()
+        weights(0, True)
+        for j in range(EARLY, min(EARLY + 1, tiles)):
+            for i in range(2):
+                tile_gather(j).start(i)
         acc[...] = jnp.zeros_like(acc)
         dx_ref[...] = jnp.zeros_like(dx_ref)
 
@@ -601,11 +636,16 @@
 
     @pl.when(step < tiles)
     def _():
+        ahead(EARLY + 1, lambda g, i: g.start(i))
+        weights(step, False)
+        wg = wbuf[lax.rem(step, 2), 0].reshape(-1, tile)
+        wu = wbuf[lax.rem(step, 2), 1].reshape(-1, tile)
+
         def rows_step(j, _):
             rows = rows_at(j, 512)
             b, e = b_ref[rows, :], e_ref[rows, :]
-            gate = dot(b, wg_ref[...])
-            up = dot(b, wu_ref[...])
+            gate = dot(b, wg)
+            up = dot(b, wu)
             dh = dot_nt(e, wd_ref[...])
             sig = jax.nn.sigmoid(gate)
             swish = gate * sig
@@ -621,10 +661,18 @@
         def sums_step(j, _):
             rows = rows_at(j, 512)
             acc[rows, :] += dot(hid[rows, :], wd_ref[...])
-            dx_ref[rows, :] += dot_nt(dgate[rows, :], wg_ref[...]) + dot_nt(dup[rows, :], wu_ref[...])
+            dx_ref[rows, :] += dot_nt(dgate[rows, :], wg) + dot_nt(dup[rows, :], wu)
             return 0
 
         lax.fori_loop(0, total // 512, rows_step, 0)
+
+        ahead(EARLY, lambda g, i: g.relay(i))
+        ahead(EARLY - 1, lambda g, i: g.pass_on(i))
+        ahead(1, lambda g, i: g.done(i))
+
+        @pl.when(step + 1 < tiles)
+        def _():
+            weights(step + 1, True)
 
         @pl.when(step > 0)
         def _():
@@ -650,7 +698,7 @@
             xn = x * inv
             db = dx_ref[rows, :]
             norm_ref[...] += jnp.sum(db * xn, axis=0, keepdims=True)
-            dbg = db * gain_ref[...]
+            dbg = db * gain_ref[1:2, :]
             dx = e_ref[rows, :].astype(F32) + inv * (dbg - xn * jnp.mean(dbg * xn, axis=-1, keepdims=True))
             dx_ref[rows, :] = dx
             dm_ref[rows, :] = dx.astype(BF)
@@ -694,21 +742,21 @@
             c.wait()
 
 
-def feed(n, reps, b, e, x2, gain, wg, wu, wd):
+def feed(n, reps, b, e, x2, gain, wd, first, owns):
     total, width = b.shape
-    ff = wg.shape[1]
-    tile, z = 256, reps // 2
+    owns = [halves(w) for w in owns]
+    ff = wd.shape[0]
+    tile, z = TILE, reps // 2
     tiles, half = ff // tile, width // (2 * n)
     once = lambda *sh: pl.BlockSpec(sh, lambda j: (0,) * len(sh), pipeline_mode=pl.Buffered(1))
-    col = lambda: pl.BlockSpec((width, tile), lambda j: (0, jnp.minimum(j, tiles - 1)))
     row = lambda: pl.BlockSpec((tile, width), lambda j: (jnp.minimum(j, tiles - 1), 0))
     anywhere = pl.BlockSpec(memory_space=pl.ANY)
     sd = jax.ShapeDtypeStruct
     return pl.pallas_call(
         functools.partial(feed_kernel, n, reps, half, tile),
         grid=(tiles + 1,),
-        in_specs=[once(total, width)] * 2 + [anywhere, once(1, width), col(), col(), row()],
-        out_specs=[anywhere] * 3 + [once(1, width), anywhere, anywhere, anywhere],
+        in_specs=[once(total, width)] * 2 + [anywhere, once(8, width), row()] + [anywhere] * 4,
+        out_specs=[anywhere] * 3 + [once(1, width)] + [anywhere] * 5,
         out_shape=[
             sd((total, width), BF),
             sd((total, width), F32),
@@ -717,6 +765,8 @@
             sd((ff, total), BF),
             sd((2, half, ff), BF),
             sd((2, half, ff), BF),
+            sd((n, 2, half, ff - EARLY * tile), BF),
+            sd((n, 2, half, ff - EARLY * tile), BF),
         ],
         scratch_shapes=[
             pltpu.VMEM((width, total), BF),
@@ -734,24 +784,32 @@
             pltpu.VMEM((total, width), BF),
             pltpu.VMEM((ff, total), BF),
             pltpu.SemaphoreType.DMA((8,)),
+            pltpu.SemaphoreType.DMA((tiles - EARLY, 2, 2 * (n - 1) + 1)),
+            pltpu.SemaphoreType.DMA((tiles - EARLY, 2, 2 * (n - 1) + 1)),
+            pltpu.VMEM((2, 2, n, 2, half, tile), BF),
+            pltpu.SemaphoreType.DMA((2, 2)),
         ],
         compiler_params=pltpu.CompilerParams(collective_id=1, has_side_effects=True, vmem_limit_bytes=63 << 20),
         name="feed_forward",
-    )(b, e, x2, gain, wg, wu, wd)
+    )(b, e, x2, gain, wd, *first, *owns)[:7]
 
 
 def forward_kernel(n, reps, width, *refs):
-    x_ref, cols_ref, segr_ref, m_ref, vec_ref, high_ref, low_ref = refs[:7]
-    owns = refs[7:15]
-    a_ref, q_ref, k_ref, v_ref, g_ref, r_ref, y_ref, o_ref, st_ref = refs[15:24]
-    x2_ref, b_ref, vec_out, high_out, low_out = refs[24:29]
-    outs = refs[29:37]
-    state, esc, xs, ys, vecs, highs, lows = refs[37:44]
-    kept = refs[44:49]
-    small_send, small_recv, ssem, rsem, lsem = refs[49:]
+    x_ref, segr_ref, m_ref, vec_ref, high_ref, low_ref = refs[:6]
+    owns = refs[6:14]
+    a_ref, q_ref, k_ref, v_ref, g_ref, r_ref, y_ref, o_ref, st_ref = refs[14:23]
+    x2_ref, b_ref, vec_out, high_out, low_out = refs[23:28]
+    outs = refs[28:36]
+    state, esc, xs, ys, vecs, highs, lows = refs[36:43]
+    kept = refs[43:48]
+    small_send, small_recv, ssem, rsem, lsem = refs[48:]
     step, nc = pl.program_id(0), pl.num_programs(0) - 1
     p = Place(n, reps)
-    gather = Gather(p, owns, list(kept) + list(outs[5:]), [ssem, rsem])
+    early = outs[6].shape[3]
+    owns = list(owns[:6]) + [own.at[:, :, 0:early] for own in owns[6:]]
+    gather = Gather(
+        p, owns, list(kept) + list(outs[5:]), [[sem.at[i] for i in range(8)] for sem in (ssem, rsem)]
+    )
     smalls = [(vec_ref, vecs), (high_ref, highs), (low_ref, lows)]
 
     def small(k, j):
@@ -782,11 +840,12 @@
         for k in range(3):
             for j in range(1, n):
                 small(k, j).wait()
-        rs = low_ref.shape[0]
+        rs = low_ref.shape[1]
         for s in range(n):
             at = slice(s * rs, (s + 1) * rs)
-            vec_out[0:2, at] = vecs[s, 0:2, 0:rs]
-            low_out[at, :] = lows[s]
+            vec_out[0:1, at] = vecs[s, :, 0:rs]
+            vec_out[1:2, at] = vecs[s, :, rs : 2 * rs]
+            low_out[:, at] = lows[s]
 
         def spread(part, out_width):
             own = part(0).shape[1]
@@ -799,8 +858,8 @@
             return total
 
         nb, ng = 512 // n, VH // n
-        vec_out[2:3, 0:512] = spread(lambda s: vecs[s, 2:3, 0:nb].astype(BF), 512)
-        vec_out[3:4, 0:VH] = spread(lambda s: vecs[s, 3:4, 0:ng].astype(BF), VH)
+        vec_out[2:3, 0:512] = spread(lambda s: vecs[s, :, 2 * rs : 2 * rs + nb].astype(BF), 512)
+        vec_out[3:4, 0:VH] = spread(lambda s: vecs[s, :, -128:][:, 0:ng].astype(BF), VH)
         high_out[...] = spread(lambda s: highs[s], 512).astype(BF)
         for i in range(4):
             gather.pass_on(i)
@@ -822,10 +881,10 @@
         k_ref[...] = dot(a, whole(1)).astype(BF)
         v_ref[...] = dot(a, whole(2)).astype(BF)
         g_ref[...] = dot(a, whole(3)).astype(BF)
-        r_ref[...] = dot(a, low_out[...]).astype(BF)
+        r_ref[...] = dot_nt(a, low_out[...]).astype(BF)
         fwd_chunk(
             step, q_ref, k_ref, v_ref, g_ref, r_ref, high_out, vec_out.at[2:3, 0:512], vec_out.at[3:4, 0:VH],
-            cols_ref, segr_ref, m_ref, y_ref, o_ref, st_ref, state, esc,
+            segr_ref, m_ref, y_ref, o_ref, st_ref, state, esc,
         )
         ys[rows, :] = y_ref[...]
 
@@ -863,7 +922,7 @@
             keep(i).wait()
 
 
-def forward(n, reps, x, cols, segr, vec, high, low, weights):
+def forward(n, reps, x, segr, vec, high, low, weights):
     T, width = x.shape
     nc = T // C
     M = jnp.asarray(level_sums(), BF)
@@ -874,16 +933,16 @@
     full = lambda *sh: pl.BlockSpec(sh, lambda i: (0,) * len(sh), pipeline_mode=pl.Buffered(1))
     anywhere = pl.BlockSpec(memory_space=pl.ANY)
     sd = jax.ShapeDtypeStruct
-    shapes = [(n,) + o.shape for o in owns]
+    shapes = [(n,) + o.shape for o in owns[:6]] + [(n,) + o.shape[:2] + (EARLY * TILE,) for o in owns[6:]]
     kinds = 2 * (n - 1) + 1
     res = pl.pallas_call(
         functools.partial(forward_kernel, n, reps, width),
         grid=(nc + 1,),
-        in_specs=[blk(width), blk(2), full(nc, 1, C), full(nr, C), full(*vec.shape), full(*high.shape), full(*low.shape)]
+        in_specs=[blk(width), full(nc, 1, C), full(nr, C), full(*vec.shape), full(*high.shape), full(*low.shape)]
         + [anywhere] * 8,
         out_specs=[blk(w) for w in (width, 512, 512, 1024, 1024, 16, 1024, 1024)]
         + [pl.BlockSpec((1, HEADS, VH, KH), lambda i: (last(i), 0, 0, 0))]
-        + [full(T, width), full(T, width), full(8, width), full(16, 512), full(width, 16)]
+        + [full(T, width), full(T, width), full(8, width), full(16, 512), full(16, width)]
         + [anywhere] * 8,
         out_shape=[sd((T, w), BF) for w in (width, 512, 512, 1024, 1024, 16, 1024, 1024)]
         + [
@@ -892,7 +951,7 @@
             sd((T, width), BF),
             sd((8, width), F32),
             sd((16, 512), BF),
-            sd((width, 16), BF),
+            sd((16, width), BF),
         ]
         + [sd(shape, BF) for shape in shapes],
         scratch_shapes=[
@@ -914,19 +973,20 @@
         ],
         compiler_params=pltpu.CompilerParams(collective_id=0, has_side_effects=True, vmem_limit_bytes=60 << 20),
         name="gla_fwd_gather",
-    )(x, cols, segr, M, vec, high, low, *owns)
-    return res[:14], [o.reshape(-1, o.shape[-1]) for o in res[14:]]
+    )(x, segr, M, vec, high, low, *owns)
+    return res[:14], [o.reshape(-1, o.shape[-1]) for o in res[14:20]] + list(res[20:])
 
 
 def backward_kernel(n,reps,plan,half,*refs):
-    (q_ref,k_ref,v_ref,g_ref,r_ref,o_ref,st_ref,dy_ref,a_ref,x_ref,dx_ref,cols_ref,
-     wh_ref,bias_ref,gain_ref,gmix_ref,nmlp_ref,segr_ref,m_ref,wq_ref,wk_ref,wv_ref,wg_ref,wl_ref)=refs[:24]
-    parts=refs[24:26]
-    gt_ref,small_ref=refs[26:28]
-    outs=refs[28:34]
-    dstate,rcar,esc,dcs,dall,at_ref,dz_ref,low_acc,high_acc,gb_ref,gg_ref,nmix_ref,smb,both=refs[34:48]
-    rest=refs[48:]
-    steps=pl.num_programs(0); step=pl.program_id(0); nc=steps-1
+    (q_ref,k_ref,v_ref,g_ref,r_ref,o_ref,st_ref,dy_ref,a_ref,x_ref,dx_ref,
+     wh_ref,vec_ref,nmlp_ref,segr_ref,m_ref,wq_ref,wk_ref,wv_ref,wg_ref,wl_ref)=refs[:21]
+    bias_ref,gain_ref=vec_ref.at[2:3,0:512],vec_ref.at[3:4,0:VH]
+    parts=refs[21:23]
+    gt_ref,small_ref=refs[23:25]
+    outs=refs[25:31]
+    dstate,rcar,esc,dcs,dall,at_ref,dz_ref,low_acc,high_acc,gb_ref,gg_ref,smb,both,drs=refs[31:45]
+    rest=refs[45:]
+    step=pl.program_id(0); nc=(pl.num_programs(0)-1)//2
     p=Place(n,reps)
     items=[]
     for which,at,width,source in plan:
@@ -944,83 +1004,93 @@
     ready=[it for it in items if it.part is not None]
     fresh=[it for it in items if it.part is None]
 
-    line=ready+[None]*(8-len(ready))+fresh
+    plan_at={}
+    def book(it,times):
+        for stage,t in enumerate(times): plan_at.setdefault(t,[]).append((stage,it))
+    for j,it in enumerate(ready): book(it,(j//2,2+j,4+j,6+j,7+j,8+j,9+j))
+    for j,it in enumerate(fresh): book(it,[8+j+s for s in range(Reduce.STAGES)])
+    last=max(plan_at)+1
 
     def slot(t):
-        for k in range(Reduce.STAGES):
-            if 0<=t-k<len(line) and line[t-k] is not None: line[t-k].stage(k)
+        for stage,it in sorted(plan_at.get(t,[]),key=lambda pair: pair[0]): it.stage(stage)
 
     @pl.when(step==0)
     def _():
         greet(Reduce.peers(p))
         for it in ready: it.start()
-        for ref in (dstate,rcar,gb_ref,gg_ref,low_acc,high_acc,nmix_ref,smb): ref[...]=jnp.zeros_like(ref)
+        for ref in (dstate,rcar,gb_ref,gg_ref,low_acc,high_acc,smb): ref[...]=jnp.zeros_like(ref)
 
     @pl.when(step<nc)
     def _():
         i=nc-1-step
         rows=pl.ds(pl.multiple_of(i*C,C),C)
-        bwd_chunk(i,q_ref,k_ref,v_ref,g_ref,r_ref,o_ref,st_ref,dy_ref,wh_ref,bias_ref,gain_ref,cols_ref,segr_ref,m_ref,
+        bwd_chunk(i,q_ref,k_ref,v_ref,g_ref,r_ref,o_ref,st_ref,dy_ref,wh_ref,bias_ref,gain_ref,segr_ref,m_ref,
                   dall.at[rows,0:512],dall.at[rows,512:1024],dall.at[rows,1024:2048],dall.at[rows,2048:3072],dz_ref,gb_ref,gg_ref,dstate,rcar,esc,dcs)
         dz=dz_ref[...]; a=a_ref[...]
         dr=dot_nt(dz,wh_ref[...]).astype(BF)
+        drs[rows,:]=dr
         high_acc[...]+=dot_tn(r_ref[...],dz)
         low_acc[...]+=dot_tn(dr,a)
         at_ref[:,rows]=jnp.transpose(a)
+
+    @pl.when(step>nc)
+    def _():
+        rows=pl.ds(pl.multiple_of((step-nc-1)*C,C),C)
         da=dot_nt(dall[rows,0:512],wq_ref[...])+dot_nt(dall[rows,512:1024],wk_ref[...])
-        da=da+dot_nt(dall[rows,1024:2048],wv_ref[...])+dot_nt(dall[rows,2048:3072],wg_ref[...])+dot_nt(dr,wl_ref[...])
+        da=da+dot_nt(dall[rows,1024:2048],wv_ref[...])+dot_nt(dall[rows,2048:3072],wg_ref[...])+dot(drs[rows,:],wl_ref[...])
         x=x_ref[...].astype(F32)
         n1=lax.rsqrt(jnp.mean(x*x,axis=-1,keepdims=True)+1e-5)
         xn=x*n1
-        nmix_ref[...]+=jnp.sum(da*xn,axis=0,keepdims=True)
-        dm=da*gmix_ref[...]
+        dm=da*vec_ref[0:1,:]
         gt_ref[...]=dx_ref[...]+n1*(dm-xn*jnp.mean(dm*xn,axis=-1,keepdims=True))
 
     for t in range(8):
         @pl.when(step==t)
         def _(): slot(t)
 
+    rs=2*half
+
     @pl.when(step==nc)
     def _():
-        rs=2*half
+        def product(at,width):
+            cols=slice(at,at+width)
+            w=dot(at_ref[...],dall[:,cols]).astype(BF)
+            for s in range(n):
+                both[p.core,s,:,cols]=w[s*rs:s*rs+half]
+                both[1-p.core,s,:,cols]=w[s*rs+half:(s+1)*rs]
+
         smb[:,16:32,:]=jnp.broadcast_to(high_acc[...][None],(n,16,512))
         smb[:,32:33,:]=jnp.broadcast_to(gb_ref[...][None],(n,1,512))
         smb[:,33:34,0:256]=jnp.broadcast_to(gg_ref[...][None],(n,1,256))
         for s in range(n):
             at=slice(s*rs,(s+1)*rs)
             smb[s,0:16,0:rs]=low_acc[:,at]
-            smb[s,34:35,0:rs]=nmix_ref[:,at]
             smb[s,35:36,0:rs]=nmlp_ref[:,at]
-        small.swap().start()
-
-        def product(at,width):
-            cols=slice(at,at+width)
-            def one(s,_):
-                rows=pl.ds(pl.multiple_of(s*rs,rs),rs)
-                w=dot(at_ref[rows,:],dall[:,cols]).astype(BF)
-                both[p.core,s,:,cols]=w[:half]
-                both[1-p.core,s,:,cols]=w[half:]
-                return 0
-            lax.fori_loop(0,n,one,0)
-
-        t=8; f=0
-        for at,width,count in ((2048,1024,2),(1024,1024,2),(0,1024,2)):
-            product(at,width)
-            for it in fresh[f:f+count]: it.start()
-            f+=count
-            slot(t); t+=1
-            small.stage((t-9))
-        last=len(line)+Reduce.STAGES-1
-        while t<last:
-            slot(t); t+=1
+        for j,at in enumerate((2048,2560,1024,1536,0,512)):
+            product(at,512)
+            fresh[j].start()
+            if j==1: small.swap().start()
+            if j%2==1: slot(8+j//2)
+            if j==5: small.stage(0)
+
+    for t in range(11,19):
+        @pl.when(step==t-11+nc+1)
+        def _():
+            slot(t)
+            if t in (13,16): small.stage((t-10)//3)
+
+    @pl.when(step==2*nc)
+    def _():
+        for t in range(19,last): slot(t)
         for it in items: it.settle()
         small.settle()
 
-def backward(n,reps,q,k,v,g,r,o,st,dy,first,tokens,dx2,wh,bias,gain,gmix,nmlp,cols,segr,weights,partials):
+def backward(n,reps,q,k,v,g,r,o,st,dy,first,tokens,dx2,wh,vecs,nmlp,segr,weights,partials):
     T=q.shape[0]; nc=T//C; z=reps//2
     assert nc==8
     M=jnp.asarray(level_sums(),BF); nr=M.shape[0]
     blk=lambda w: pl.BlockSpec((C,w),lambda i:(jnp.maximum(nc-1-i,0),0))
+    late=lambda w: pl.BlockSpec((C,w),lambda i:(jnp.clip(i-nc-1,0,nc-1),0))
     full=lambda *sh: pl.BlockSpec(sh,lambda i:(0,)*len(sh),pipeline_mode=pl.Buffered(1))
     sd=jax.ShapeDtypeStruct
     anywhere=pl.BlockSpec(memory_space=pl.ANY)
@@ -1036,19 +1106,19 @@
         plan.append((which,at,width,source)); scratch+=Reduce.scratch(n,z,half,width,False)
     scratch+=Small.scratch(n,z,40,512)
     out=lambda h,w: sd((2,h,w),BF)
-    res=pl.pallas_call(functools.partial(backward_kernel,n,reps,tuple(plan),half),grid=(nc+1,),
+    res=pl.pallas_call(functools.partial(backward_kernel,n,reps,tuple(plan),half),grid=(2*nc+1,),
         in_specs=[blk(512),blk(512),blk(1024),blk(1024),blk(16),blk(1024),pl.BlockSpec((1,HEADS,VH,KH),lambda i:(jnp.maximum(nc-1-i,0),0,0,0)),blk(1024),
-                  blk(1024),blk(1024),blk(1024),blk(2),
-                  full(16,512),full(1,512),full(1,256),full(1,1024),full(1,1024),full(nc,1,C),full(nr,C),
-                  full(1024,512),full(1024,512),full(1024,1024),full(1024,1024),full(1024,16)]+[anywhere]*2,
-        out_specs=[blk(1024),pl.BlockSpec((40,512),lambda i:(0,0))]+[anywhere]*6,
+                  blk(1024),late(1024),late(1024),
+                  full(16,512),full(8,1024),full(1,1024),full(nc,1,C),full(nr,C),
+                  full(1024,512),full(1024,512),full(1024,1024),full(1024,1024),full(16,1024)]+[anywhere]*2,
+        out_specs=[late(1024),pl.BlockSpec((40,512),lambda i:(0,0))]+[anywhere]*6,
         out_shape=[sd((T,1024),F32),sd((40,512),F32)]+[out(q.shape[2],q.shape[3]) for q in pairs]+[out(half,512),out(half,512),out(half,1024),out(half,1024)],
         scratch_shapes=[pltpu.VMEM((HEADS,VH,KH),F32),pltpu.VMEM((1,512),F32),pltpu.VMEM((nr,512),F32),pltpu.VMEM((C,1024),BF),
                         pltpu.VMEM((T,3072),BF),pltpu.VMEM((1024,T),BF),pltpu.VMEM((C,512),BF),pltpu.VMEM((16,1024),F32),pltpu.VMEM((16,512),F32),
-                        pltpu.VMEM((1,512),F32),pltpu.VMEM((1,256),F32),pltpu.VMEM((1,1024),F32),pltpu.VMEM((n,40,512),F32),
-                        pltpu.VMEM((2,n,half,3072),BF)]+scratch,
+                        pltpu.VMEM((1,512),F32),pltpu.VMEM((1,256),F32),pltpu.VMEM((n,40,512),F32),
+                        pltpu.VMEM((2,n,half,3072),BF),pltpu.VMEM((T,16),BF)]+scratch,
         compiler_params=pltpu.CompilerParams(collective_id=2,has_side_effects=True,vmem_limit_bytes=63<<20),
-        name="gla_bwd_reduce")(q,k,v,g,r,o,st,dy,first,tokens,dx2,cols,wh,bias,gain,gmix,nmlp,segr,M,*weights,*pairs)
+        name="gla_bwd_reduce")(q,k,v,g,r,o,st,dy,first,tokens,dx2,wh,vecs,nmlp,segr,M,*weights,*pairs)
     return res[0],res[1],[x.reshape(-1,x.shape[2]) for x in res[2:]]
 
 
@@ -1079,28 +1149,26 @@
 ):
     total = tokens.shape[0] * tokens.shape[1]
     width = tokens.shape[2]
-    cols, segr = seg_views(segments)
-    wide = max(norm_mix.shape[0], 128)
-    rows = [jnp.pad(v.astype(F32), (0, wide - v.shape[0])) for v in (norm_mix, norm_mlp, decay_bias, head_gain)]
-    vec = jnp.concatenate([jnp.stack(rows), jnp.zeros((4, wide), F32)])
+    segr = seg_rows(segments)
+    pads = [-v.shape[0] % 128 for v in (decay_bias, head_gain)]
+    zeros = [jnp.zeros((pad,), BF) for pad in pads]
+    vec = jnp.concatenate([norm_mix, norm_mlp, decay_bias, zeros[0], head_gain, zeros[1]]).astype(F32)[None]
     (
         (first, query, keys, values, outgate, lowrank, mixed, heads, states, resid, second, vecs, high_w, low_w),
-        (query_w, key_w, value_w, outgate_w, out_w, gate_w, up_w, down_w),
+        (query_w, key_w, value_w, outgate_w, out_w, down_w, gate_w, up_w),
     ) = forward(
         shards,
         reps,
         tokens.reshape(total, width),
-        cols,
         segr,
         vec,
         w_high,
-        w_low,
-        (w_query, w_key, w_value, w_outgate, w_out, w_gate, w_up, w_down),
+        w_low.T,
+        (w_query, w_key, w_value, w_outgate, w_out, w_down, w_gate, w_up),
     )
-    gain_mix, gain_feed, bias, gain_head = vecs[0:1], vecs[1:2], vecs[2:3, :512], vecs[3:4, :VH]
     grad_out = cotangent.reshape(total, width)
     result, grad_resid, branch, part_norm_mlp, part_down, sum_gate, sum_up = feed(
-        shards, reps, second, grad_out, resid, gain_feed, gate_w, up_w, down_w
+        shards, reps, second, grad_out, resid, vecs, down_w, (gate_w, up_w), (w_gate, w_up)
     )
     part_out = dot_tn(mixed, branch)
     grad_mixed = dot_nt(branch, out_w).astype(BF)
@@ -1119,11 +1187,8 @@
         tokens.reshape(total, width),
         grad_resid,
         high_w,
-        bias,
-        gain_head,
-        gain_mix,
+        vecs,
         part_norm_mlp,
-        cols,
         segr,
         (query_w, key_w, value_w, outgate_w, low_w),
         (part_down, part_out.astype(BF)),
@@ -1136,12 +1201,20 @@
     def across(block, width):
         return lax.dynamic_slice_in_dim(block, me * width, width, axis=1)
 
+    grad_low_w = small_sums[:16, :rs].T
+    mixer = (
+        (w_query, sum_query),
+        (w_key, sum_key),
+        (w_value, sum_value),
+        (w_outgate, sum_outgate),
+        (w_low, grad_low_w),
+    )
     own = (
-        small_sums[34, :rs],
+        sum(jnp.sum(w.astype(F32) * g, axis=1) for w, g in mixer) / norm_mix.astype(F32),
         small_sums[35, :rs],
         across(small_sums[32:33], decay_bias.shape[0]).reshape(-1),
         across(small_sums[33:34, :VH], head_gain.shape[0]).reshape(-1),
-        small_sums[:16, :rs].T,
+        grad_low_w,
         across(small_sums[16:32], w_high.shape[1]),
     )
     return (

time: 402 us -> 360 us (0.90)
  Pallas kernels: 357 us -> 328 us
  local copies, waits for them, and re-layouts: 18.7 us -> 9.38 us
    pallas_call x1, Pallas kernels: 139 us -> 101 us  [forward(): pl.pallas_call(functools.partial(forward_kernel, n, reps, width), grid=(n...]
    pallas_call x1, Pallas kernels: 102 us -> 118 us  [feed(): pl.pallas_call(functools.partial(feed_kernel, n, reps, half, tile), grid=...]
    pallas_call x1, Pallas kernels: 116 us -> 109 us  [backward(): pl.pallas_call(functools.partial(backward_kernel, n, reps, tuple(plan), h...]
    convert_element_type x4 -> x2, other arithmetic: 8.03 us -> 3.15 us  [local(): s.astype(F32)]
    reduce_sum x0 -> x3, other arithmetic: none -> 4.47 us  [local(): jnp.sum(w.astype(F32) * g, axis=1)]
where the time goes in v4:
time: 360 us; the launch traced here: 359 us
  Pallas kernels  328 us (91%)
  other arithmetic  13.7 us (4%)
  local copies, waits for them, and re-layouts  9.38 us (3%)
  matrix products  7.46 us (2%)
    pallas_call x1, Pallas kernels, feed(): pl.pallas_call(functools.partial(feed_kernel, n, reps, half, tile), grid=...  118 us
    pallas_call x1, Pallas kernels, backward(): pl.pallas_call(functools.partial(backward_kernel, n, reps, tuple(plan), h...  109 us
    pallas_call x1, Pallas kernels, forward(): pl.pallas_call(functools.partial(forward_kernel, n, reps, width), grid=(n...  101 us

profile of v4, /device:TPU:1, one launch (start us, length us, event | category | flops | bytes accessed | tf_op | source)
XLA Modules:
  0.0 359.3 jit_solution(6488377475935680240)
XLA Ops:
  0.6 0.7 concatenate.18
  1.3 0.7 concatenate.19
  2.0 0.8 concatenate.22
  2.7 0.6 convert_element_type.82.refs_3_
  3.3 101.1 %gla_fwd_gather.1 = (bf16[1024,1024]{1,0:T(8,128)(2,1)}, bf16[1024,512]{1,0:T(8,128)(2,1)}, bf16[1024,512]{1,0:T(8,128)(2,1)}, bf16[1024,1024]{1,0:T(8,128)(2,1)...) custom-call(bf16[1024,1024]{1,0:T(8,128)(2,1)} %bitcast.64, ...), custom_call_target="tpu_custom_call" | custom-call | tf_op jit(solution)/shard_map/gla_fwd_gather/pallas_call | solution.py:938
  104.4 118.2 %feed_forward.1 = (bf16[1024,1024]{1,0:T(8,128)(2,1)}, f32[1024,1024]{1,0:T(8,128)}, bf16[1024,1024]{1,0:T(8,128)(2,1)}, f32[1,1024]{1,0:T(1,128)}, bf16[2816,10...) custom-call(bf16[1024,1024]{1,0:T(8,128)(2,1)} %get-tuple-element.53, ...), custom_call_target="tpu_custom_call" | custom-call | tf_op jit(solution)/shard_map/feed_forward/pallas_call | solution.py:755
  222.7 0.0 copy-start.14
  222.7 0.0 copy-start.15
  222.7 4.9 %bitcast_convert_fusion.1 = (f32[256,2816]{1,0:T(8,128)}, f32[256,2816]{1,0:T(8,128)}) fusion(bf16[2,128,2816]{2,1,0:T(8,128)(2,1)} %get-tuple-element.88, bf16[2,128,2816]{2,1,0:T(8,128)(2,1)} %get-tuple-element.87), kind=kLoop, calls=%fused_computation.3 | loop fusion | flops 1441792 | bytes 8650752 | tf_op jit(solution)/shard_map/convert_element_type | solution.py:1196
  227.6 0.0 copy-done.14
  227.6 0.0 copy-done.15
  227.6 0.0 copy-start.13
  227.6 3.8 %convolution_convert_fusion = bf16[1024,1024]{1,0:T(8,128)(2,1)} fusion(bf16[1024,1024]{1,0:T(8,128)(2,1)S(1)} %copy-done.14, bf16[1024,1024]{1,0:T(8,128)(2,1)S(1)} %copy-done.15), kind=kOutput, calls=%fused_computation | convolution fusion | flops 2148532224 | bytes 6291456 | tf_op jit(solution)/shard_map/dot_general | solution.py:25
  231.3 0.0 copy-done.13
  231.3 3.7 %convolution_convert_fusion.1.refs_7_ = bf16[1024,1024]{1,0:T(8,128)(2,1)} fusion(bf16[1024,1024]{1,0:T(8,128)(2,1)S(1)} %copy-done.15, bf16[1024,1024]{1,0:T(8,128)(2,1)S(1)} %bitcast.92), kind=kOutput, calls=%fused_computation.1 | convolution fusion | flops 2148532224 | bytes 6291456 | tf_op jit(solution)/shard_map/dot_general | solution.py:24
  235.0 0.0 copy-start.5
  235.0 0.0 copy-start.6
  235.0 108.6 %gla_bwd_reduce.1 = (f32[1024,1024]{1,0:T(8,128)}, f32[40,512]{1,0:T(8,128)}, bf16[2,352,1024]{2,1,0:T(8,128)(2,1)}, bf16[2,128,1024]{2,1,0:T(8,128)(2,1)}, bf16...) custom-call(bf16[1024,512]{1,0:T(8,128)(2,1)} %get-tuple-element.60., ...), custom_call_target="tpu_custom_call" | custom-call | tf_op jit(solution)/shard_map/gla_bwd_reduce/pallas_call | solution.py:1109
  343.7 0.0 copy-start.2
  343.7 0.0 copy-start.3
  343.7 0.0 copy-start.8
  343.7 0.0 copy-start.9
  343.7 0.0 copy-done.5
  343.8 0.0 copy-done.6
  343.8 2.3 multiply_reduce_fusion.2
  346.0 0.0 copy-done.2
  346.0 0.0 copy-done.3
  346.0 0.0 copy-done.8
  346.0 0.0 copy-done.9
  346.0 0.0 copy-start.10
  346.0 0.0 copy-start.11
  346.1 0.0 copy-start.12
  346.1 0.0 copy-start.4
  346.1 1.6 multiply_reduce_fusion
  347.7 0.0 copy-done.10
  347.7 0.0 copy-done.11
  347.7 0.6 multiply_reduce_fusion.4
  348.3 0.0 copy-done.12
  348.3 0.6 convert_divide_fusion
  348.9 0.0 copy-done.4
  348.9 0.0 copy-start.7
  348.9 0.0 copy-start.1
  348.9 2.0 bitcast_convert_fusion
  350.9 0.0 copy-done.7
  350.9 1.1 bitcast_convert_fusion.3
  352.0 0.6 constant_dynamic-slice_fusion.2
  352.6 0.6 fusion.2
  353.2 0.6 fusion.1
  353.8 0.5 fusion
  354.3 0.0 copy-done.1
  354.3 0.0 copy-start
  354.3 1.3 copy.37
  355.6 1.6 copy-done
  357.3 2.0 copy.38
  (3 shorter events, 0.0 us)
Async XLA Ops:
  222.7 4.9 %copy-start.14 = (bf16[1024,1024]{1,0:T(8,128)(2,1)S(1)}, bf16[1024,1024]{1,0:T(8,128)(2,1)}, u32[]{:S(2)}) copy-start(bf16[1024,1024]{1,0:T(8,128)(2,1)} %get-tuple-element.79) | copy-start | bytes 6291460
  222.7 4.9 %copy-start.15 = (bf16[1024,1024]{1,0:T(8,128)(2,1)S(1)}, bf16[1024,1024]{1,0:T(8,128)(2,1)}, u32[]{:S(2)}) copy-start(bf16[1024,1024]{1,0:T(8,128)(2,1)} %get-tuple-element.67) | copy-start | bytes 6291460
  227.6 3.8 %copy-start.13 = (bf16[4,2,128,1024]{3,2,1,0:T(8,128)(2,1)S(1)}, bf16[4,2,128,1024]{3,2,1,0:T(8,128)(2,1)}, u32[]{:S(2)}) copy-start(bf16[4,2,128,1024]{3,2,1,0:T(8,128)(2,1)} %get-tuple-element.68) | copy-start | bytes 6291460
  235.0 108.7 %copy-start.5 = (bf16[256,512]{1,0:T(8,128)(2,1)S(1)}, bf16[256,512]{1,0:T(8,128)(2,1)}, u32[]{:S(2)}) copy-start(bf16[256,512]{1,0:T(8,128)(2,1)} %param.23) | copy-start | bytes 786436
  235.0 108.7 %copy-start.6 = (bf16[256,512]{1,0:T(8,128)(2,1)S(1)}, bf16[256,512]{1,0:T(8,128)(2,1)}, u32[]{:S(2)}) copy-start(bf16[256,512]{1,0:T(8,128)(2,1)} %param.24) | copy-start | bytes 786436
  343.7 2.3 copy-start.2
  343.7 2.3 copy-start.3
  343.7 2.3 copy-start.8
  343.7 2.3 copy-start.9
  346.0 1.7 copy-start.10
  346.0 1.6 copy-start.11
  346.1 2.2 copy-start.12
  346.1 2.8 copy-start.4
  348.9 2.0 copy-start.7
  348.9 5.4 %copy-start.1 = (bf16[1024,1024]{1,0:T(8,128)(2,1)S(1)}, bf16[1024,1024]{1,0:T(8,128)(2,1)}, u32[]{:S(2)}) copy-start(bf16[1024,1024]{1,0:T(8,128)(2,1)} %get-tuple-element.59) | copy-start | bytes 6291460
  354.3 2.9 copy-start

commit v5 on v4

--- a/solution.py
+++ b/solution.py
@@ -888,17 +888,18 @@
         )
         ys[rows, :] = y_ref[...]
 
-    @pl.when(step == 2)
-    def _():
-        gather.relay(4)
-
-    @pl.when(step == 4)
-    def _():
-        gather.pass_on(4)
+    for at, run in (
+        (1, lambda: gather.relay(4)),
+        (3, lambda: gather.pass_on(4)),
+        (4, lambda: gather.relay(5)),
+        (5, lambda: gather.relay(6)),
+        (6, lambda: gather.relay(7)),
+        (7, lambda: gather.pass_on(5)),
+    ):
+        pl.when(step == at)(run)
 
     @pl.when(step == nc)
     def _():
-        gather.relay(5)
         gather.done(4)
         keep(4).start()
 
@@ -911,10 +912,7 @@
             return 0
 
         lax.fori_loop(0, xs.shape[0] // 256, join, 0)
-        gather.pass_on(5)
-        gather.relay(6)
         gather.pass_on(6)
-        gather.relay(7)
         gather.pass_on(7)
         for i in range(5, 8):
             gather.done(i)

time: 360 us -> 346 us (0.961)
  Pallas kernels: 328 us -> 315 us
    pallas_call x1, Pallas kernels: 101 us -> 88.6 us  [forward(): pl.pallas_call(functools.partial(forward_kernel, n, reps, width), grid=(n...]
where the time goes in v5:
time: 346 us
  Pallas kernels  315 us (91%)
  other arithmetic  13.7 us (4%)
  local copies, waits for them, and re-layouts  9.38 us (3%)
  matrix products  7.46 us (2%)
    pallas_call x1, Pallas kernels, feed(): pl.pallas_call(functools.partial(feed_kernel, n, reps, half, tile), grid=...  118 us
    pallas_call x1, Pallas kernels, backward(): pl.pallas_call(functools.partial(backward_kernel, n, reps, tuple(plan), h...  108 us
    pallas_call x1, Pallas kernels, forward(): pl.pallas_call(functools.partial(forward_kernel, n, reps, width), grid=(n...  88.6 us

profile of v5, /device:TPU:1, one launch (start us, length us, event | category | flops | bytes accessed | tf_op | source)
XLA Modules:
  0.0 346.3 jit_solution(6050762899952588358)
XLA Ops:
  0.6 0.7 concatenate.18
  1.3 0.7 concatenate.19
  2.0 0.8 concatenate.22
  2.7 0.6 convert_element_type.82.refs_3_
  3.3 88.6 %gla_fwd_gather.1 = (bf16[1024,1024]{1,0:T(8,128)(2,1)}, bf16[1024,512]{1,0:T(8,128)(2,1)}, bf16[1024,512]{1,0:T(8,128)(2,1)}, bf16[1024,1024]{1,0:T(8,128)(2,1)...) custom-call(bf16[1024,1024]{1,0:T(8,128)(2,1)} %bitcast.64, ...), custom_call_target="tpu_custom_call" | custom-call | tf_op jit(solution)/shard_map/gla_fwd_gather/pallas_call | solution.py:936
  92.0 118.1 %feed_forward.1 = (bf16[1024,1024]{1,0:T(8,128)(2,1)}, f32[1024,1024]{1,0:T(8,128)}, bf16[1024,1024]{1,0:T(8,128)(2,1)}, f32[1,1024]{1,0:T(1,128)}, bf16[2816,10...) custom-call(bf16[1024,1024]{1,0:T(8,128)(2,1)} %get-tuple-element.53, ...), custom_call_target="tpu_custom_call" | custom-call | tf_op jit(solution)/shard_map/feed_forward/pallas_call | solution.py:755
  210.1 0.0 copy-start.14
  210.1 0.0 copy-start.15
  210.1 4.9 %bitcast_convert_fusion.1 = (f32[256,2816]{1,0:T(8,128)}, f32[256,2816]{1,0:T(8,128)}) fusion(bf16[2,128,2816]{2,1,0:T(8,128)(2,1)} %get-tuple-element.88, bf16[2,128,2816]{2,1,0:T(8,128)(2,1)} %get-tuple-element.87), kind=kLoop, calls=%fused_computation.3 | loop fusion | flops 1441792 | bytes 8650752 | tf_op jit(solution)/shard_map/convert_element_type | solution.py:1194
  215.0 0.0 copy-done.14
  215.0 0.0 copy-done.15
  215.0 0.0 copy-start.13
  215.0 3.8 %convolution_convert_fusion = bf16[1024,1024]{1,0:T(8,128)(2,1)} fusion(bf16[1024,1024]{1,0:T(8,128)(2,1)S(1)} %copy-done.14, bf16[1024,1024]{1,0:T(8,128)(2,1)S(1)} %copy-done.15), kind=kOutput, calls=%fused_computation | convolution fusion | flops 2148532224 | bytes 6291456 | tf_op jit(solution)/shard_map/dot_general | solution.py:25
  218.7 0.0 copy-done.13
  218.7 3.7 %convolution_convert_fusion.1.refs_7_ = bf16[1024,1024]{1,0:T(8,128)(2,1)} fusion(bf16[1024,1024]{1,0:T(8,128)(2,1)S(1)} %copy-done.15, bf16[1024,1024]{1,0:T(8,128)(2,1)S(1)} %bitcast.92), kind=kOutput, calls=%fused_computation.1 | convolution fusion | flops 2148532224 | bytes 6291456 | tf_op jit(solution)/shard_map/dot_general | solution.py:24
  222.4 0.0 copy-start.5
  222.4 0.0 copy-start.6
  222.4 108.3 %gla_bwd_reduce.1 = (f32[1024,1024]{1,0:T(8,128)}, f32[40,512]{1,0:T(8,128)}, bf16[2,352,1024]{2,1,0:T(8,128)(2,1)}, bf16[2,128,1024]{2,1,0:T(8,128)(2,1)}, bf16...) custom-call(bf16[1024,512]{1,0:T(8,128)(2,1)} %get-tuple-element.60., ...), custom_call_target="tpu_custom_call" | custom-call | tf_op jit(solution)/shard_map/gla_bwd_reduce/pallas_call | solution.py:1107
  330.7 0.0 copy-start.2
  330.7 0.0 copy-start.3
  330.7 0.0 copy-start.8
  330.7 0.0 copy-start.9
  330.7 0.0 copy-done.5
  330.8 0.0 copy-done.6
  330.8 2.3 multiply_reduce_fusion.2
  333.0 0.0 copy-done.2
  333.0 0.0 copy-done.3
  333.0 0.0 copy-done.8
  333.0 0.0 copy-done.9
  333.0 0.0 copy-start.10
  333.0 0.0 copy-start.11
  333.1 0.0 copy-start.12
  333.1 0.0 copy-start.4
  333.1 1.6 multiply_reduce_fusion
  334.7 0.0 copy-done.10
  334.7 0.0 copy-done.11
  334.7 0.6 multiply_reduce_fusion.4
  335.3 0.0 copy-done.12
  335.3 0.6 convert_divide_fusion
  335.9 0.0 copy-done.4
  335.9 0.0 copy-start.7
  335.9 0.0 copy-start.1
  335.9 2.0 bitcast_convert_fusion
  337.9 0.0 copy-done.7
  337.9 1.1 bitcast_convert_fusion.3
  339.0 0.6 constant_dynamic-slice_fusion.2
  339.6 0.6 fusion.2
  340.2 0.6 fusion.1
  340.8 0.5 fusion
  341.3 0.0 copy-done.1
  341.3 0.0 copy-start
  341.3 1.3 copy.37
  342.6 1.6 copy-done
  344.3 2.0 copy.38
  (3 shorter events, 0.0 us)
Async XLA Ops:
  210.1 4.9 %copy-start.14 = (bf16[1024,1024]{1,0:T(8,128)(2,1)S(1)}, bf16[1024,1024]{1,0:T(8,128)(2,1)}, u32[]{:S(2)}) copy-start(bf16[1024,1024]{1,0:T(8,128)(2,1)} %get-tuple-element.79) | copy-start | bytes 6291460
  210.1 4.9 %copy-start.15 = (bf16[1024,1024]{1,0:T(8,128)(2,1)S(1)}, bf16[1024,1024]{1,0:T(8,128)(2,1)}, u32[]{:S(2)}) copy-start(bf16[1024,1024]{1,0:T(8,128)(2,1)} %get-tuple-element.67) | copy-start | bytes 6291460
  215.0 3.8 %copy-start.13 = (bf16[4,2,128,1024]{3,2,1,0:T(8,128)(2,1)S(1)}, bf16[4,2,128,1024]{3,2,1,0:T(8,128)(2,1)}, u32[]{:S(2)}) copy-start(bf16[4,2,128,1024]{3,2,1,0:T(8,128)(2,1)} %get-tuple-element.68) | copy-start | bytes 6291460
  222.4 108.3 %copy-start.5 = (bf16[256,512]{1,0:T(8,128)(2,1)S(1)}, bf16[256,512]{1,0:T(8,128)(2,1)}, u32[]{:S(2)}) copy-start(bf16[256,512]{1,0:T(8,128)(2,1)} %param.23) | copy-start | bytes 786436
  222.4 108.3 %copy-start.6 = (bf16[256,512]{1,0:T(8,128)(2,1)S(1)}, bf16[256,512]{1,0:T(8,128)(2,1)}, u32[]{:S(2)}) copy-start(bf16[256,512]{1,0:T(8,128)(2,1)} %param.24) | copy-start | bytes 786436
  330.7 2.3 copy-start.2
  330.7 2.3 copy-start.3
  330.7 2.3 copy-start.8
  330.7 2.3 copy-start.9
  333.0 1.7 copy-start.10
  333.0 1.6 copy-start.11
  333.1 2.2 copy-start.12
  333.1 2.8 copy-start.4
  335.9 2.0 copy-start.7
  335.9 5.4 %copy-start.1 = (bf16[1024,1024]{1,0:T(8,128)(2,1)S(1)}, bf16[1024,1024]{1,0:T(8,128)(2,1)}, u32[]{:S(2)}) copy-start(bf16[1024,1024]{1,0:T(8,128)(2,1)} %get-tuple-element.59) | copy-start | bytes 6291460
  341.3 2.9 copy-start

commit v6 on v5

--- a/solution.py
+++ b/solution.py
@@ -136,6 +136,7 @@
 
 MESH = pl.DeviceIdType.MESH
 TILE = 256
+LEADS = (6, 3, 2)
 EARLY = 3
 
 
@@ -551,6 +552,7 @@
     step, tiles = pl.program_id(0), pl.num_programs(0) - 1
     p = Place(n, reps)
     total = b_ref.shape[0]
+    tiles_count = down_out.shape[0] // tile
     rs = 2 * half
     rows_at = lambda j, size: pl.ds(pl.multiple_of(j * size, size), size)
 
@@ -589,6 +591,14 @@
             one(late, j - EARLY)
 
     def ahead(lead, run):
+        if lead > EARLY:
+
+            @pl.when(step == 0)
+            def _():
+                for j in range(EARLY, min(lead, tiles_count)):
+                    for i in range(2):
+                        run(tile_gather(j), i)
+
         @pl.when((step + lead >= EARLY) & (step + lead < tiles))
         def _():
             for i in range(2):
@@ -612,18 +622,17 @@
     def slot(t):
         for k in range(Reduce.STAGES):
 
-            @pl.when((t >= k) & (t - k < tiles))
+            lag = k + (k > 0)
+
+            @pl.when((t >= lag) & (t - lag < tiles))
             def _():
-                item(t - k).stage(k)
+                item(t - lag).stage(k)
 
     @pl.when(step == 0)
     def _():
         greet(Reduce.peers(p))
         fetch().start()
         weights(0, True)
-        for j in range(EARLY, min(EARLY + 1, tiles)):
-            for i in range(2):
-                tile_gather(j).start(i)
         acc[...] = jnp.zeros_like(acc)
         dx_ref[...] = jnp.zeros_like(dx_ref)
 
@@ -636,7 +645,7 @@
 
     @pl.when(step < tiles)
     def _():
-        ahead(EARLY + 1, lambda g, i: g.start(i))
+        ahead(LEADS[0], lambda g, i: g.start(i))
         weights(step, False)
         wg = wbuf[lax.rem(step, 2), 0].reshape(-1, tile)
         wu = wbuf[lax.rem(step, 2), 1].reshape(-1, tile)
@@ -664,10 +673,10 @@
             dx_ref[rows, :] += dot_nt(dgate[rows, :], wg) + dot_nt(dup[rows, :], wu)
             return 0
 
-        lax.fori_loop(0, total // 512, rows_step, 0)
-
-        ahead(EARLY, lambda g, i: g.relay(i))
-        ahead(EARLY - 1, lambda g, i: g.pass_on(i))
+        lax.fori_loop(0, total // 512, rows_step, 0, unroll=True)
+
+        ahead(LEADS[1], lambda g, i: g.relay(i))
+        ahead(LEADS[2], lambda g, i: g.pass_on(i))
         ahead(1, lambda g, i: g.done(i))
 
         @pl.when(step + 1 < tiles)
@@ -684,7 +693,7 @@
                 both[step, p.core, s, :, at : at + tile] = w[s * rs : s * rs + half]
                 both[step, 1 - p.core, s, :, at : at + tile] = w[s * rs + half : (s + 1) * rs]
         item(step).start()
-        lax.fori_loop(0, total // 512, sums_step, 0)
+        lax.fori_loop(0, total // 512, sums_step, 0, unroll=True)
 
     @pl.when(step == tiles)
     def _():
@@ -729,7 +738,7 @@
             slot(t)
             return 0
 
-        lax.fori_loop(tiles + 4, tiles + Reduce.STAGES - 1, tail, 0)
+        lax.fori_loop(tiles + 4, tiles + Reduce.STAGES, tail, 0)
 
         def settle(j, _):
             item(j).settle()
@@ -977,13 +986,13 @@
 
 def backward_kernel(n,reps,plan,half,*refs):
     (q_ref,k_ref,v_ref,g_ref,r_ref,o_ref,st_ref,dy_ref,a_ref,x_ref,dx_ref,
-     wh_ref,vec_ref,nmlp_ref,segr_ref,m_ref,wq_ref,wk_ref,wv_ref,wg_ref,wl_ref)=refs[:21]
+     wh_ref,vec_ref,nmlp_ref,segr_ref,m_ref,*w_any,wl_ref)=refs[:21]
     bias_ref,gain_ref=vec_ref.at[2:3,0:512],vec_ref.at[3:4,0:VH]
     parts=refs[21:23]
     gt_ref,small_ref=refs[23:25]
     outs=refs[25:31]
-    dstate,rcar,esc,dcs,dall,at_ref,dz_ref,low_acc,high_acc,gb_ref,gg_ref,smb,both,drs=refs[31:45]
-    rest=refs[45:]
+    dstate,rcar,esc,dcs,dall,at_ref,dz_ref,low_acc,high_acc,gb_ref,gg_ref,smb,both,drs,*w_kept,w_sem=refs[31:50]
+    rest=refs[50:]
     step=pl.program_id(0); nc=(pl.num_programs(0)-1)//2
     p=Place(n,reps)
     items=[]
@@ -1012,9 +1021,13 @@
     def slot(t):
         for stage,it in sorted(plan_at.get(t,[]),key=lambda pair: pair[0]): it.stage(stage)
 
+    def weight(j):
+        return pltpu.make_async_copy(w_any[j],w_kept[j],w_sem.at[j])
+
     @pl.when(step==0)
     def _():
         greet(Reduce.peers(p))
+        for j in range(4): weight(j).start()
         for it in ready: it.start()
         for ref in (dstate,rcar,gb_ref,gg_ref,low_acc,high_acc,smb): ref[...]=jnp.zeros_like(ref)
 
@@ -1034,8 +1047,8 @@
     @pl.when(step>nc)
     def _():
         rows=pl.ds(pl.multiple_of((step-nc-1)*C,C),C)
-        da=dot_nt(dall[rows,0:512],wq_ref[...])+dot_nt(dall[rows,512:1024],wk_ref[...])
-        da=da+dot_nt(dall[rows,1024:2048],wv_ref[...])+dot_nt(dall[rows,2048:3072],wg_ref[...])+dot(drs[rows,:],wl_ref[...])
+        da=dot_nt(dall[rows,0:512],w_kept[0][...])+dot_nt(dall[rows,512:1024],w_kept[1][...])
+        da=da+dot_nt(dall[rows,1024:2048],w_kept[2][...])+dot_nt(dall[rows,2048:3072],w_kept[3][...])+dot(drs[rows,:],wl_ref[...])
         x=x_ref[...].astype(F32)
         n1=lax.rsqrt(jnp.mean(x*x,axis=-1,keepdims=True)+1e-5)
         xn=x*n1
@@ -1070,6 +1083,7 @@
             if j==1: small.swap().start()
             if j%2==1: slot(8+j//2)
             if j==5: small.stage(0)
+        for j in range(4): weight(j).wait()
 
     for t in range(11,19):
         @pl.when(step==t-11+nc+1)
@@ -1108,13 +1122,14 @@
         in_specs=[blk(512),blk(512),blk(1024),blk(1024),blk(16),blk(1024),pl.BlockSpec((1,HEADS,VH,KH),lambda i:(jnp.maximum(nc-1-i,0),0,0,0)),blk(1024),
                   blk(1024),late(1024),late(1024),
                   full(16,512),full(8,1024),full(1,1024),full(nc,1,C),full(nr,C),
-                  full(1024,512),full(1024,512),full(1024,1024),full(1024,1024),full(16,1024)]+[anywhere]*2,
+                  anywhere,anywhere,anywhere,anywhere,full(16,1024)]+[anywhere]*2,
         out_specs=[late(1024),pl.BlockSpec((40,512),lambda i:(0,0))]+[anywhere]*6,
         out_shape=[sd((T,1024),F32),sd((40,512),F32)]+[out(q.shape[2],q.shape[3]) for q in pairs]+[out(half,512),out(half,512),out(half,1024),out(half,1024)],
         scratch_shapes=[pltpu.VMEM((HEADS,VH,KH),F32),pltpu.VMEM((1,512),F32),pltpu.VMEM((nr,512),F32),pltpu.VMEM((C,1024),BF),
                         pltpu.VMEM((T,3072),BF),pltpu.VMEM((1024,T),BF),pltpu.VMEM((C,512),BF),pltpu.VMEM((16,1024),F32),pltpu.VMEM((16,512),F32),
                         pltpu.VMEM((1,512),F32),pltpu.VMEM((1,256),F32),pltpu.VMEM((n,40,512),F32),
-                        pltpu.VMEM((2,n,half,3072),BF),pltpu.VMEM((T,16),BF)]+scratch,
+                        pltpu.VMEM((2,n,half,3072),BF),pltpu.VMEM((T,16),BF)]
+                       +[pltpu.VMEM((1024,w),BF) for w in (512,512,1024,1024)]+[pltpu.SemaphoreType.DMA((4,))]+scratch,
         compiler_params=pltpu.CompilerParams(collective_id=2,has_side_effects=True,vmem_limit_bytes=63<<20),
         name="gla_bwd_reduce")(q,k,v,g,r,o,st,dy,first,tokens,dx2,wh,vecs,nmlp,segr,M,*weights,*pairs)
     return res[0],res[1],[x.reshape(-1,x.shape[2]) for x in res[2:]]

time: 346 us -> 336 us (0.971)
  Pallas kernels: 315 us -> 304 us
    pallas_call x1, Pallas kernels: 118 us -> 112 us  [feed(): pl.pallas_call(functools.partial(feed_kernel, n, reps, half, tile), grid=...]
    pallas_call x1, Pallas kernels: 108 us -> 103 us  [backward(): pl.pallas_call(functools.partial(backward_kernel, n, reps, tuple(plan), h...]
where the time goes in v6:
time: 336 us
  Pallas kernels  304 us (90%)
  other arithmetic  13.7 us (4%)
  local copies, waits for them, and re-layouts  9.38 us (3%)
  matrix products  7.46 us (2%)
    pallas_call x1, Pallas kernels, feed(): pl.pallas_call(functools.partial(feed_kernel, n, reps, half, tile), grid=...  112 us
    pallas_call x1, Pallas kernels, backward(): pl.pallas_call(functools.partial(backward_kernel, n, reps, tuple(plan), h...  103 us
    pallas_call x1, Pallas kernels, forward(): pl.pallas_call(functools.partial(forward_kernel, n, reps, width), grid=(n...  88.6 us

profile of v6, /device:TPU:1, one launch (start us, length us, event | category | flops | bytes accessed | tf_op | source)
XLA Modules:
  0.0 335.7 jit_solution(3181172844297867094)
XLA Ops:
  0.6 0.7 concatenate.18
  1.3 0.7 concatenate.19
  2.0 0.8 concatenate.22
  2.7 0.6 convert_element_type.82.refs_3_
  3.3 88.6 %gla_fwd_gather.1 = (bf16[1024,1024]{1,0:T(8,128)(2,1)}, bf16[1024,512]{1,0:T(8,128)(2,1)}, bf16[1024,512]{1,0:T(8,128)(2,1)}, bf16[1024,1024]{1,0:T(8,128)(2,1)...) custom-call(bf16[1024,1024]{1,0:T(8,128)(2,1)} %bitcast.64, ...), custom_call_target="tpu_custom_call" | custom-call | tf_op jit(solution)/shard_map/gla_fwd_gather/pallas_call | solution.py:945
  92.0 112.4 %feed_forward.1 = (bf16[1024,1024]{1,0:T(8,128)(2,1)}, f32[1024,1024]{1,0:T(8,128)}, bf16[1024,1024]{1,0:T(8,128)(2,1)}, f32[1,1024]{1,0:T(1,128)}, bf16[2816,10...) custom-call(bf16[1024,1024]{1,0:T(8,128)(2,1)} %get-tuple-element.53, ...), custom_call_target="tpu_custom_call" | custom-call | tf_op jit(solution)/shard_map/feed_forward/pallas_call | solution.py:764
  204.4 0.0 copy-start.14
  204.4 0.0 copy-start.15
  204.4 4.9 %bitcast_convert_fusion.1 = (f32[256,2816]{1,0:T(8,128)}, f32[256,2816]{1,0:T(8,128)}) fusion(bf16[2,128,2816]{2,1,0:T(8,128)(2,1)} %get-tuple-element.88, bf16[2,128,2816]{2,1,0:T(8,128)(2,1)} %get-tuple-element.87), kind=kLoop, calls=%fused_computation.3 | loop fusion | flops 1441792 | bytes 8650752 | tf_op jit(solution)/shard_map/convert_element_type | solution.py:1209
  209.3 0.0 copy-done.14
  209.3 0.0 copy-done.15
  209.3 0.0 copy-start.13
  209.3 3.8 %convolution_convert_fusion = bf16[1024,1024]{1,0:T(8,128)(2,1)} fusion(bf16[1024,1024]{1,0:T(8,128)(2,1)S(1)} %copy-done.14, bf16[1024,1024]{1,0:T(8,128)(2,1)S(1)} %copy-done.15), kind=kOutput, calls=%fused_computation | convolution fusion | flops 2148532224 | bytes 6291456 | tf_op jit(solution)/shard_map/dot_general | solution.py:25
  213.1 0.0 copy-done.13
  213.1 3.7 %convolution_convert_fusion.1.refs_7_ = bf16[1024,1024]{1,0:T(8,128)(2,1)} fusion(bf16[1024,1024]{1,0:T(8,128)(2,1)S(1)} %copy-done.15, bf16[1024,1024]{1,0:T(8,128)(2,1)S(1)} %bitcast.92), kind=kOutput, calls=%fused_computation.1 | convolution fusion | flops 2148532224 | bytes 6291456 | tf_op jit(solution)/shard_map/dot_general | solution.py:24
  216.8 0.0 copy-start.5
  216.8 0.0 copy-start.6
  216.8 103.3 %gla_bwd_reduce.1 = (f32[1024,1024]{1,0:T(8,128)}, f32[40,512]{1,0:T(8,128)}, bf16[2,352,1024]{2,1,0:T(8,128)(2,1)}, bf16[2,128,1024]{2,1,0:T(8,128)(2,1)}, bf16...) custom-call(bf16[1024,512]{1,0:T(8,128)(2,1)} %get-tuple-element.60., ...), custom_call_target="tpu_custom_call" | custom-call | tf_op jit(solution)/shard_map/gla_bwd_reduce/pallas_call | solution.py:1121
  320.1 0.0 copy-start.2
  320.1 0.0 copy-start.3
  320.1 0.0 copy-start.8
  320.2 0.0 copy-start.9
  320.2 0.0 copy-done.5
  320.2 0.0 copy-done.6
  320.2 2.3 multiply_reduce_fusion.2
  322.4 0.0 copy-done.2
  322.4 0.0 copy-done.3
  322.4 0.0 copy-done.8
  322.5 0.0 copy-done.9
  322.5 0.0 copy-start.10
  322.5 0.0 copy-start.11
  322.5 0.0 copy-start.12
  322.5 0.0 copy-start.4
  322.5 1.6 multiply_reduce_fusion
  324.1 0.0 copy-done.10
  324.1 0.0 copy-done.11
  324.1 0.6 multiply_reduce_fusion.4
  324.7 0.0 copy-done.12
  324.7 0.6 convert_divide_fusion
  325.3 0.0 copy-done.4
  325.3 0.0 copy-start.7
  325.3 0.0 copy-start.1
  325.3 2.0 bitcast_convert_fusion
  327.3 0.0 copy-done.7
  327.3 1.1 bitcast_convert_fusion.3
  328.5 0.6 constant_dynamic-slice_fusion.2
  329.1 0.6 fusion.2
  329.6 0.6 fusion.1
  330.2 0.5 fusion
  330.7 0.0 copy-done.1
  330.7 0.0 copy-start
  330.7 1.3 copy.37
  332.1 1.6 copy-done
  333.7 2.0 copy.38
  (3 shorter events, 0.0 us)
Async XLA Ops:
  204.4 4.9 %copy-start.14 = (bf16[1024,1024]{1,0:T(8,128)(2,1)S(1)}, bf16[1024,1024]{1,0:T(8,128)(2,1)}, u32[]{:S(2)}) copy-start(bf16[1024,1024]{1,0:T(8,128)(2,1)} %get-tuple-element.79) | copy-start | bytes 6291460
  204.4 4.9 %copy-start.15 = (bf16[1024,1024]{1,0:T(8,128)(2,1)S(1)}, bf16[1024,1024]{1,0:T(8,128)(2,1)}, u32[]{:S(2)}) copy-start(bf16[1024,1024]{1,0:T(8,128)(2,1)} %get-tuple-element.67) | copy-start | bytes 6291460
  209.3 3.8 %copy-start.13 = (bf16[4,2,128,1024]{3,2,1,0:T(8,128)(2,1)S(1)}, bf16[4,2,128,1024]{3,2,1,0:T(8,128)(2,1)}, u32[]{:S(2)}) copy-start(bf16[4,2,128,1024]{3,2,1,0:T(8,128)(2,1)} %get-tuple-element.68) | copy-start | bytes 6291460
  216.8 103.4 %copy-start.5 = (bf16[256,512]{1,0:T(8,128)(2,1)S(1)}, bf16[256,512]{1,0:T(8,128)(2,1)}, u32[]{:S(2)}) copy-start(bf16[256,512]{1,0:T(8,128)(2,1)} %param.23) | copy-start | bytes 786436
  216.8 103.4 %copy-start.6 = (bf16[256,512]{1,0:T(8,128)(2,1)S(1)}, bf16[256,512]{1,0:T(8,128)(2,1)}, u32[]{:S(2)}) copy-start(bf16[256,512]{1,0:T(8,128)(2,1)} %param.24) | copy-start | bytes 786436
  320.1 2.3 copy-start.2
  320.1 2.3 copy-start.3
  320.1 2.3 copy-start.8
  320.2 2.3 copy-start.9
  322.5 1.7 copy-start.10
  322.5 1.6 copy-start.11
  322.5 2.2 copy-start.12
  322.5 2.8 copy-start.4
  325.3 2.0 copy-start.7
  325.3 5.4 %copy-start.1 = (bf16[1024,1024]{1,0:T(8,128)(2,1)S(1)}, bf16[1024,1024]{1,0:T(8,128)(2,1)}, u32[]{:S(2)}) copy-start(bf16[1024,1024]{1,0:T(8,128)(2,1)} %get-tuple-element.59) | copy-start | bytes 6291460
  330.7 2.9 copy-start

commit v7 on v6

--- a/solution.py
+++ b/solution.py
@@ -136,8 +136,8 @@
 
 MESH = pl.DeviceIdType.MESH
 TILE = 256
-LEADS = (6, 3, 2)
-EARLY = 3
+LEADS = (7, 3, 2)
+EARLY = 4
 
 
 class Place:

time: 336 us -> 335 us (level)
    pallas_call x1, Pallas kernels: 112 us -> 108 us  [feed(): pl.pallas_call(functools.partial(feed_kernel, n, reps, half, tile), grid=...]
    pallas_call x1, Pallas kernels: 88.6 us -> 93 us  [forward(): pl.pallas_call(functools.partial(forward_kernel, n, reps, width), grid=(n...]
where the time goes in v7:
time: 335 us
  Pallas kernels  303 us (90%)
  other arithmetic  13.7 us (4%)
  local copies, waits for them, and re-layouts  9.38 us (3%)
  matrix products  7.46 us (2%)
    pallas_call x1, Pallas kernels, feed(): pl.pallas_call(functools.partial(feed_kernel, n, reps, half, tile), grid=...  108 us
    pallas_call x1, Pallas kernels, backward(): pl.pallas_call(functools.partial(backward_kernel, n, reps, tuple(plan), h...  103 us
    pallas_call x1, Pallas kernels, forward(): pl.pallas_call(functools.partial(forward_kernel, n, reps, width), grid=(n...  93 us

profile of v7, /device:TPU:1, one launch (start us, length us, event | category | flops | bytes accessed | tf_op | source)
XLA Modules:
  0.0 334.6 jit_solution(755470428848589267)
XLA Ops:
  0.6 0.7 concatenate.18
  1.3 0.7 concatenate.19
  2.0 0.8 concatenate.22
  2.7 0.6 convert_element_type.82.refs_3_
  3.3 93.0 %gla_fwd_gather.1 = (bf16[1024,1024]{1,0:T(8,128)(2,1)}, bf16[1024,512]{1,0:T(8,128)(2,1)}, bf16[1024,512]{1,0:T(8,128)(2,1)}, bf16[1024,1024]{1,0:T(8,128)(2,1)...) custom-call(bf16[1024,1024]{1,0:T(8,128)(2,1)} %bitcast.64, ...), custom_call_target="tpu_custom_call" | custom-call | tf_op jit(solution)/shard_map/gla_fwd_gather/pallas_call | solution.py:945
  96.3 107.8 %feed_forward.1 = (bf16[1024,1024]{1,0:T(8,128)(2,1)}, f32[1024,1024]{1,0:T(8,128)}, bf16[1024,1024]{1,0:T(8,128)(2,1)}, f32[1,1024]{1,0:T(1,128)}, bf16[2816,10...) custom-call(bf16[1024,1024]{1,0:T(8,128)(2,1)} %get-tuple-element.53, ...), custom_call_target="tpu_custom_call" | custom-call | tf_op jit(solution)/shard_map/feed_forward/pallas_call | solution.py:764
  204.1 0.0 copy-start.14
  204.1 0.0 copy-start.15
  204.1 4.9 %bitcast_convert_fusion.1 = (f32[256,2816]{1,0:T(8,128)}, f32[256,2816]{1,0:T(8,128)}) fusion(bf16[2,128,2816]{2,1,0:T(8,128)(2,1)} %get-tuple-element.88, bf16[2,128,2816]{2,1,0:T(8,128)(2,1)} %get-tuple-element.87), kind=kLoop, calls=%fused_computation.3 | loop fusion | flops 1441792 | bytes 8650752 | tf_op jit(solution)/shard_map/convert_element_type | solution.py:1209
  209.0 0.0 copy-done.14
  209.0 0.0 copy-done.15
  209.0 0.0 copy-start.13
  209.0 3.8 %convolution_convert_fusion = bf16[1024,1024]{1,0:T(8,128)(2,1)} fusion(bf16[1024,1024]{1,0:T(8,128)(2,1)S(1)} %copy-done.14, bf16[1024,1024]{1,0:T(8,128)(2,1)S(1)} %copy-done.15), kind=kOutput, calls=%fused_computation | convolution fusion | flops 2148532224 | bytes 6291456 | tf_op jit(solution)/shard_map/dot_general | solution.py:25
  212.8 0.0 copy-done.13
  212.8 3.7 %convolution_convert_fusion.1.refs_7_ = bf16[1024,1024]{1,0:T(8,128)(2,1)} fusion(bf16[1024,1024]{1,0:T(8,128)(2,1)S(1)} %copy-done.15, bf16[1024,1024]{1,0:T(8,128)(2,1)S(1)} %bitcast.92), kind=kOutput, calls=%fused_computation.1 | convolution fusion | flops 2148532224 | bytes 6291456 | tf_op jit(solution)/shard_map/dot_general | solution.py:24
  216.5 0.0 copy-start.5
  216.5 0.0 copy-start.6
  216.5 102.5 %gla_bwd_reduce.1 = (f32[1024,1024]{1,0:T(8,128)}, f32[40,512]{1,0:T(8,128)}, bf16[2,352,1024]{2,1,0:T(8,128)(2,1)}, bf16[2,128,1024]{2,1,0:T(8,128)(2,1)}, bf16...) custom-call(bf16[1024,512]{1,0:T(8,128)(2,1)} %get-tuple-element.60., ...), custom_call_target="tpu_custom_call" | custom-call | tf_op jit(solution)/shard_map/gla_bwd_reduce/pallas_call | solution.py:1121
  319.0 0.0 copy-start.2
  319.0 0.0 copy-start.3
  319.1 0.0 copy-start.8
  319.1 0.0 copy-start.9
  319.1 0.0 copy-done.5
  319.1 0.0 copy-done.6
  319.1 2.3 multiply_reduce_fusion.2
  321.4 0.0 copy-done.2
  321.4 0.0 copy-done.3
  321.4 0.0 copy-done.8
  321.4 0.0 copy-done.9
  321.4 0.0 copy-start.10
  321.4 0.0 copy-start.11
  321.4 0.0 copy-start.12
  321.4 0.0 copy-start.4
  321.4 1.6 multiply_reduce_fusion
  323.0 0.0 copy-done.10
  323.0 0.0 copy-done.11
  323.0 0.6 multiply_reduce_fusion.4
  323.6 0.0 copy-done.12
  323.6 0.6 convert_divide_fusion
  324.2 0.0 copy-done.4
  324.2 0.0 copy-start.7
  324.2 0.0 copy-start.1
  324.2 2.0 bitcast_convert_fusion
  326.3 0.0 copy-done.7
  326.3 1.1 bitcast_convert_fusion.3
  327.4 0.6 constant_dynamic-slice_fusion.2
  328.0 0.6 fusion.2
  328.5 0.6 fusion.1
  329.1 0.5 fusion
  329.6 0.0 copy-done.1
  329.6 0.0 copy-start
  329.7 1.3 copy.37
  331.0 1.6 copy-done
  332.6 2.0 copy.38
  (3 shorter events, 0.0 us)
Async XLA Ops:
  204.1 4.9 %copy-start.14 = (bf16[1024,1024]{1,0:T(8,128)(2,1)S(1)}, bf16[1024,1024]{1,0:T(8,128)(2,1)}, u32[]{:S(2)}) copy-start(bf16[1024,1024]{1,0:T(8,128)(2,1)} %get-tuple-element.79) | copy-start | bytes 6291460
  204.1 4.9 %copy-start.15 = (bf16[1024,1024]{1,0:T(8,128)(2,1)S(1)}, bf16[1024,1024]{1,0:T(8,128)(2,1)}, u32[]{:S(2)}) copy-start(bf16[1024,1024]{1,0:T(8,128)(2,1)} %get-tuple-element.67) | copy-start | bytes 6291460
  209.0 3.8 %copy-start.13 = (bf16[4,2,128,1024]{3,2,1,0:T(8,128)(2,1)S(1)}, bf16[4,2,128,1024]{3,2,1,0:T(8,128)(2,1)}, u32[]{:S(2)}) copy-start(bf16[4,2,128,1024]{3,2,1,0:T(8,128)(2,1)} %get-tuple-element.68) | copy-start | bytes 6291460
  216.5 102.6 %copy-start.5 = (bf16[256,512]{1,0:T(8,128)(2,1)S(1)}, bf16[256,512]{1,0:T(8,128)(2,1)}, u32[]{:S(2)}) copy-start(bf16[256,512]{1,0:T(8,128)(2,1)} %param.23) | copy-start | bytes 786436
  216.5 102.6 %copy-start.6 = (bf16[256,512]{1,0:T(8,128)(2,1)S(1)}, bf16[256,512]{1,0:T(8,128)(2,1)}, u32[]{:S(2)}) copy-start(bf16[256,512]{1,0:T(8,128)(2,1)} %param.24) | copy-start | bytes 786436
  319.0 2.3 copy-start.2
  319.0 2.3 copy-start.3
  319.1 2.3 copy-start.8
  319.1 2.3 copy-start.9
  321.4 1.7 copy-start.10
  321.4 1.6 copy-start.11
  321.4 2.2 copy-start.12
  321.4 2.8 copy-start.4
  324.2 2.0 copy-start.7
  324.2 5.4 %copy-start.1 = (bf16[1024,1024]{1,0:T(8,128)(2,1)S(1)}, bf16[1024,1024]{1,0:T(8,128)(2,1)}, u32[]{:S(2)}) copy-start(bf16[1024,1024]{1,0:T(8,128)(2,1)} %get-tuple-element.59) | copy-start | bytes 6291460
  329.6 2.9 copy-start
